TPU v7x, 256 devices: a whole 4x4x8 slice. The times are simulated.
256 devices in a mesh: date: 32 (over z, y_lo, core), strip: 8 (over x, y_hi).
Axes of the slice: x: 4, y: 4 (y_hi: 2, y_lo: 2; y = y_hi * 2 + y_lo), z: 8, core: 2. Of those that a mesh axis runs over, the one named last changes fastest.
Arguments:
- acquisitions: bfloat16 [64, 2, 2, 344, 2560], P('date', None, None, None, 'strip'), may hold values from -6 to 6
- shifts: int32 [2, 64, 2, 5, 40], P(None, 'date', None, None, 'strip'), may hold values from -8 to 8, as said below
- fractions: int32 [2, 64, 2, 5, 40], P(None, 'date', None, None, 'strip'), may hold values from 0 to 63
- ref_dates: int32 [2], replicated, may hold values from 0 to 63, as said below
Outputs:
- chip_corr: float32 [2, 64, 2, 5, 40], P(None, 'date', None, None, 'strip')
- coherence: float32 [2, 63, 2, 64, 128], P(None, None, None, 'date', 'strip')
Inputs may be any that keep to these rules, and one draw needn't show every extreme that they name: `shifts`: zero at every chip of date ref_dates[t] in tile t. `ref_dates`: the reference dates of consecutive tiles lie in different blocks of 2 dates.
All inputs are finite; a program needn't handle non-finite values.
Results may differ from a plain program's by a relative error of at most 0.0021.
Values may be sent and summed in bfloat16 or wider, within the bound.
No kernel may reach another device: no remote copies, remote signals or barrier semaphores. Data moves between devices by JAX's collectives and lax.ppermute only.
A program may use at most 64 MiB of HBM per device.

v0:
```python
import jax
import jax.numpy as jnp
from jax import lax
from jax.sharding import PartitionSpec as P

TILE_COUNT = 2
CHIP_SIZE = 64
TAP_COUNT = 8
SUBSTEPS = 64
LOOK_AZ = 5
LOOK_RG = 20
MARGIN = 12


epsilon = 1e-06


def padded_2(block, sides, width):
    for axis, dim in sides:
        count = lax.axis_size(axis)
        forward = [(i, i + 1) for i in range(count - 1)]
        backward = [(target, source) for source, target in forward]
        low = lax.ppermute(
            lax.slice_in_dim(block, block.shape[dim] - width, None, axis=dim), axis, forward
        )
        high = lax.ppermute(lax.slice_in_dim(block, 0, width, axis=dim), axis, backward)
        block = jnp.concatenate([low, block, high], axis=dim)
    return block


def spread(value, axis, source):
    kept = jnp.where(lax.axis_index(axis) == source, value, 0).astype(value.dtype)
    return lax.psum(kept, axis)


def sinc_matrix(shift_part, fraction_part):
    window_size = CHIP_SIZE + 2 * MARGIN
    offset = fraction_part.astype(jnp.float32) / SUBSTEPS
    tap_axis = jnp.arange(TAP_COUNT).astype(jnp.float32)
    distance = tap_axis - (TAP_COUNT // 2 - 1) - offset[..., None]
    weights = jnp.sinc(distance) * (0.5 + 0.5 * jnp.cos(jnp.pi * distance / (TAP_COUNT // 2)))
    weights = weights / jnp.sum(weights, axis=-1, keepdims=True)
    out_rows = jnp.arange(CHIP_SIZE, dtype=jnp.int32)[:, None]
    in_rows = jnp.arange(window_size, dtype=jnp.int32)[None, :]
    matrix = jnp.zeros(shift_part.shape + (CHIP_SIZE, window_size), jnp.float32)
    for tap_index in range(TAP_COUNT):
        target = out_rows + shift_part[..., None, None] + (tap_index - TAP_COUNT // 2 + 1 + MARGIN)
        matrix = matrix + jnp.where(
            in_rows == target, weights[..., tap_index][..., None, None], 0.0
        )
    return matrix.astype(jnp.bfloat16)


def correlate(reference_tiles, resampled):
    chips_az = resampled.shape[-2] // CHIP_SIZE
    chips_rg = resampled.shape[-1] // CHIP_SIZE

    def as_chips(values):
        return values.astype(jnp.float32).reshape(
            values.shape[:-2] + (chips_az, CHIP_SIZE, chips_rg, CHIP_SIZE)
        )

    ref_chips = as_chips(reference_tiles)
    sec_chips = as_chips(resampled)
    ref_real = ref_chips[..., 0, :, :, :, :]
    ref_imag = ref_chips[..., 1, :, :, :, :]
    sec_real = sec_chips[..., 0, :, :, :, :]
    sec_imag = sec_chips[..., 1, :, :, :, :]
    cross_real = jnp.sum(ref_real * sec_real + ref_imag * sec_imag, axis=(-3, -1))
    cross_imag = jnp.sum(ref_imag * sec_real - ref_real * sec_imag, axis=(-3, -1))
    ref_power = jnp.sum(ref_real * ref_real + ref_imag * ref_imag, axis=(-3, -1))
    sec_power = jnp.sum(sec_real * sec_real + sec_imag * sec_imag, axis=(-3, -1))
    denominator = jnp.sqrt((ref_power + epsilon) * (sec_power + epsilon))
    return jnp.stack([cross_real / denominator, cross_imag / denominator])


def multilook_pairs(series):
    values = series.astype(jnp.float32)
    earlier = values[:-1]
    second = values[1:]
    early_real = earlier[:, :, 0]
    early_imag = earlier[:, :, 1]
    later_real = second[:, :, 0]
    later_imag = second[:, :, 1]
    cross_real = early_real * later_real + early_imag * later_imag
    cross_imag = early_imag * later_real - early_real * later_imag
    power_early = early_real * early_real + early_imag * early_imag
    power_later = later_real * later_real + later_imag * later_imag

    def box_sum(quantity):
        blocked = quantity.reshape(
            quantity.shape[:2]
            + (quantity.shape[2] // LOOK_AZ, LOOK_AZ, quantity.shape[3] // LOOK_RG, LOOK_RG)
        )
        return jnp.sum(blocked, axis=(3, 5))

    denominator = jnp.sqrt((box_sum(power_early) + epsilon) * (box_sum(power_later) + epsilon))
    return jnp.stack([box_sum(cross_real) / denominator, box_sum(cross_imag) / denominator])


def resample(padded, shift_part, fraction_part):
    window_size = CHIP_SIZE + 2 * MARGIN
    chips_az = shift_part.shape[3]
    chips_rg = shift_part.shape[4]
    pieces = [
        padded[
            :,
            :,
            :,
            chip_row * CHIP_SIZE : chip_row * CHIP_SIZE + window_size,
            chip_col * CHIP_SIZE : chip_col * CHIP_SIZE + window_size,
        ]
        for chip_row in range(chips_az)
        for chip_col in range(chips_rg)
    ]
    windows = jnp.stack(pieces, axis=3).reshape(
        padded.shape[:3] + (chips_az, chips_rg, window_size, window_size)
    )
    azimuth = sinc_matrix(shift_part[0], fraction_part[0])
    across = sinc_matrix(shift_part[1], fraction_part[1])
    partial_rows = jnp.einsum(
        "dtariw,dtcarwv->dtcariv", azimuth, windows, preferred_element_type=jnp.float32
    ).astype(jnp.bfloat16)
    chips_out = jnp.einsum(
        "dtcariv,dtarjv->dtcarij", partial_rows, across, preferred_element_type=jnp.float32
    ).astype(jnp.bfloat16)
    return chips_out.transpose(0, 1, 2, 3, 5, 4, 6).reshape(
        padded.shape[:3] + (chips_az * CHIP_SIZE, chips_rg * CHIP_SIZE)
    )


def per_device(acquisitions, shifts, fractions, ref_dates):
    dates_local = acquisitions.shape[0]
    tile_rows = acquisitions.shape[3] - 2 * MARGIN
    padded = padded_2(acquisitions, (("strip", 4),), MARGIN)
    owners = ref_dates // dates_local
    slots = ref_dates % dates_local
    candidates = [
        lax.dynamic_index_in_dim(acquisitions[:, tile_index], slots[tile_index], 0, keepdims=False)[
            :, MARGIN : MARGIN + tile_rows, :
        ]
        for tile_index in range(TILE_COUNT)
    ]
    reference_tiles = jnp.stack(
        [
            spread(candidates[tile_index], "date", owners[tile_index])
            for tile_index in range(TILE_COUNT)
        ]
    )
    resampled = resample(padded, shifts, fractions)
    chip_corr = correlate(reference_tiles, resampled)
    coherence = multilook_pairs(
        lax.all_to_all(resampled, "date", split_axis=3, concat_axis=0, tiled=True)
    )
    return (chip_corr, coherence)


def solution(mesh):
    return jax.shard_map(
        per_device,
        mesh=mesh,
        in_specs=(
            P("date", None, None, None, "strip"),
            P(None, "date", None, None, "strip"),
            P(None, "date", None, None, "strip"),
            P(),
        ),
        out_specs=(P(None, "date", None, None, "strip"), P(None, None, None, "date", "strip")),
        check_vma=False,
    )
```

profile of v0, /device:TPU:19, one launch (start us, length us, event | category | flops | bytes accessed | tf_op | source)
XLA Modules:
  0.0 460.6 jit_solution(9222938451931565228)
XLA Ops:
  7.2 1.8 fusion.119
  9.0 2.0 collective-permute-start.1
  10.9 5.7 %collective-permute-start = (bf16[2,2,2,344,12]{3,4,2,1,0:T(8,128)(2,1)}, bf16[2,2,2,344,12]{3,4,2,1,0:T(8,128)(2,1)S(1)}, u32[]{:S(2)}, u32[]{:S(2)}) collective-permute-start(bf16[2,2,2,344,12]{3,4,2,1,0:T(8,128)(2,1)} %get-tuple-element.23), channel_id=1, source_target_pairs={{0,1},{1,2},{2,3},{3,4},{4,5},{5,6},{6,7},{8,9},{9,10},{10,11},{11... | collective-permute-start | bytes 198152 | tf_op jit(solution)/shard_map/ppermute | solution.py:23
  16.7 0.7 and_select_fusion.1
  17.3 0.6 fusion.120
  20.5 2.7 fusion.118
  23.1 1.5 constant_dynamic-update-slice_fusion.1
  26.0 3.2 fusion.114
  29.2 3.1 broadcast_divide_fusion.1
  42.6 1.2 fusion.104
  43.9 1.1 dynamic-slice_bitcast_fusion.1
  45.1 0.9 dynamic-slice_bitcast_fusion
  46.0 0.7 fusion.72
  46.7 0.7 bitcast_dynamic-update-slice_fusion.14
  47.5 0.7 bitcast_dynamic-update-slice_fusion.13
  48.2 0.7 bitcast_dynamic-update-slice_fusion.12
  48.9 1.5 constant_dynamic-update-slice_fusion
  50.5 1.6 fusion.71
  52.1 0.8 fusion.70
  53.0 0.8 bitcast_dynamic-update-slice_fusion.11
  53.8 0.8 bitcast_dynamic-update-slice_fusion.10
  54.7 0.8 bitcast_dynamic-update-slice_fusion.9
  55.5 1.8 fusion.69
  57.3 0.7 fusion.68
  58.0 0.7 bitcast_dynamic-update-slice_fusion.8
  58.8 0.7 bitcast_dynamic-update-slice_fusion.7
  59.5 0.7 bitcast_dynamic-update-slice_fusion.6
  60.2 1.6 fusion.67
  61.9 0.8 fusion.66
  62.7 0.8 bitcast_dynamic-update-slice_fusion.5
  63.5 0.8 bitcast_dynamic-update-slice_fusion.4
  64.4 0.8 bitcast_dynamic-update-slice_fusion.3
  65.2 1.8 fusion.65
  67.1 0.8 fusion.64
  67.8 0.7 bitcast_dynamic-update-slice_fusion.2
  68.5 0.7 bitcast_dynamic-update-slice_fusion.1
  69.3 0.7 bitcast_dynamic-update-slice_fusion
  70.0 1.6 fusion.62
  71.8 7.4 %copy.137 = bf16[2,2,2,25,88,88]{5,4,2,3,1,0:T(8,128)(2,1)} copy(bf16[2,2,2,25,88,88]{4,5,2,1,0,3:T(8,128)(2,1)} %fusion.62) | data formatting | bytes 6195200 | tf_op jit(solution)/shard_map/stack | solution.py:116
  79.5 13.2 %fusion.4.clone.5 = bf16[2,2,2,5,5,64,88]{6,5,2,4,3,1,0:T(8,128)(2,1)S(1)} fusion(bf16[2,2,2,5,5,88,88]{6,5,2,4,3,1,0:T(8,128)(2,1)} %bitcast.220, f32[2,2,5,5]{3,2,1,0:T(8,128)S(1)} %copy-done.26, s32[2,2,5,5,64]{4,3,2,1,0:T(8,128)S(1)} %copy-done.11, f32[2,2,5,5]{3,2,1,0:T(8,128)S(1)} %copy-done.28, ...), kind=kOutput, calls=%fused_computation.3.clone.clone.clone.clone.clone.2 | convolution fusion | flops 212889600 | bytes 5558400 | tf_op jit(solution)/shard_map/dtariw,dtcarwv->dtcariv/dot_general | solution.py:121
  92.9 13.8 %fusion.122 = (f32[2,2,2,5,64,5,64]{4,6,2,5,3,1,0:T(8,128)}, bf16[2,2,2,5,64,5,64]{4,6,2,5,3,1,0:T(8,128)(2,1)}) fusion(f32[2,2,5,5]{3,2,1,0:T(8,128)S(1)} %copy-done.27, s32[2,2,5,5,64]{4,3,2,1,0:T(8,128)S(1)} %copy-done.8, f32[2,2,5,5]{3,2,1,0:T(8,128)S(1)} %copy-done.25, s32[2,2,5,5,64]{4,3,2,1,0:T(8,128)S(1)} %copy-done.7, ...), kind=kOutput, calls=%fused_computation.226 | convolution fusion | flops 159334400 | bytes 7376000 | tf_op jit(solution)/shard_map/dtcariv,dtarjv->dtcarij/dot_general | solution.py:124
  106.7 7.8 %copy.165 = bf16[2,2,2,5,64,5,64]{6,5,2,1,0,4,3:T(8,128)(2,1)} copy(bf16[2,2,2,5,64,5,64]{4,6,2,5,3,1,0:T(8,128)(2,1)} %get-tuple-element.73) | data formatting | bytes 3276800 | tf_op jit(solution)/shard_map/reshape | solution.py:127
  114.4 8.2 %reshape.249 = bf16[2,2,2,320,320]{4,2,1,0,3:T(2,128)(2,1)} reshape(bf16[2,2,2,5,64,5,64]{6,5,2,1,0,4,3:T(8,128)(2,1)} %copy.165) | data formatting | bytes 3276800 | tf_op jit(solution)/shard_map/reshape | solution.py:127
  122.6 10.7 %all-to-all-start = ((bf16[2,2,2,320,320]{4,2,1,0,3:T(2,128)(2,1)}), bf16[2,2,2,320,320]{4,2,1,0,3:T(2,128)(2,1)S(1)}, u32[]{:S(2)}, u32[]{:S(2)}) async-start(bf16[2,2,2,320,320]{4,2,1,0,3:T(2,128)(2,1)} %reshape.249), calls=%async_computation | async-start | bytes 3932160 | tf_op jit(solution)/shard_map/all_to_all | solution.py:153
  134.3 1.6 stack.98
  135.9 1.6 stack.97
  137.5 244.2 %all-reduce.3.cloned.1.call-done = (bf16[1,2,5,64,5,64]{5,4,3,2,1,0:T(8,128)(2,1)}, bf16[1,2,5,64,5,64]{5,4,3,2,1,0:T(8,128)(2,1)}) async-done(((bf16[1,2,5,64,5,64]{5,4,3,2,1,0:T(8,128)(2,1)}, bf16[1,2,5,64,5,64]{5,4,3,2,1,0:T(8,128)(2,1)}), (bf16[1,2,5,64,5,64]{5,4,3,2,1,0:T(8,128)(2,1)}, bf16[1,2,5,64,5,64]{5,4,3,2,1,0:T(8,128)(2,1)})) %all-reduce.3.cloned.1.call-update) | async-done | bytes 819216 | tf_op jit(solution)/shard_map/psum | solution.py:33
  381.7 2.7 maximum_convert_fusion
  385.0 2.8 slice_bitcast_fusion.3
  387.8 2.9 copy.127
  390.7 2.9 copy.148
  393.6 4.9 %add_reduce_fusion.1 = (f32[2,2,5,5]{3,2,1,0:T(8,128)S(1)}, f32[2,2,5,5]{3,2,1,0:T(8,128)S(1)}, f32[2,2,5,5]{3,2,1,0:T(8,128)S(1)}) fusion(f32[2,2,2,5,64,5,64]{4,6,2,5,3,1,0:T(8,128)} %get-tuple-element.72, f32[2,5,64,5,64]{2,4,3,1,0:T(8,128)} %copy.148, f32[2,5,64,5,64]{2,4,3,1,0:T(8,128)} %copy.127), kind=kLoop, calls=%fused_computation.6 | loop fusion | flops 4914900 | bytes 4916400 | tf_op jit(solution)/shard_map/reduce_sum | solution.py:69
  399.4 3.0 copy.156
  402.4 1.3 copy.157
  403.8 9.2 %multiply_add_fusion.2 = (f32[63,2,1,10,320]{4,2,3,1,0:T(1,128)}, f32[63,2,1,10,320]{4,2,3,1,0:T(1,128)}, f32[63,2,1,10,320]{4,2,3,1,0:T(1,128)}, f32[63,2,1,10,320]{4,2,3,1,0:T(1,128)S(1)}) fusion(f32[64,2,2,10,320]{4,2,3,1,0:T(2,128)S(1)} %bitcast.214), kind=kLoop, calls=%fused_computation.35 | loop fusion | flops 4838400 | bytes 12902400 | tf_op jit(solution)/shard_map/add | solution.py:85
  413.0 7.4 %copy.158 = f32[63,2,1,10,320]{0,1,4,3,2:T(2,128)} copy(f32[63,2,1,10,320]{4,2,3,1,0:T(1,128)} %get-tuple-element.16) | data formatting | bytes 3225600 | tf_op jit(solution)/shard_map/add | solution.py:85
  420.4 7.4 %copy.159 = f32[63,2,1,10,320]{0,1,4,3,2:T(2,128)} copy(f32[63,2,1,10,320]{4,2,3,1,0:T(1,128)} %get-tuple-element.17) | data formatting | bytes 3225600 | tf_op jit(solution)/shard_map/add | solution.py:87
  427.8 3.2 reduce_sum.102
  431.0 3.2 reduce_sum.103
  434.2 7.4 %copy.160 = f32[63,2,1,10,320]{0,1,4,3,2:T(2,128)} copy(f32[63,2,1,10,320]{4,2,3,1,0:T(1,128)} %get-tuple-element.18) | data formatting | bytes 3225600 | tf_op jit(solution)/shard_map/add | solution.py:88
  441.6 3.2 reduce_sum.104
  444.8 4.9 %copy.161 = f32[63,2,1,10,320]{0,1,4,3,2:T(2,128)} copy(f32[63,2,1,10,320]{4,2,3,1,0:T(1,128)S(1)} %get-tuple-element.19) | data formatting | bytes 3225600 | tf_op jit(solution)/shard_map/sub | solution.py:86
  449.8 3.2 reduce_sum.105
  453.1 0.6 copy.162
  (110 shorter events, 12.1 us)
Async XLA Ops:
  7.2 16.0 %copy-start = (bf16[2,2,2,344,320]{3,4,2,1,0:T(8,128)(2,1)S(1)}, bf16[2,2,2,344,320]{3,4,2,1,0:T(8,128)(2,1)}, u32[]{:S(2)}) copy-start(bf16[2,2,2,344,320]{3,4,2,1,0:T(8,128)(2,1)} %param.5) | copy-start | bytes 5283844
  9.0 40.0 %collective-permute-start.1 = (bf16[2,2,2,344,12]{3,4,2,1,0:T(8,128)(2,1)}, bf16[2,2,2,344,12]{3,4,2,1,0:T(8,128)(2,1)}, u32[]{:S(2)}, u32[]{:S(2)}) collective-permute-start(bf16[2,2,2,344,12]{3,4,2,1,0:T(8,128)(2,1)} %get-tuple-element.22), channel_id=1, source_target_pairs={{1,0},{2,1},{3,2},{4,3},{5,4},{6,5},{7,6},{9,8},{10,9},{11,10},{12... | collective-permute-start | bytes 198152 | tf_op jit(solution)/shard_map/ppermute | solution.py:26
  10.9 35.1 %collective-permute-start = (bf16[2,2,2,344,12]{3,4,2,1,0:T(8,128)(2,1)}, bf16[2,2,2,344,12]{3,4,2,1,0:T(8,128)(2,1)S(1)}, u32[]{:S(2)}, u32[]{:S(2)}) collective-permute-start(bf16[2,2,2,344,12]{3,4,2,1,0:T(8,128)(2,1)} %get-tuple-element.23), channel_id=1, source_target_pairs={{0,1},{1,2},{2,3},{3,4},{4,5},{5,6},{6,7},{8,9},{9,10},{10,11},{11... | collective-permute-start | bytes 198152 | tf_op jit(solution)/shard_map/ppermute | solution.py:23
  20.4 5.5 %copy-start.18 = (s32[2,2,2,5,5]{4,2,3,1,0:T(2,128)S(1)}, s32[2,2,2,5,5]{4,2,3,1,0:T(2,128)}, u32[]{:S(2)}) copy-start(s32[2,2,2,5,5]{4,2,3,1,0:T(2,128)} %param.6) | copy-start | bytes 2404
  20.5 5.5 %copy-start.19 = (s32[2,2,2,5,5]{4,2,3,1,0:T(2,128)S(1)}, s32[2,2,2,5,5]{4,2,3,1,0:T(2,128)}, u32[]{:S(2)}) copy-start(s32[2,2,2,5,5]{4,2,3,1,0:T(2,128)} %param.7) | copy-start | bytes 2404
  71.7 7.5 %copy-start.10 = (s32[2,2,5,5,64]{4,3,2,1,0:T(8,128)S(1)}, s32[2,2,5,5,64]{4,3,2,1,0:T(8,128)}, u32[]{:S(2)}) copy-start(s32[2,2,5,5,64]{4,3,2,1,0:T(8,128)} %get-tuple-element.56) | copy-start | bytes 76804
  71.7 7.5 %copy-start.11 = (s32[2,2,5,5,64]{4,3,2,1,0:T(8,128)S(1)}, s32[2,2,5,5,64]{4,3,2,1,0:T(8,128)}, u32[]{:S(2)}) copy-start(s32[2,2,5,5,64]{4,3,2,1,0:T(8,128)} %get-tuple-element.57) | copy-start | bytes 76804
  71.7 7.5 %copy-start.12 = (s32[2,2,5,5,64]{4,3,2,1,0:T(8,128)S(1)}, s32[2,2,5,5,64]{4,3,2,1,0:T(8,128)}, u32[]{:S(2)}) copy-start(s32[2,2,5,5,64]{4,3,2,1,0:T(8,128)} %get-tuple-element.58) | copy-start | bytes 76804
  71.7 7.5 %copy-start.13 = (s32[2,2,5,5,64]{4,3,2,1,0:T(8,128)S(1)}, s32[2,2,5,5,64]{4,3,2,1,0:T(8,128)}, u32[]{:S(2)}) copy-start(s32[2,2,5,5,64]{4,3,2,1,0:T(8,128)} %get-tuple-element.59) | copy-start | bytes 76804
  71.7 7.5 %copy-start.14 = (s32[2,2,5,5,64]{4,3,2,1,0:T(8,128)S(1)}, s32[2,2,5,5,64]{4,3,2,1,0:T(8,128)}, u32[]{:S(2)}) copy-start(s32[2,2,5,5,64]{4,3,2,1,0:T(8,128)} %get-tuple-element.60) | copy-start | bytes 76804
  71.7 7.5 %copy-start.15 = (s32[2,2,5,5,64]{4,3,2,1,0:T(8,128)S(1)}, s32[2,2,5,5,64]{4,3,2,1,0:T(8,128)}, u32[]{:S(2)}) copy-start(s32[2,2,5,5,64]{4,3,2,1,0:T(8,128)} %get-tuple-element.61) | copy-start | bytes 76804
  71.7 7.5 %copy-start.16 = (s32[2,2,5,5,64]{4,3,2,1,0:T(8,128)S(1)}, s32[2,2,5,5,64]{4,3,2,1,0:T(8,128)}, u32[]{:S(2)}) copy-start(s32[2,2,5,5,64]{4,3,2,1,0:T(8,128)} %get-tuple-element.62) | copy-start | bytes 76804
  71.7 7.5 %copy-start.17 = (s32[2,2,5,5,64]{4,3,2,1,0:T(8,128)S(1)}, s32[2,2,5,5,64]{4,3,2,1,0:T(8,128)}, u32[]{:S(2)}) copy-start(s32[2,2,5,5,64]{4,3,2,1,0:T(8,128)} %get-tuple-element.63) | copy-start | bytes 76804
  71.7 7.5 %copy-start.24 = (f32[2,2,5,5]{3,2,1,0:T(8,128)S(1)}, f32[2,2,5,5]{3,2,1,0:T(8,128)}, u32[]{:S(2)}) copy-start(f32[2,2,5,5]{3,2,1,0:T(8,128)} %copy.139) | copy-start | bytes 1204
  71.7 7.5 %copy-start.26 = (f32[2,2,5,5]{3,2,1,0:T(8,128)S(1)}, f32[2,2,5,5]{3,2,1,0:T(8,128)}, u32[]{:S(2)}) copy-start(f32[2,2,5,5]{3,2,1,0:T(8,128)} %copy.146) | copy-start | bytes 1204
  71.7 7.5 %copy-start.28 = (f32[2,2,5,5]{3,2,1,0:T(8,128)S(1)}, f32[2,2,5,5]{3,2,1,0:T(8,128)}, u32[]{:S(2)}) copy-start(f32[2,2,5,5]{3,2,1,0:T(8,128)} %copy.145) | copy-start | bytes 1204
  71.7 7.5 %copy-start.29 = (f32[2,2,5,5]{3,2,1,0:T(8,128)S(1)}, f32[2,2,5,5]{3,2,1,0:T(8,128)}, u32[]{:S(2)}) copy-start(f32[2,2,5,5]{3,2,1,0:T(8,128)} %copy.144) | copy-start | bytes 1204
  71.8 7.5 %copy-start.31 = (f32[2,2,5,5]{3,2,1,0:T(8,128)S(1)}, f32[2,2,5,5]{3,2,1,0:T(8,128)}, u32[]{:S(2)}) copy-start(f32[2,2,5,5]{3,2,1,0:T(8,128)} %copy.143) | copy-start | bytes 1204
  71.8 7.5 %copy-start.32 = (f32[2,2,5,5]{3,2,1,0:T(8,128)S(1)}, f32[2,2,5,5]{3,2,1,0:T(8,128)}, u32[]{:S(2)}) copy-start(f32[2,2,5,5]{3,2,1,0:T(8,128)} %copy.142) | copy-start | bytes 1204
  71.8 7.5 %copy-start.33 = (f32[2,2,5,5]{3,2,1,0:T(8,128)S(1)}, f32[2,2,5,5]{3,2,1,0:T(8,128)}, u32[]{:S(2)}) copy-start(f32[2,2,5,5]{3,2,1,0:T(8,128)} %copy.141) | copy-start | bytes 1204
  71.8 7.5 %copy-start.34 = (f32[2,2,5,5]{3,2,1,0:T(8,128)S(1)}, f32[2,2,5,5]{3,2,1,0:T(8,128)}, u32[]{:S(2)}) copy-start(f32[2,2,5,5]{3,2,1,0:T(8,128)} %copy.140) | copy-start | bytes 1204
  79.3 13.4 %copy-start.2 = (s32[2,2,5,5,64]{4,3,2,1,0:T(8,128)S(1)}, s32[2,2,5,5,64]{4,3,2,1,0:T(8,128)}, u32[]{:S(2)}) copy-start(s32[2,2,5,5,64]{4,3,2,1,0:T(8,128)} %get-tuple-element.84) | copy-start | bytes 76804
  79.3 13.4 %copy-start.3 = (s32[2,2,5,5,64]{4,3,2,1,0:T(8,128)S(1)}, s32[2,2,5,5,64]{4,3,2,1,0:T(8,128)}, u32[]{:S(2)}) copy-start(s32[2,2,5,5,64]{4,3,2,1,0:T(8,128)} %get-tuple-element.85) | copy-start | bytes 76804
  79.3 13.4 %copy-start.4 = (s32[2,2,5,5,64]{4,3,2,1,0:T(8,128)S(1)}, s32[2,2,5,5,64]{4,3,2,1,0:T(8,128)}, u32[]{:S(2)}) copy-start(s32[2,2,5,5,64]{4,3,2,1,0:T(8,128)} %get-tuple-element.86) | copy-start | bytes 76804
  79.4 13.4 %copy-start.5 = (s32[2,2,5,5,64]{4,3,2,1,0:T(8,128)S(1)}, s32[2,2,5,5,64]{4,3,2,1,0:T(8,128)}, u32[]{:S(2)}) copy-start(s32[2,2,5,5,64]{4,3,2,1,0:T(8,128)} %get-tuple-element.87) | copy-start | bytes 76804
  79.4 13.4 %copy-start.6 = (s32[2,2,5,5,64]{4,3,2,1,0:T(8,128)S(1)}, s32[2,2,5,5,64]{4,3,2,1,0:T(8,128)}, u32[]{:S(2)}) copy-start(s32[2,2,5,5,64]{4,3,2,1,0:T(8,128)} %get-tuple-element.88) | copy-start | bytes 76804
  79.4 13.4 %copy-start.7 = (s32[2,2,5,5,64]{4,3,2,1,0:T(8,128)S(1)}, s32[2,2,5,5,64]{4,3,2,1,0:T(8,128)}, u32[]{:S(2)}) copy-start(s32[2,2,5,5,64]{4,3,2,1,0:T(8,128)} %get-tuple-element.89) | copy-start | bytes 76804
  79.4 13.4 %copy-start.8 = (s32[2,2,5,5,64]{4,3,2,1,0:T(8,128)S(1)}, s32[2,2,5,5,64]{4,3,2,1,0:T(8,128)}, u32[]{:S(2)}) copy-start(s32[2,2,5,5,64]{4,3,2,1,0:T(8,128)} %get-tuple-element.90) | copy-start | bytes 76804
  79.4 13.4 %copy-start.9 = (s32[2,2,5,5,64]{4,3,2,1,0:T(8,128)S(1)}, s32[2,2,5,5,64]{4,3,2,1,0:T(8,128)}, u32[]{:S(2)}) copy-start(s32[2,2,5,5,64]{4,3,2,1,0:T(8,128)} %get-tuple-element.91) | copy-start | bytes 76804
  79.4 13.4 %copy-start.20 = (f32[2,2,5,5]{3,2,1,0:T(8,128)S(1)}, f32[2,2,5,5]{3,2,1,0:T(8,128)}, u32[]{:S(2)}) copy-start(f32[2,2,5,5]{3,2,1,0:T(8,128)} %copy.131) | copy-start | bytes 1204
  79.4 13.4 %copy-start.21 = (f32[2,2,5,5]{3,2,1,0:T(8,128)S(1)}, f32[2,2,5,5]{3,2,1,0:T(8,128)}, u32[]{:S(2)}) copy-start(f32[2,2,5,5]{3,2,1,0:T(8,128)} %copy.132) | copy-start | bytes 1204
  79.4 13.4 %copy-start.22 = (f32[2,2,5,5]{3,2,1,0:T(8,128)S(1)}, f32[2,2,5,5]{3,2,1,0:T(8,128)}, u32[]{:S(2)}) copy-start(f32[2,2,5,5]{3,2,1,0:T(8,128)} %copy.133) | copy-start | bytes 1204
  79.4 13.4 %copy-start.23 = (f32[2,2,5,5]{3,2,1,0:T(8,128)S(1)}, f32[2,2,5,5]{3,2,1,0:T(8,128)}, u32[]{:S(2)}) copy-start(f32[2,2,5,5]{3,2,1,0:T(8,128)} %copy.134) | copy-start | bytes 1204
  79.4 13.4 %copy-start.25 = (f32[2,2,5,5]{3,2,1,0:T(8,128)S(1)}, f32[2,2,5,5]{3,2,1,0:T(8,128)}, u32[]{:S(2)}) copy-start(f32[2,2,5,5]{3,2,1,0:T(8,128)} %copy.135) | copy-start | bytes 1204
  79.5 13.4 %copy-start.27 = (f32[2,2,5,5]{3,2,1,0:T(8,128)S(1)}, f32[2,2,5,5]{3,2,1,0:T(8,128)}, u32[]{:S(2)}) copy-start(f32[2,2,5,5]{3,2,1,0:T(8,128)} %copy.136) | copy-start | bytes 1204
  79.5 13.4 %copy-start.30 = (f32[2,2,5,5]{3,2,1,0:T(8,128)S(1)}, f32[2,2,5,5]{3,2,1,0:T(8,128)}, u32[]{:S(2)}) copy-start(f32[2,2,5,5]{3,2,1,0:T(8,128)} %copy.129) | copy-start | bytes 1204
  122.6 10.9 %copy-start.1 = (bf16[2,344,320]{1,2,0:T(8,128)(2,1)S(1)}, bf16[2,344,320]{1,2,0:T(8,128)(2,1)}, u32[]{:S(2)}) copy-start(bf16[2,344,320]{1,2,0:T(8,128)(2,1)} %dynamic-slice_bitcast_fusion) | copy-start | bytes 1320964
  122.6 276.6 %all-to-all-start = ((bf16[2,2,2,320,320]{4,2,1,0,3:T(2,128)(2,1)}), bf16[2,2,2,320,320]{4,2,1,0,3:T(2,128)(2,1)S(1)}, u32[]{:S(2)}, u32[]{:S(2)}) async-start(bf16[2,2,2,320,320]{4,2,1,0,3:T(2,128)(2,1)} %reshape.249), calls=%async_computation | async-start | bytes 3932160 | tf_op jit(solution)/shard_map/all_to_all | solution.py:153
  133.3 248.4 %all-reduce.3.cloned.1.call-start = ((), (), s32[]{:S(2)}) async-start(), calls=%async_computation.1 | async-start | bytes 5242880 | tf_op jit(solution)/shard_map/psum | solution.py:33
Sparse Core Ops, SparseCore 0:
  137.6 244.0 all-reduce.2
where the time goes:
time: 464 us; the launch traced here: 461 us
  waiting for transfers between devices  244 us (53%)
  local copies, waits for them, and re-layouts  107 us (23%)
  other arithmetic  43.7 us (9%)
  matrix products  27 us (6%)
  between operations  19.7 us (4%)
  starting transfers between devices  18.6 us (4%)
    psum x1, waiting for transfers between devices, spread(): return lax.psum(kept, axis)  244 us
    unnamed x91, local copies, waits for them, and re-layouts  20.8 us
    reshape x2, local copies, waits for them, and re-layouts, resample(): chips_out.transpose(0, 1, 2, 3, 5, 4, 6)  15.9 us
    dot_general x1, matrix products, resample(): jnp.einsum('dtcariv,dtarjv->dtcarij', partial_rows, across, preferred_ele...  13.8 us
    dot_general x1, matrix products, resample(): jnp.einsum('dtariw,dtcarwv->dtcariv', azimuth, windows, preferred_element...  13.2 us
    reduce_sum x4, other arithmetic, box_sum(): return jnp.sum(blocked, axis=(3, 5))  12.9 us
    all_to_all x1, starting transfers between devices, per_device(): lax.all_to_all(resampled, 'date', split_axis=3, concat_axis=0, tiled=True)  10.7 us
  transfers between devices with their start and end apart: 4, of which 1 were waited for; matrix products, arithmetic and copies ran while one was open for 11% of the time, Pallas kernels for 0%

commit v1 on v0

v1 whole, which is shorter than its diff:
```python
import functools

import jax
import jax.numpy as jnp
import numpy as np
from jax import lax
from jax.experimental import pallas as pl
from jax.experimental.pallas import tpu as pltpu
from jax.sharding import PartitionSpec as P

CHIP = 64
TAPS = 8
SUBSTEPS = 64
LOOK_AZ = 5
LOOK_RG = 20
MARGIN = 12
WINDOW = CHIP + 2 * MARGIN
LANES = 128
EDGE = 16
UNROLL = 1
EPSILON = 1e-06

VMEM = pl.BlockSpec(memory_space=pltpu.VMEM)
SMEM = pl.BlockSpec(memory_space=pltpu.SMEM)
F32 = jnp.float32
BF16 = jnp.bfloat16


def tap_table():
    x = np.arange(TAPS)[None, :] - (TAPS // 2 - 1) - np.arange(SUBSTEPS)[:, None] / SUBSTEPS
    weights = np.sinc(x) * (0.5 + 0.5 * np.cos(2 * np.pi * x / TAPS))
    weights = weights / weights.sum(axis=1, keepdims=True)
    table = np.zeros((SUBSTEPS, CHIP, LANES), np.float32)
    for line in range(CHIP):
        table[:, line, line : line + TAPS] = weights
    return table.astype(jnp.bfloat16)


def look_matrices(lines):
    chips = lines // CHIP
    looks = lines // LOOK_AZ
    plain = np.zeros((looks, chips, 2, CHIP), np.float32)
    for line in range(lines):
        plain[line // LOOK_AZ, line // CHIP, :, line % CHIP] = 1.0
    signed = plain.copy()
    signed[:, :, 1] *= -1.0
    return [m.reshape(looks, chips * LANES).astype(jnp.bfloat16) for m in (plain, signed)]


def lane_index(shape):
    return lax.broadcasted_iota(jnp.int32, shape, len(shape) - 1)


def call(body, outs, in_specs, scratch=(), cost=(0, 0)):
    return pl.pallas_call(
        body,
        out_shape=outs,
        in_specs=in_specs,
        out_specs=VMEM,
        scratch_shapes=list(scratch),
        cost_estimate=pl.CostEstimate(flops=cost[0], bytes_accessed=cost[1], transcendentals=0),
        compiler_params=pltpu.CompilerParams(vmem_limit_bytes=48 << 20),
    )


def reversed_bits(value, count):
    result = 0
    while count > 1:
        result = result * 2 + value % 2
        value //= 2
        count //= 2
    return result


def lane_tiles(image_ref, stage, index):
    lines = image_ref.shape[-1]
    whole = lines // LANES
    tiles = [image_ref[index + (slice(None), slice(k * LANES, (k + 1) * LANES))] for k in range(whole)]
    stage[:, 0 : lines - whole * LANES] = image_ref[index + (slice(None), slice(whole * LANES, lines))]
    return tiles + [stage[...]]


def candidate_body(group, dates_ref, me_ref, x_ref, out_ref, stage):
    cols, lines = x_ref.shape[-2:]
    chips_az = (lines - 2 * MARGIN) // CHIP
    lane = lane_index((cols, LANES))
    octets = out_ref.shape[0] // 8 // group

    def place(octet):
        return (reversed_bits(octet // octets, group) * octets + octet % octets) * 8

    parts = [[tile.astype(F32) for tile in lane_tiles(x_ref, stage.at[p], (0, 0, p))] for p in range(2)]
    for a in range(chips_az):
        start = MARGIN + a * CHIP
        tile, offset = start // LANES, start % LANES
        halves = []
        for p in range(2):
            shift = (p * CHIP - offset) % LANES
            value = pltpu.roll(parts[p][tile], shift, 1)
            if offset + CHIP > LANES:
                value = jnp.where(lane < p * CHIP + LANES - offset, value, pltpu.roll(parts[p][tile + 1], shift, 1))
            halves.append(value)
        value = jnp.where(lane < CHIP, halves[0], halves[1])
        for k in range(cols // 8):
            at = place(a * (cols // 8) + k)
            out_ref[at : at + 8, :] = value[8 * k : 8 * k + 8].astype(BF16)
    for octet in range(chips_az * cols // 8, out_ref.shape[0] // 8):
        at = place(octet)
        out_ref[at : at + 8, :] = jnp.zeros((8, LANES), BF16)


def resample_body(date, shift_ref, frac_ref, table_ref, x_ref, left_ref, right_ref, out_ref, stage, window):
    t = pl.program_id(0)
    cols, lines = x_ref.shape[-2:]
    chips_az = (lines - 2 * MARGIN) // CHIP
    chips_rg = cols // CHIP
    depth = CHIP + 2 * EDGE

    def fill(source_ref, scratch, at):
        count = source_ref.shape[-2]
        lane = lane_index((count, LANES))
        for p in range(2):
            tiles = lane_tiles(source_ref, scratch.at[p], (0, 0, p))
            turned = [pltpu.roll(tile, CHIP, 1) for tile in tiles]
            for a in range(chips_az):
                tile = tiles[a // 2]
                if a % 2:
                    tile = jnp.where(lane < CHIP, turned[a // 2], turned[a // 2 + 1])
                window[a, p, at : at + count, :] = tile

    for p in range(2):
        stage[p, :, :] = jnp.zeros(stage.shape[1:], BF16)
    fill(left_ref, stage.at[:, 0:EDGE], 0)
    fill(x_ref, stage, EDGE)
    fill(right_ref, stage.at[:, 0:EDGE], EDGE + cols)
    half = lane_index((depth, LANES)) < CHIP

    def skewed(fraction, offset):
        return pltpu.roll(table_ref[fraction], offset, 1)

    def chip_column(r, carry):
        start = pl.multiple_of(r * CHIP, CHIP)
        for a in range(chips_az):
            azimuth = skewed(frac_ref[0, date, a, t, r], shift_ref[0, date, a, t, r] + 9)
            across = skewed(frac_ref[1, date, a, t, r], shift_ref[1, date, a, t, r] + 13)
            both = jnp.concatenate([azimuth, azimuth], axis=0)
            data = jnp.concatenate([window[a, p, pl.ds(start, depth), :] for p in range(2)], axis=0)
            partial = lax.dot_general(data, both, (((1,), (1,)), ((), ())), preferred_element_type=F32)
            partial = jnp.where(half, partial[:depth], partial[depth:]).astype(BF16)
            chip = jnp.dot(across[:, :depth], partial, preferred_element_type=F32)
            out_ref[0, pl.ds(pl.multiple_of(a * cols + start, CHIP), CHIP), :] = chip.astype(BF16)
        return carry

    lax.fori_loop(0, chips_rg, chip_column, 0, unroll=UNROLL)


def pair_body(pair, plain_ref, signed_ref, a_ref, b_ref, *rest):
    if pair == 1:
        before_ref, out_ref, product, looked = rest
    else:
        out_ref, product, looked = rest
    chips_az = plain_ref.shape[1] // LANES
    cols = a_ref.shape[1] // chips_az
    looks = cols // LOOK_RG
    for t in range(2):
        for a in range(chips_az):
            first = a_ref[t, a * cols : (a + 1) * cols, :].astype(F32)
            second = b_ref[t, a * cols : (a + 1) * cols, :].astype(F32)
            product[0] = first * second
            product[1] = pltpu.roll(first, CHIP, 1) * second
            product[2] = first * first
            product[3] = second * second
            for q in range(4):
                total = product[q, pl.ds(0, looks, stride=LOOK_RG), :]
                for k in range(1, LOOK_RG):
                    total = total + product[q, pl.ds(k, looks, stride=LOOK_RG), :]
                row = (q * 2 + t) * looks
                looked[row : row + looks, a * LANES : (a + 1) * LANES] = total

    value = looked[...]
    top = value.astype(BF16)
    low = (value - top.astype(F32)).astype(BF16)

    def line_sums(matrix_ref):
        dims = (((1,), (1,)), ((), ()))
        matrix = matrix_ref[...]
        return lax.dot_general(matrix, top, dims, preferred_element_type=F32) + lax.dot_general(
            matrix, low, dims, preferred_element_type=F32
        )

    plain = line_sums(plain_ref)
    signed = line_sums(signed_ref)
    lane = lane_index(plain.shape)
    real = lane < LANES // 4
    by_32, by_64, by_96 = (pltpu.roll(plain, k, 1) for k in (32, 64, 96))
    power_first = jnp.where(real, by_64, by_96)
    power_second = jnp.where(real, by_32, by_64)
    value = jnp.where(real, plain, signed) / jnp.sqrt((power_first + EPSILON) * (power_second + EPSILON))
    if pair == 1:
        value = jnp.where(lane < CHIP, before_ref[...], pltpu.roll(value, CHIP, 1))
    out_ref[...] = value


def correlate_body(other, me_ref, ref_ref, s0_ref, s1_ref, out_ref, sums):
    half_chips = ref_ref.shape[1] // CHIP
    chips = s0_ref.shape[1] // CHIP
    half = lax.rem(me_ref[0], 2)
    base = (1 - half if other else half) * half_chips
    lane = lane_index((8, LANES))
    sign = jnp.where(lane < CHIP, 1.0, -1.0)

    def fold(value):
        total = value[0:8]
        for k in range(1, CHIP // 8):
            total = total + value[8 * k : 8 * k + 8]
        return total

    for t in range(2):

        def one_chip(k, carry):
            row = pl.multiple_of(k * CHIP, CHIP)
            source = pl.multiple_of(jnp.minimum(base + k, chips - 1) * CHIP, CHIP)
            ref = ref_ref[t, pl.ds(row, CHIP), :].astype(F32)
            turned = pltpu.roll(ref, CHIP, 1)
            power = jnp.sum(fold(ref * ref), axis=0, keepdims=True)
            for d, s_ref in enumerate((s0_ref, s1_ref)):
                sec = s_ref[t, pl.ds(source, CHIP), :].astype(F32)
                at = (d * 2 + t) * 16 + k
                sums[0, pl.ds(at, 1), :] = jnp.sum(fold(ref * sec), axis=0, keepdims=True)
                sums[1, pl.ds(at, 1), :] = jnp.sum(fold(turned * sec) * sign, axis=0, keepdims=True)
                sums[2, pl.ds(at, 1), :] = jnp.sum(fold(sec * sec), axis=0, keepdims=True)
                sums[3, pl.ds(at, 1), :] = power
            return carry

        lax.fori_loop(0, half_chips, one_chip, 0)
        for d in range(2):
            at = (d * 2 + t) * 16 + half_chips
            sums[:, at : at + 16 - half_chips, :] = jnp.zeros((4, 16 - half_chips, LANES), F32)
    real, imag, sec_power, ref_power = (jnp.sum(sums[q], axis=1, keepdims=True) for q in range(4))
    denominator = jnp.sqrt((ref_power + EPSILON) * (sec_power + EPSILON))
    wide = lane_index(out_ref.shape)
    out_ref[...] = jnp.where(wide == 0, real, imag) / denominator


def per_device(acquisitions, shifts, fractions, ref_dates):
    dates, tiles, parts, rows, cols = acquisitions.shape
    group = lax.axis_size("date")
    strips = lax.axis_size("strip")
    me = lax.axis_index("date")
    me_one = me.reshape(1).astype(jnp.int32)
    chips_az = (rows - 2 * MARGIN) // CHIP
    chips_rg = cols // CHIP
    chips = chips_az * chips_rg
    lines = chips * CHIP
    looks = cols // LOOK_RG
    blocks = chips_az * CHIP // LOOK_AZ
    piece = -(-lines // (group * 8)) * 8
    shape = jax.ShapeDtypeStruct
    image_bytes = rows * cols * 2
    images = acquisitions.transpose(0, 1, 2, 4, 3)
    shifts = shifts.transpose(0, 1, 3, 2, 4)
    fractions = fractions.transpose(0, 1, 3, 2, 4)
    owners = ref_dates // dates

    table = jnp.asarray(tap_table())
    plain, signed = (jnp.asarray(m) for m in look_matrices(chips_az * CHIP))

    left = lax.ppermute(images[:, :, :, cols - EDGE :], "strip", [(i, i + 1) for i in range(strips - 1)])
    right = lax.ppermute(images[:, :, :, :EDGE], "strip", [(i + 1, i) for i in range(strips - 1)])

    def owned(step, dates_ref, me_ref):
        tile = (dates_ref[1] // dates == me_ref[0]).astype(jnp.int32)
        return (lax.rem(dates_ref[tile], dates), tile, 0, 0, 0)

    candidate = pl.pallas_call(
        functools.partial(candidate_body, group),
        out_shape=shape((piece * group, LANES), BF16),
        grid_spec=pltpu.PrefetchScalarGridSpec(
            num_scalar_prefetch=2,
            grid=(1,),
            in_specs=[pl.BlockSpec((1, 1, parts, cols, rows), owned)],
            out_specs=pl.BlockSpec((piece * group, LANES), lambda *_: (0, 0)),
            scratch_shapes=[pltpu.VMEM((parts, cols, LANES), BF16)],
        ),
        cost_estimate=pl.CostEstimate(flops=10**6, bytes_accessed=4 * image_bytes, transcendentals=0),
        compiler_params=pltpu.CompilerParams(vmem_limit_bytes=32 << 20),
    )(ref_dates, me_one, images)
    scattered = lax.all_to_all(candidate.reshape(group, piece, LANES), "date", 0, 0, tiled=True)
    reference = jnp.concatenate([lax.dynamic_slice_in_dim(scattered, owners[t], 1) for t in range(tiles)])

    def resample(d):
        def of_tile(t):
            return (d, t, 0, 0, 0)

        edge = pl.BlockSpec((1, 1, parts, EDGE, rows), of_tile)
        return pl.pallas_call(
            functools.partial(resample_body, d),
            out_shape=shape((tiles, lines, LANES), BF16),
            grid=(tiles,),
            in_specs=[
                SMEM,
                SMEM,
                pl.BlockSpec(table.shape, lambda t: (0, 0, 0), pipeline_mode=pl.Buffered(1)),
                pl.BlockSpec((1, 1, parts, cols, rows), of_tile),
                edge,
                edge,
            ],
            out_specs=pl.BlockSpec((1, lines, LANES), lambda t: (t, 0, 0)),
            scratch_shapes=[
                pltpu.VMEM((parts, cols, LANES), BF16),
                pltpu.VMEM((chips_az, parts, cols + 2 * EDGE, LANES), BF16),
            ],
            cost_estimate=pl.CostEstimate(
                flops=tiles * chips * 64 * 128 * 256 * 4, bytes_accessed=8 * image_bytes, transcendentals=0
            ),
            compiler_params=pltpu.CompilerParams(vmem_limit_bytes=32 << 20),
        )(shifts, fractions, table, images, left, right)

    def pair(index, *values):
        return call(
            functools.partial(pair_body, index),
            shape((blocks, LANES), F32),
            [VMEM] * (2 + len(values)),
            [
                pltpu.VMEM((4, cols, LANES), F32),
                pltpu.VMEM((4 * tiles * looks, chips_az * LANES), F32),
            ],
            cost=(10**8, 8 * image_bytes),
        )(plain, signed, *values)

    def correlate(other, value):
        return call(
            functools.partial(correlate_body, other),
            shape((4 * 16, LANES), F32),
            [SMEM, VMEM, VMEM, VMEM],
            [pltpu.VMEM((4, 4 * 16, LANES), F32)],
            cost=(10**7, 3 * image_bytes),
        )(me_one, value.reshape(tiles, -1, LANES), first, second)

    def exchange(value, step):
        other = lax.ppermute(value, "date", [(i, i ^ step) for i in range(group)])
        high = (me & step) != 0
        return jnp.concatenate([jnp.where(high, other, value), jnp.where(high, value, other)], axis=1)

    def after(value, *events):
        return lax.optimization_barrier((value,) + events)[0]

    first = resample(0)
    following = lax.ppermute(first, "date", [(i + 1, i) for i in range(group - 1)])
    reference = exchange(after(reference, first), 16)
    second = resample(1)
    reference = exchange(after(reference, second), 8)
    looked = pair(0, first, second)
    reference = exchange(after(reference, looked), 4)
    looked = pair(1, second, following, looked)
    reference = exchange(after(reference, looked), 2)
    relayed = lax.all_to_all(looked.reshape(group, -1, LANES), "date", 0, 0, tiled=True)
    other = lax.ppermute(reference, "date", [(i, i ^ 1) for i in range(group)])

    relayed = relayed.reshape(group, blocks // group, 2, 2, tiles, looks)
    coherence = relayed.transpose(3, 0, 2, 4, 1, 5).reshape(2, 2 * group, tiles, blocks // group, looks)
    coherence = coherence[:, : 2 * group - 1]

    here = correlate(False, reference)
    there = correlate(True, other)
    half = me & 1
    half_chips = piece * group // 2 // CHIP
    low = jnp.where(half == 0, here, there).reshape(4, 16, LANES)[:, :half_chips, :2]
    high = jnp.where(half == 0, there, here).reshape(4, 16, LANES)[:, : chips - half_chips, :2]
    chip_corr = jnp.concatenate([low, high], axis=1).reshape(dates, tiles, chips_az, chips_rg, 2)
    return chip_corr.transpose(4, 0, 1, 2, 3), coherence


def solution(mesh):
    return jax.shard_map(
        per_device,
        mesh=mesh,
        in_specs=(
            P("date", None, None, None, "strip"),
            P(None, "date", None, None, "strip"),
            P(None, "date", None, None, "strip"),
            P(),
        ),
        out_specs=(P(None, "date", None, None, "strip"), P(None, None, None, "date", "strip")),
        check_vma=False,
    )
```

time: 464 us -> 104 us (0.22)
  waiting for transfers between devices: 244 us -> 14 us
  local copies, waits for them, and re-layouts: 107 us -> 7.26 us
  other arithmetic: 43.7 us -> 0.26 us
  Pallas kernels: 0 us -> 38.5 us
  matrix products: 27 us -> 0 us
  starting transfers between devices: 18.6 us -> 37.2 us
  between operations: 19.7 us -> 4.74 us
    psum x1 -> x0, waiting for transfers between devices: 244 us -> none  [spread(): return lax.psum(kept, axis)]
    pallas_call x0 -> x7, Pallas kernels: none -> 38.5 us  [the longest x2 23.2 us: resample(): pl.pallas_call(functools.partial(resample_body, d), out_shape=shape((tile...]
    dot_general x2 -> x0, matrix products: 27 us -> none  [the longest x1 13.8 us: resample(): jnp.einsum('dtcariv,dtarjv->dtcarij', partial_rows, across, preferred_ele...]
    add x7 -> x0, local copies, waits for them, and re-layouts: 22.2 us -> none  [the longest x1 7.41 us: multilook_pairs(): power_later = later_real * later_real + later_imag * later_imag]
    reduce_sum x7 -> x0, other arithmetic: 21.6 us -> none  [the longest x4 12.9 us: box_sum(): return jnp.sum(blocked, axis=(3, 5))]
    reshape x2 -> x1, local copies, waits for them, and re-layouts: 15.9 us -> 0.08 us  [per_device(): jnp.concatenate([low, high], axis=1)]
    ppermute x2 -> x8, starting transfers between devices: 7.67 us -> 22.5 us  [the longest x4 9.58 us: exchange(): other = lax.ppermute(value, 'date', [(i, i ^ step) for i in range(group)])]
    unnamed x91 -> x24, local copies, waits for them, and re-layouts: 20.8 us -> 6.27 us
  transfers between devices with their start and end apart: 4 -> 10, of which waited for: 1 -> 5; matrix products, arithmetic and copies ran while one was open for 11% -> 2% of each run, Pallas kernels for 0% -> 32%
where the time goes in v1:
time: 104 us; the launch traced here: 102 us
  Pallas kernels  38.5 us (37%)
  starting transfers between devices  37.2 us (36%)
  waiting for transfers between devices  14 us (13%)
  local copies, waits for them, and re-layouts  7.26 us (7%)
  between operations  4.74 us (5%)
    pallas_call x2, Pallas kernels, resample(): pl.pallas_call(functools.partial(resample_body, d), out_shape=shape((tile...  23.2 us
    all_to_all x1, starting transfers between devices, per_device(): lax.all_to_all(candidate.reshape(group, piece, LANES), 'date', 0, 0, tile...  10 us
    ppermute x4, starting transfers between devices, exchange(): other = lax.ppermute(value, 'date', [(i, i ^ step) for i in range(group)])  9.58 us
    all_to_all x1, waiting for transfers between devices, per_device(): lax.all_to_all(looked.reshape(group, -1, LANES), 'date', 0, 0, tiled=True)  8.12 us
    pallas_call x2, Pallas kernels, correlate(): call(functools.partial(correlate_body, other), shape((4 * 16, LANES), F32...  7.41 us
    unnamed x24, local copies, waits for them, and re-layouts  6.27 us
    pallas_call x2, Pallas kernels, pair(): call(functools.partial(pair_body, index), shape((blocks, LANES), F32), [V...  6.21 us
    ppermute x4, waiting for transfers between devices, exchange(): other = lax.ppermute(value, 'date', [(i, i ^ step) for i in range(group)])  5.74 us
  transfers between devices with their start and end apart: 10, of which 5 were waited for; matrix products, arithmetic and copies ran while one was open for 2% of the time, Pallas kernels for 32%

profile of v1, /device:TPU:19, one launch (start us, length us, event | category | flops | bytes accessed | tf_op | source)
XLA Modules:
  0.0 102.0 jit_solution(863306646799038927)
XLA Ops:
  0.6 0.0 copy-start.9
  0.6 0.0 copy-start
  0.7 1.5 %copy-done = bf16[2,2,2,344,320]{3,4,2,1,0:T(8,128)(2,1)S(1)} copy-done((bf16[2,2,2,344,320]{3,4,2,1,0:T(8,128)(2,1)S(1)}, bf16[2,2,2,344,320]{3,4,2,1,0:T(8,128)(2,1)}, u32[]{:S(2)}) %copy-start) | copy-done | bytes 1761304
  2.2 0.0 copy-start.8
  2.2 0.7 copy-done.8
  2.8 0.0 copy-start.1
  2.9 0.0 copy-start.6
  2.9 0.0 copy-start.7
  2.9 1.7 %shard_map.86 = bf16[1792,128]{1,0:T(8,128)(2,1)} custom-call(s32[2]{0:T(128)S(1)} %copy-done.8, s32[1]{0:T(128)} %bitcast.me_ref, bf16[2,2,2,320,344]{4,3,2,1,0:T(8,128)(2,1)S(1)} %bitcast.20), custom_call_target="tpu_custom_call" | custom-call | flops 1000000 | bytes 880640 | tf_op jit(solution)/shard_map/pallas_call | solution.py:275
  4.5 10.0 %all-to-all-start = ((bf16[32,56,128]{2,1,0:T(8,128)(2,1)}), bf16[32,56,128]{2,1,0:T(8,128)(2,1)S(1)}, u32[]{:S(2)}, u32[]{:S(2)}) async-start(bf16[32,56,128]{2,1,0:T(8,128)(2,1)} %bitcast.2), calls=%async_computation | async-start | bytes 917504 | tf_op jit(solution)/shard_map/all_to_all | solution.py:288
  14.5 0.0 copy-done.1
  14.6 3.2 %collective-permute-start = (bf16[2,2,2,16,344]{4,3,2,1,0:T(8,128)(2,1)S(1)}, bf16[2,2,2,16,344]{4,3,2,1,0:T(8,128)(2,1)S(1)}, u32[]{:S(2)}, u32[]{:S(2)}) collective-permute-start(bf16[2,2,2,16,344]{4,3,2,1,0:T(8,128)(2,1)S(1)} %get-tuple-element.15), channel_id=1, source_target_pairs={{0,1},{1,2},{2,3},{3,4},{4,5},{5,6},{6,7},{8,9},{9,10},{10,11},{11... | collective-permute-start | bytes 264200 | tf_op jit(solution)/shard_map/ppermute | solution.py:268
  17.8 3.6 %collective-permute-start.1 = (bf16[2,2,2,16,344]{4,3,2,1,0:T(8,128)(2,1)S(1)}, bf16[2,2,2,16,344]{4,3,2,1,0:T(8,128)(2,1)S(1)}, u32[]{:S(2)}, u32[]{:S(2)}) collective-permute-start(bf16[2,2,2,16,344]{4,3,2,1,0:T(8,128)(2,1)S(1)} %get-tuple-element.14), channel_id=1, source_target_pairs={{1,0},{2,1},{3,2},{4,3},{5,4},{6,5},{7,6},{9,8},{10,9},{11,10},{12... | collective-permute-start | bytes 264200 | tf_op jit(solution)/shard_map/ppermute | solution.py:269
  21.4 0.0 copy-done.9
  21.4 0.6 fusion.1
  25.9 0.0 collective-permute-done.left_ref
  25.9 0.1 collective-permute-done.1.right_ref
  26.0 0.0 copy-done.6
  26.0 0.0 copy-done.7
  26.0 0.0 copy-start.2
  26.0 1.2 %copy-done.2 = bf16[64,64,128]{2,1,0:T(8,128)(2,1)S(1)} copy-done((bf16[64,64,128]{2,1,0:T(8,128)(2,1)S(1)}, bf16[64,64,128]{2,1,0:T(8,128)(2,1)}, u32[]{:S(2)}) %copy-start.2) | copy-done | bytes 1048600
  27.3 12.0 %shard_map.87.a_ref.s0_ref = bf16[2,1600,128]{2,1,0:T(8,128)(2,1)} custom-call(s32[2,2,5,2,5]{4,3,2,1,0:T(2,128)S(1)} %bitcast.24, s32[2,2,5,2,5]{4,3,2,1,0:T(2,128)S(1)} %bitcast.26, bf16[64,64,128]{2,1,0:T(8,128)(2,1)S(1)} %copy-done.2, bf16[2,2,2,320,344]{4,3,2,1,0:T(8,128)(2,1)S(1)} %bitcast.22, ...), custom_call_target="tpu_custom_call" | custom-call | flops 419430400 | bytes 1761280 | tf_op jit(solution)/shard_map/pallas_call | solution.py:296
  39.2 4.0 %collective-permute-start.5 = (bf16[2,1600,128]{2,1,0:T(8,128)(2,1)}, bf16[2,1600,128]{2,1,0:T(8,128)(2,1)}, u32[]{:S(2)}, u32[]{:S(2)}) collective-permute-start(bf16[2,1600,128]{2,1,0:T(8,128)(2,1)} %shard_map.87.a_ref.s0_ref), channel_id=1, source_target_pairs={{8,0},{16,8},{24,16},{32,24},{40,32},{48,40},{56,48},{64,56},{72,6... | collective-permute-start | bytes 2457608 | tf_op jit(solution)/shard_map/ppermute | solution.py:349
  43.3 0.0 all-to-all-done
  43.3 4.7 %collective-permute-start.2 = (bf16[2,56,128]{2,1,0:T(8,128)(2,1)S(1)}, bf16[2,56,128]{2,1,0:T(8,128)(2,1)S(1)}, u32[]{:S(2)}, u32[]{:S(2)}) collective-permute-start(bf16[2,56,128]{2,1,0:T(8,128)(2,1)S(1)} %pad_maximum_fusion.4), channel_id=1, source_target_pairs={{0,128},{8,136},{16,144},{24,152},{32,160},{40,168},{48,176},{56,1... | collective-permute-start | bytes 86024 | tf_op jit(solution)/shard_map/ppermute | solution.py:341
  48.0 0.0 copy-start.3
  48.0 1.2 %copy-done.3 = bf16[64,64,128]{2,1,0:T(8,128)(2,1)S(1)} copy-done((bf16[64,64,128]{2,1,0:T(8,128)(2,1)S(1)}, bf16[64,64,128]{2,1,0:T(8,128)(2,1)}, u32[]{:S(2)}) %copy-start.3) | copy-done | bytes 1048600
  49.2 0.0 copy-start.4
  49.2 0.0 copy-start.5
  49.2 11.2 %shard_map.88.b_ref.a_ref.s1_ref = bf16[2,1600,128]{2,1,0:T(8,128)(2,1)S(1)} custom-call(s32[2,2,5,2,5]{4,3,2,1,0:T(2,128)S(1)} %bitcast.25, s32[2,2,5,2,5]{4,3,2,1,0:T(2,128)S(1)} %bitcast.27, bf16[64,64,128]{2,1,0:T(8,128)(2,1)S(1)} %copy-done.3, bf16[2,2,2,320,344]{4,3,2,1,0:T(8,128)(2,1)S(1)} %bitcast.23, ...), custom_call_target="tpu_custom_call" | custom-call | flops 419430400 | bytes 1761280 | tf_op jit(solution)/shard_map/pallas_call | solution.py:296
  60.4 0.0 collective-permute-done.2
  60.5 0.8 collective-permute-start.3
  61.3 0.0 copy-done.4
  61.3 0.0 copy-done.5
  61.3 2.8 %shard_map.89.rest_0_ = f32[64,128]{1,0:T(8,128)S(1)} custom-call(bf16[64,640]{1,0:T(8,128)(2,1)S(1)} %copy-done.4, bf16[64,640]{1,0:T(8,128)(2,1)S(1)} %copy-done.5, bf16[2,1600,128]{2,1,0:T(8,128)(2,1)} %shard_map.87.a_ref.s0_ref, bf16[2,1600,128]{2,1,0:T(8,128)(2,1)S(1)} %shard_map.88.b_ref.a_ref.s1_ref), custom_call_target="tpu_custom_call" | custom-call | flops 100000000 | bytes 1761280 | tf_op jit(solution)/shard_map/pallas_call | solution.py:320
  64.1 1.1 %collective-permute-done.3 = bf16[2,112,128]{2,1,0:T(8,128)(2,1)S(1)} collective-permute-done((bf16[2,112,128]{2,1,0:T(8,128)(2,1)S(1)}, bf16[2,112,128]{2,1,0:T(8,128)(2,1)S(1)}, u32[]{:S(2)}, u32[]{:S(2)}) %collective-permute-start.3) | collective-permute-done | bytes 57376 | tf_op jit(solution)/shard_map/ppermute | solution.py:341
  65.2 0.1 collective-permute-start.4
  65.3 0.0 collective-permute-done.5.b_ref
  65.3 3.5 %shard_map.90 = f32[64,128]{1,0:T(8,128)} custom-call(bf16[64,640]{1,0:T(8,128)(2,1)S(1)} %copy-done.4, bf16[64,640]{1,0:T(8,128)(2,1)S(1)} %copy-done.5, bf16[2,1600,128]{2,1,0:T(8,128)(2,1)S(1)} %shard_map.88.b_ref.a_ref.s1_ref, bf16[2,1600,128]{2,1,0:T(8,128)(2,1)} %collective-permute-done.5.b_ref, f32[64,128]{1,0:T(8,128)S(1)} %shard_map.89.rest_0_), custom_call_target="tpu_custom_call" | custom-call | flops 100000000 | bytes 1761280 | tf_op jit(solution)/shard_map/pallas_call | solution.py:320
  68.7 0.2 collective-permute-done.4
  68.9 4.0 %collective-permute-start.6 = (bf16[2,448,128]{2,1,0:T(8,128)(2,1)S(1)}, bf16[2,448,128]{2,1,0:T(8,128)(2,1)S(1)}, u32[]{:S(2)}, u32[]{:S(2)}) collective-permute-start(bf16[2,448,128]{2,1,0:T(8,128)(2,1)S(1)} %pad_maximum_fusion.1), channel_id=1, source_target_pairs={{0,16},{8,24},{16,0},{24,8},{32,48},{40,56},{48,32},{56,40},{64,80... | collective-permute-start | bytes 688136 | tf_op jit(solution)/shard_map/ppermute | solution.py:341
  73.0 4.5 %collective-permute-done.6 = bf16[2,448,128]{2,1,0:T(8,128)(2,1)S(1)} collective-permute-done((bf16[2,448,128]{2,1,0:T(8,128)(2,1)S(1)}, bf16[2,448,128]{2,1,0:T(8,128)(2,1)S(1)}, u32[]{:S(2)}, u32[]{:S(2)}) %collective-permute-start.6) | collective-permute-done | bytes 229408 | tf_op jit(solution)/shard_map/ppermute | solution.py:341
  77.6 2.1 %collective-permute-start.7 = (bf16[2,896,128]{2,1,0:T(8,128)(2,1)S(1)}, bf16[2,896,128]{2,1,0:T(8,128)(2,1)S(1)}, u32[]{:S(2)}, u32[]{:S(2)}) collective-permute-start(bf16[2,896,128]{2,1,0:T(8,128)(2,1)S(1)} %pad_maximum_fusion.ref_ref), channel_id=1, source_target_pairs={{0,8},{8,0},{16,24},{24,16},{32,40},{40,32},{48,56},{56,48},{64,72... | collective-permute-start | bytes 1376264 | tf_op jit(solution)/shard_map/ppermute | solution.py:358
  79.7 4.6 %all-to-all-start.1 = ((f32[32,2,128]{2,1,0:T(2,128)}), f32[32,2,128]{2,1,0:T(2,128)S(1)}, u32[]{:S(2)}, u32[]{:S(2)}) async-start(f32[32,2,128]{2,1,0:T(2,128)} %bitcast.10), calls=%async_computation.1 | async-start | bytes 65536 | tf_op jit(solution)/shard_map/all_to_all | solution.py:357
  84.3 8.1 %all-to-all-done.1 = f32[32,2,128]{2,1,0:T(2,128)S(1)} async-done(((f32[32,2,128]{2,1,0:T(2,128)}), f32[32,2,128]{2,1,0:T(2,128)S(1)}, u32[]{:S(2)}, u32[]{:S(2)}) %all-to-all-start.1) | async-done | bytes 32800 | tf_op jit(solution)/shard_map/all_to_all | solution.py:357
  92.5 0.1 copy.18
  92.6 0.2 copy.19
  92.7 0.8 copy.21
  93.5 3.7 %shard_map.91 = f32[64,128]{1,0:T(8,128)S(1)} custom-call(s32[1]{0:T(128)} %bitcast.me_ref, bf16[2,896,128]{2,1,0:T(8,128)(2,1)S(1)} %pad_maximum_fusion.ref_ref, bf16[2,1600,128]{2,1,0:T(8,128)(2,1)} %shard_map.87.a_ref.s0_ref, bf16[2,1600,128]{2,1,0:T(8,128)(2,1)S(1)} %shard_map.88.b_ref.a_ref.s1_ref), custom_call_target="tpu_custom_call" | custom-call | flops 10000000 | bytes 660480 | tf_op jit(solution)/shard_map/pallas_call | solution.py:332
  97.2 0.0 collective-permute-done.7.ref_ref
  97.2 3.7 %shard_map.92 = f32[64,128]{1,0:T(8,128)S(1)} custom-call(s32[1]{0:T(128)} %bitcast.me_ref, bf16[2,896,128]{2,1,0:T(8,128)(2,1)S(1)} %collective-permute-done.7.ref_ref, bf16[2,1600,128]{2,1,0:T(8,128)(2,1)} %shard_map.87.a_ref.s0_ref, bf16[2,1600,128]{2,1,0:T(8,128)(2,1)S(1)} %shard_map.88.b_ref.a_ref.s1_ref), custom_call_target="tpu_custom_call" | custom-call | flops 10000000 | bytes 660480 | tf_op jit(solution)/shard_map/pallas_call | solution.py:332
  101.0 0.1 copy.22
  101.1 0.1 copy.23
  101.2 0.1 pad_maximum_fusion.5
  101.3 0.1 reshape.32
  101.3 0.6 copy.20
  (13 shorter events, 0.2 us)
Async XLA Ops:
  0.6 20.8 %copy-start.9 = (s32[2]{0:T(128)S(1)}, s32[2]{0:T(128)}, u32[]{:S(2)}) copy-start(s32[2]{0:T(128)} %dates_ref.1) | copy-start | bytes 28
  0.6 1.5 %copy-start = (bf16[2,2,2,344,320]{3,4,2,1,0:T(8,128)(2,1)S(1)}, bf16[2,2,2,344,320]{3,4,2,1,0:T(8,128)(2,1)}, u32[]{:S(2)}) copy-start(bf16[2,2,2,344,320]{3,4,2,1,0:T(8,128)(2,1)} %param.7) | copy-start | bytes 5283844
  2.2 0.7 copy-start.8
  2.8 11.7 %copy-start.1 = (bf16[2,2,2,344,320]{3,4,2,1,0:T(8,128)(2,1)S(1)}, bf16[2,2,2,344,320]{3,4,2,1,0:T(8,128)(2,1)}, u32[]{:S(2)}) copy-start(bf16[2,2,2,344,320]{3,4,2,1,0:T(8,128)(2,1)} %param.7) | copy-start | bytes 5283844
  2.9 23.2 %copy-start.6 = (s32[2,2,2,5,5]{4,2,3,1,0:T(2,128)S(1)}, s32[2,2,2,5,5]{4,2,3,1,0:T(2,128)}, u32[]{:S(2)}) copy-start(s32[2,2,2,5,5]{4,2,3,1,0:T(2,128)} %param.8) | copy-start | bytes 2404
  2.9 23.2 %copy-start.7 = (s32[2,2,2,5,5]{4,2,3,1,0:T(2,128)S(1)}, s32[2,2,2,5,5]{4,2,3,1,0:T(2,128)}, u32[]{:S(2)}) copy-start(s32[2,2,2,5,5]{4,2,3,1,0:T(2,128)} %param.9) | copy-start | bytes 2404
  4.5 38.8 %all-to-all-start = ((bf16[32,56,128]{2,1,0:T(8,128)(2,1)}), bf16[32,56,128]{2,1,0:T(8,128)(2,1)S(1)}, u32[]{:S(2)}, u32[]{:S(2)}) async-start(bf16[32,56,128]{2,1,0:T(8,128)(2,1)} %bitcast.2), calls=%async_computation | async-start | bytes 917504 | tf_op jit(solution)/shard_map/all_to_all | solution.py:288
  14.6 11.3 %collective-permute-start = (bf16[2,2,2,16,344]{4,3,2,1,0:T(8,128)(2,1)S(1)}, bf16[2,2,2,16,344]{4,3,2,1,0:T(8,128)(2,1)S(1)}, u32[]{:S(2)}, u32[]{:S(2)}) collective-permute-start(bf16[2,2,2,16,344]{4,3,2,1,0:T(8,128)(2,1)S(1)} %get-tuple-element.15), channel_id=1, source_target_pairs={{0,1},{1,2},{2,3},{3,4},{4,5},{5,6},{6,7},{8,9},{9,10},{10,11},{11... | collective-permute-start | bytes 264200 | tf_op jit(solution)/shard_map/ppermute | solution.py:268
  17.8 8.2 %collective-permute-start.1 = (bf16[2,2,2,16,344]{4,3,2,1,0:T(8,128)(2,1)S(1)}, bf16[2,2,2,16,344]{4,3,2,1,0:T(8,128)(2,1)S(1)}, u32[]{:S(2)}, u32[]{:S(2)}) collective-permute-start(bf16[2,2,2,16,344]{4,3,2,1,0:T(8,128)(2,1)S(1)} %get-tuple-element.14), channel_id=1, source_target_pairs={{1,0},{2,1},{3,2},{4,3},{5,4},{6,5},{7,6},{9,8},{10,9},{11,10},{12... | collective-permute-start | bytes 264200 | tf_op jit(solution)/shard_map/ppermute | solution.py:269
  26.0 1.2 %copy-start.2 = (bf16[64,64,128]{2,1,0:T(8,128)(2,1)S(1)}, bf16[64,64,128]{2,1,0:T(8,128)(2,1)}, u32[]{:S(2)}) copy-start(bf16[64,64,128]{2,1,0:T(8,128)(2,1)} %constant.37.clone.table_ref) | copy-start | bytes 3145732
  39.2 26.0 %collective-permute-start.5 = (bf16[2,1600,128]{2,1,0:T(8,128)(2,1)}, bf16[2,1600,128]{2,1,0:T(8,128)(2,1)}, u32[]{:S(2)}, u32[]{:S(2)}) collective-permute-start(bf16[2,1600,128]{2,1,0:T(8,128)(2,1)} %shard_map.87.a_ref.s0_ref), channel_id=1, source_target_pairs={{8,0},{16,8},{24,16},{32,24},{40,32},{48,40},{56,48},{64,56},{72,6... | collective-permute-start | bytes 2457608 | tf_op jit(solution)/shard_map/ppermute | solution.py:349
  43.3 17.1 %collective-permute-start.2 = (bf16[2,56,128]{2,1,0:T(8,128)(2,1)S(1)}, bf16[2,56,128]{2,1,0:T(8,128)(2,1)S(1)}, u32[]{:S(2)}, u32[]{:S(2)}) collective-permute-start(bf16[2,56,128]{2,1,0:T(8,128)(2,1)S(1)} %pad_maximum_fusion.4), channel_id=1, source_target_pairs={{0,128},{8,136},{16,144},{24,152},{32,160},{40,168},{48,176},{56,1... | collective-permute-start | bytes 86024 | tf_op jit(solution)/shard_map/ppermute | solution.py:341
  48.0 1.2 %copy-start.3 = (bf16[64,64,128]{2,1,0:T(8,128)(2,1)S(1)}, bf16[64,64,128]{2,1,0:T(8,128)(2,1)}, u32[]{:S(2)}) copy-start(bf16[64,64,128]{2,1,0:T(8,128)(2,1)} %constant.37.clone.table_ref) | copy-start | bytes 3145732
  49.2 12.1 %copy-start.4 = (bf16[64,640]{1,0:T(8,128)(2,1)S(1)}, bf16[64,640]{1,0:T(8,128)(2,1)}, u32[]{:S(2)}) copy-start(bf16[64,640]{1,0:T(8,128)(2,1)} %constant.38.clone.plain_ref) | copy-start | bytes 245764
  49.2 12.1 %copy-start.5 = (bf16[64,640]{1,0:T(8,128)(2,1)S(1)}, bf16[64,640]{1,0:T(8,128)(2,1)}, u32[]{:S(2)}) copy-start(bf16[64,640]{1,0:T(8,128)(2,1)} %constant.39.clone.signed_ref) | copy-start | bytes 245764
  60.5 4.6 %collective-permute-start.3 = (bf16[2,112,128]{2,1,0:T(8,128)(2,1)S(1)}, bf16[2,112,128]{2,1,0:T(8,128)(2,1)S(1)}, u32[]{:S(2)}, u32[]{:S(2)}) collective-permute-start(bf16[2,112,128]{2,1,0:T(8,128)(2,1)S(1)} %pad_maximum_fusion.3), channel_id=1, source_target_pairs={{0,64},{8,72},{16,80},{24,88},{32,96},{40,104},{48,112},{56,120},{... | collective-permute-start | bytes 172040 | tf_op jit(solution)/shard_map/ppermute | solution.py:341
  65.2 3.7 %collective-permute-start.4 = (bf16[2,224,128]{2,1,0:T(8,128)(2,1)S(1)}, bf16[2,224,128]{2,1,0:T(8,128)(2,1)S(1)}, u32[]{:S(2)}, u32[]{:S(2)}) collective-permute-start(bf16[2,224,128]{2,1,0:T(8,128)(2,1)S(1)} %pad_maximum_fusion.2), channel_id=1, source_target_pairs={{0,32},{8,40},{16,48},{24,56},{32,0},{40,8},{48,16},{56,24},{64,96... | collective-permute-start | bytes 344072 | tf_op jit(solution)/shard_map/ppermute | solution.py:341
  68.9 8.5 %collective-permute-start.6 = (bf16[2,448,128]{2,1,0:T(8,128)(2,1)S(1)}, bf16[2,448,128]{2,1,0:T(8,128)(2,1)S(1)}, u32[]{:S(2)}, u32[]{:S(2)}) collective-permute-start(bf16[2,448,128]{2,1,0:T(8,128)(2,1)S(1)} %pad_maximum_fusion.1), channel_id=1, source_target_pairs={{0,16},{8,24},{16,0},{24,8},{32,48},{40,56},{48,32},{56,40},{64,80... | collective-permute-start | bytes 688136 | tf_op jit(solution)/shard_map/ppermute | solution.py:341
  77.6 19.7 %collective-permute-start.7 = (bf16[2,896,128]{2,1,0:T(8,128)(2,1)S(1)}, bf16[2,896,128]{2,1,0:T(8,128)(2,1)S(1)}, u32[]{:S(2)}, u32[]{:S(2)}) collective-permute-start(bf16[2,896,128]{2,1,0:T(8,128)(2,1)S(1)} %pad_maximum_fusion.ref_ref), channel_id=1, source_target_pairs={{0,8},{8,0},{16,24},{24,16},{32,40},{40,32},{48,56},{56,48},{64,72... | collective-permute-start | bytes 1376264 | tf_op jit(solution)/shard_map/ppermute | solution.py:358
  79.7 12.8 %all-to-all-start.1 = ((f32[32,2,128]{2,1,0:T(2,128)}), f32[32,2,128]{2,1,0:T(2,128)S(1)}, u32[]{:S(2)}, u32[]{:S(2)}) async-start(f32[32,2,128]{2,1,0:T(2,128)} %bitcast.10), calls=%async_computation.1 | async-start | bytes 65536 | tf_op jit(solution)/shard_map/all_to_all | solution.py:357

commit v2 on v1

--- a/solution.py
+++ b/solution.py
@@ -17,7 +17,8 @@
 WINDOW = CHIP + 2 * MARGIN
 LANES = 128
 EDGE = 16
-UNROLL = 1
+SKEW = 16
+PACK = 16
 EPSILON = 1e-06
 
 VMEM = pl.BlockSpec(memory_space=pltpu.VMEM)
@@ -30,8 +31,8 @@
     x = np.arange(TAPS)[None, :] - (TAPS // 2 - 1) - np.arange(SUBSTEPS)[:, None] / SUBSTEPS
     weights = np.sinc(x) * (0.5 + 0.5 * np.cos(2 * np.pi * x / TAPS))
     weights = weights / weights.sum(axis=1, keepdims=True)
-    table = np.zeros((SUBSTEPS, CHIP, LANES), np.float32)
-    for line in range(CHIP):
+    table = np.zeros((SUBSTEPS, SKEW, LANES), np.float32)
+    for line in range(SKEW):
         table[:, line, line : line + TAPS] = weights
     return table.astype(jnp.bfloat16)
 
@@ -84,12 +85,12 @@
     cols, lines = x_ref.shape[-2:]
     chips_az = (lines - 2 * MARGIN) // CHIP
     lane = lane_index((cols, LANES))
-    octets = out_ref.shape[0] // 8 // group
-
-    def place(octet):
-        return (reversed_bits(octet // octets, group) * octets + octet % octets) * 8
-
-    parts = [[tile.astype(F32) for tile in lane_tiles(x_ref, stage.at[p], (0, 0, p))] for p in range(2)]
+    steps = out_ref.shape[0] // PACK // group
+
+    def place(step):
+        return (reversed_bits(step // steps, group) * steps + step % steps) * PACK
+
+    parts = [lane_tiles(x_ref, stage.at[p], (0, 0, p)) for p in range(2)]
     for a in range(chips_az):
         start = MARGIN + a * CHIP
         tile, offset = start // LANES, start % LANES
@@ -101,12 +102,12 @@
                 value = jnp.where(lane < p * CHIP + LANES - offset, value, pltpu.roll(parts[p][tile + 1], shift, 1))
             halves.append(value)
         value = jnp.where(lane < CHIP, halves[0], halves[1])
-        for k in range(cols // 8):
-            at = place(a * (cols // 8) + k)
-            out_ref[at : at + 8, :] = value[8 * k : 8 * k + 8].astype(BF16)
-    for octet in range(chips_az * cols // 8, out_ref.shape[0] // 8):
-        at = place(octet)
-        out_ref[at : at + 8, :] = jnp.zeros((8, LANES), BF16)
+        for k in range(cols // PACK):
+            at = place(a * (cols // PACK) + k)
+            out_ref[at : at + PACK, :] = value[PACK * k : PACK * (k + 1)]
+    for step in range(chips_az * cols // PACK, out_ref.shape[0] // PACK):
+        at = place(step)
+        out_ref[at : at + PACK, :] = jnp.zeros((PACK, LANES), BF16)
 
 
 def resample_body(date, shift_ref, frac_ref, table_ref, x_ref, left_ref, right_ref, out_ref, stage, window):
@@ -136,22 +137,61 @@
     half = lane_index((depth, LANES)) < CHIP
 
     def skewed(fraction, offset):
-        return pltpu.roll(table_ref[fraction], offset, 1)
-
-    def chip_column(r, carry):
-        start = pl.multiple_of(r * CHIP, CHIP)
+        base = table_ref[fraction]
+        return jnp.concatenate([pltpu.roll(base, offset + k, 1) for k in range(0, CHIP, SKEW)], axis=0)
+
+    for r in range(chips_rg):
+        start = r * CHIP
+        firsts = []
         for a in range(chips_az):
             azimuth = skewed(frac_ref[0, date, a, t, r], shift_ref[0, date, a, t, r] + 9)
-            across = skewed(frac_ref[1, date, a, t, r], shift_ref[1, date, a, t, r] + 13)
             both = jnp.concatenate([azimuth, azimuth], axis=0)
-            data = jnp.concatenate([window[a, p, pl.ds(start, depth), :] for p in range(2)], axis=0)
+            data = jnp.concatenate([window[a, p, start : start + depth, :] for p in range(2)], axis=0)
             partial = lax.dot_general(data, both, (((1,), (1,)), ((), ())), preferred_element_type=F32)
-            partial = jnp.where(half, partial[:depth], partial[depth:]).astype(BF16)
-            chip = jnp.dot(across[:, :depth], partial, preferred_element_type=F32)
-            out_ref[0, pl.ds(pl.multiple_of(a * cols + start, CHIP), CHIP), :] = chip.astype(BF16)
-        return carry
-
-    lax.fori_loop(0, chips_rg, chip_column, 0, unroll=UNROLL)
+            firsts.append(jnp.where(half, partial[:depth], partial[depth:]).astype(BF16))
+        if r:
+            for a in range(chips_az):
+                across = skewed(frac_ref[1, date, a, t, r - 1], shift_ref[1, date, a, t, r - 1] + 13)
+                chip = jnp.dot(across[:, :depth], before[a], preferred_element_type=F32)
+                out_ref[0, a * cols + start - CHIP : a * cols + start, :] = chip.astype(BF16)
+        before = firsts
+    for a in range(chips_az):
+        across = skewed(frac_ref[1, date, a, t, r], shift_ref[1, date, a, t, r] + 13)
+        chip = jnp.dot(across[:, :depth], before[a], preferred_element_type=F32)
+        out_ref[0, a * cols + start : a * cols + start + CHIP, :] = chip.astype(BF16)
+
+
+def resample_call(d, shifts, fractions, table, images, left, right):
+    dates, tiles, parts, cols, rows = images.shape
+    chips_az = (rows - 2 * MARGIN) // CHIP
+    lines = chips_az * cols
+
+    def of_tile(t):
+        return (d, t, 0, 0, 0)
+
+    edge = pl.BlockSpec((1, 1, parts, EDGE, rows), of_tile)
+    return pl.pallas_call(
+        functools.partial(resample_body, d),
+        out_shape=jax.ShapeDtypeStruct((tiles, lines, LANES), BF16),
+        grid=(tiles,),
+        in_specs=[
+            SMEM,
+            SMEM,
+            pl.BlockSpec(table.shape, lambda t: (0, 0, 0)),
+            pl.BlockSpec((1, 1, parts, cols, rows), of_tile),
+            edge,
+            edge,
+        ],
+        out_specs=pl.BlockSpec((1, lines, LANES), lambda t: (t, 0, 0)),
+        scratch_shapes=[
+            pltpu.VMEM((parts, cols, LANES), BF16),
+            pltpu.VMEM((chips_az, parts, cols + 2 * EDGE, LANES), BF16),
+        ],
+        cost_estimate=pl.CostEstimate(
+            flops=tiles * lines * 128 * 256 * 4, bytes_accessed=16 * rows * cols, transcendentals=0
+        ),
+        compiler_params=pltpu.CompilerParams(vmem_limit_bytes=60 << 20),
+    )(shifts, fractions, table, images, left, right)
 
 
 def pair_body(pair, plain_ref, signed_ref, a_ref, b_ref, *rest):
@@ -166,14 +206,15 @@
         for a in range(chips_az):
             first = a_ref[t, a * cols : (a + 1) * cols, :].astype(F32)
             second = b_ref[t, a * cols : (a + 1) * cols, :].astype(F32)
-            product[0] = first * second
-            product[1] = pltpu.roll(first, CHIP, 1) * second
-            product[2] = first * first
-            product[3] = second * second
+            work = product.at[a % 2]
+            work[0] = first * second
+            work[1] = pltpu.roll(first, CHIP, 1) * second
+            work[2] = first * first
+            work[3] = second * second
             for q in range(4):
-                total = product[q, pl.ds(0, looks, stride=LOOK_RG), :]
+                total = work[q, pl.ds(0, looks, stride=LOOK_RG), :]
                 for k in range(1, LOOK_RG):
-                    total = total + product[q, pl.ds(k, looks, stride=LOOK_RG), :]
+                    total = total + work[q, pl.ds(k, looks, stride=LOOK_RG), :]
                 row = (q * 2 + t) * looks
                 looked[row : row + looks, a * LANES : (a + 1) * LANES] = total
 
@@ -215,24 +256,22 @@
             total = total + value[8 * k : 8 * k + 8]
         return total
 
+    def total(value):
+        return jnp.sum(fold(value), axis=0, keepdims=True)
+
     for t in range(2):
-
-        def one_chip(k, carry):
-            row = pl.multiple_of(k * CHIP, CHIP)
+        for k in range(half_chips):
             source = pl.multiple_of(jnp.minimum(base + k, chips - 1) * CHIP, CHIP)
-            ref = ref_ref[t, pl.ds(row, CHIP), :].astype(F32)
+            ref = ref_ref[t, k * CHIP : (k + 1) * CHIP, :].astype(F32)
             turned = pltpu.roll(ref, CHIP, 1)
-            power = jnp.sum(fold(ref * ref), axis=0, keepdims=True)
+            power = total(ref * ref)
             for d, s_ref in enumerate((s0_ref, s1_ref)):
                 sec = s_ref[t, pl.ds(source, CHIP), :].astype(F32)
                 at = (d * 2 + t) * 16 + k
-                sums[0, pl.ds(at, 1), :] = jnp.sum(fold(ref * sec), axis=0, keepdims=True)
-                sums[1, pl.ds(at, 1), :] = jnp.sum(fold(turned * sec) * sign, axis=0, keepdims=True)
-                sums[2, pl.ds(at, 1), :] = jnp.sum(fold(sec * sec), axis=0, keepdims=True)
-                sums[3, pl.ds(at, 1), :] = power
-            return carry
-
-        lax.fori_loop(0, half_chips, one_chip, 0)
+                sums[0, at : at + 1, :] = total(ref * sec)
+                sums[1, at : at + 1, :] = jnp.sum(fold(turned * sec) * sign, axis=0, keepdims=True)
+                sums[2, at : at + 1, :] = total(sec * sec)
+                sums[3, at : at + 1, :] = power
         for d in range(2):
             at = (d * 2 + t) * 16 + half_chips
             sums[:, at : at + 16 - half_chips, :] = jnp.zeros((4, 16 - half_chips, LANES), F32)
@@ -254,7 +293,8 @@
     lines = chips * CHIP
     looks = cols // LOOK_RG
     blocks = chips_az * CHIP // LOOK_AZ
-    piece = -(-lines // (group * 8)) * 8
+    near = 8
+    piece = -(-lines // (near * 2 * PACK)) * 2 * PACK
     shape = jax.ShapeDtypeStruct
     image_bytes = rows * cols * 2
     images = acquisitions.transpose(0, 1, 2, 4, 3)
@@ -265,56 +305,44 @@
     table = jnp.asarray(tap_table())
     plain, signed = (jnp.asarray(m) for m in look_matrices(chips_az * CHIP))
 
-    left = lax.ppermute(images[:, :, :, cols - EDGE :], "strip", [(i, i + 1) for i in range(strips - 1)])
-    right = lax.ppermute(images[:, :, :, :EDGE], "strip", [(i + 1, i) for i in range(strips - 1)])
+    high_edge = images[:, :, :, cols - EDGE :]
+    low_edge = images[:, :, :, :EDGE]
+    left = lax.ppermute(high_edge, "strip", [(i, i + 1) for i in range(strips - 1)])
+    right = lax.ppermute(low_edge, "strip", [(i + 1, i) for i in range(strips - 1)])
+
+    def after(value, *events):
+        return lax.optimization_barrier((value, events))[0]
 
     def owned(step, dates_ref, me_ref):
         tile = (dates_ref[1] // dates == me_ref[0]).astype(jnp.int32)
         return (lax.rem(dates_ref[tile], dates), tile, 0, 0, 0)
 
     candidate = pl.pallas_call(
-        functools.partial(candidate_body, group),
-        out_shape=shape((piece * group, LANES), BF16),
+        functools.partial(candidate_body, near),
+        out_shape=shape((piece * near, LANES), BF16),
         grid_spec=pltpu.PrefetchScalarGridSpec(
             num_scalar_prefetch=2,
             grid=(1,),
             in_specs=[pl.BlockSpec((1, 1, parts, cols, rows), owned)],
-            out_specs=pl.BlockSpec((piece * group, LANES), lambda *_: (0, 0)),
+            out_specs=pl.BlockSpec((piece * near, LANES), lambda *_: (0, 0)),
             scratch_shapes=[pltpu.VMEM((parts, cols, LANES), BF16)],
         ),
         cost_estimate=pl.CostEstimate(flops=10**6, bytes_accessed=4 * image_bytes, transcendentals=0),
-        compiler_params=pltpu.CompilerParams(vmem_limit_bytes=32 << 20),
-    )(ref_dates, me_one, images)
-    scattered = lax.all_to_all(candidate.reshape(group, piece, LANES), "date", 0, 0, tiled=True)
-    reference = jnp.concatenate([lax.dynamic_slice_in_dim(scattered, owners[t], 1) for t in range(tiles)])
-
-    def resample(d):
-        def of_tile(t):
-            return (d, t, 0, 0, 0)
-
-        edge = pl.BlockSpec((1, 1, parts, EDGE, rows), of_tile)
-        return pl.pallas_call(
-            functools.partial(resample_body, d),
-            out_shape=shape((tiles, lines, LANES), BF16),
-            grid=(tiles,),
-            in_specs=[
-                SMEM,
-                SMEM,
-                pl.BlockSpec(table.shape, lambda t: (0, 0, 0), pipeline_mode=pl.Buffered(1)),
-                pl.BlockSpec((1, 1, parts, cols, rows), of_tile),
-                edge,
-                edge,
-            ],
-            out_specs=pl.BlockSpec((1, lines, LANES), lambda t: (t, 0, 0)),
-            scratch_shapes=[
-                pltpu.VMEM((parts, cols, LANES), BF16),
-                pltpu.VMEM((chips_az, parts, cols + 2 * EDGE, LANES), BF16),
-            ],
-            cost_estimate=pl.CostEstimate(
-                flops=tiles * chips * 64 * 128 * 256 * 4, bytes_accessed=8 * image_bytes, transcendentals=0
-            ),
-            compiler_params=pltpu.CompilerParams(vmem_limit_bytes=32 << 20),
-        )(shifts, fractions, table, images, left, right)
+        compiler_params=pltpu.CompilerParams(vmem_limit_bytes=60 << 20),
+    )(after(ref_dates, high_edge, low_edge), me_one, images)
+    scattered = lax.all_to_all(
+        candidate.reshape(near, piece, LANES),
+        "date",
+        0,
+        0,
+        axis_index_groups=[list(range(k, k + near)) for k in range(0, group, near)],
+        tiled=True,
+    )
+    from_owner = jnp.arange(near)[None, :] == (owners % near)[:, None]
+    reference = jnp.sum(jnp.where(from_owner[:, :, None, None], scattered[None], 0), axis=1, dtype=BF16)
+    left, right = after((left, right), reference)
+
+    resample = functools.partial(resample_call, shifts=shifts, fractions=fractions, table=table, images=images, left=left, right=right)
 
     def pair(index, *values):
         return call(
@@ -322,7 +350,7 @@
             shape((blocks, LANES), F32),
             [VMEM] * (2 + len(values)),
             [
-                pltpu.VMEM((4, cols, LANES), F32),
+                pltpu.VMEM((2, 4, cols, LANES), F32),
                 pltpu.VMEM((4 * tiles * looks, chips_az * LANES), F32),
             ],
             cost=(10**8, 8 * image_bytes),
@@ -342,19 +370,22 @@
         high = (me & step) != 0
         return jnp.concatenate([jnp.where(high, other, value), jnp.where(high, value, other)], axis=1)
 
-    def after(value, *events):
-        return lax.optimization_barrier((value,) + events)[0]
-
+    def flood(value, step):
+        other = lax.ppermute(value, "date", [(i, i ^ step) for i in range(group)])
+        same = ((me ^ owners) & step) == 0
+        return jnp.where(same[:, None, None], value, other)
+
+    reference = flood(reference, 16)
     first = resample(0)
     following = lax.ppermute(first, "date", [(i + 1, i) for i in range(group - 1)])
-    reference = exchange(after(reference, first), 16)
+    reference = flood(after(reference, first), 8)
     second = resample(1)
-    reference = exchange(after(reference, second), 8)
     looked = pair(0, first, second)
     reference = exchange(after(reference, looked), 4)
     looked = pair(1, second, following, looked)
+    relayed = lax.all_to_all(looked.reshape(group, -1, LANES), "date", 0, 0, tiled=True)
     reference = exchange(after(reference, looked), 2)
-    relayed = lax.all_to_all(looked.reshape(group, -1, LANES), "date", 0, 0, tiled=True)
+    reference, relayed = lax.optimization_barrier((reference, relayed))
     other = lax.ppermute(reference, "date", [(i, i ^ 1) for i in range(group)])
 
     relayed = relayed.reshape(group, blocks // group, 2, 2, tiles, looks)
@@ -364,7 +395,7 @@
     here = correlate(False, reference)
     there = correlate(True, other)
     half = me & 1
-    half_chips = piece * group // 2 // CHIP
+    half_chips = piece * near // 2 // CHIP
     low = jnp.where(half == 0, here, there).reshape(4, 16, LANES)[:, :half_chips, :2]
     high = jnp.where(half == 0, there, here).reshape(4, 16, LANES)[:, : chips - half_chips, :2]
     chip_corr = jnp.concatenate([low, high], axis=1).reshape(dates, tiles, chips_az, chips_rg, 2)

time: 104 us -> 77.4 us (0.74)
  the two profiles are of different devices: /device:TPU:19 before, /device:TPU:7 now
where the time goes in v2:
time: 77.4 us; the launch traced here: 76.9 us
  starting transfers between devices  42 us (54%)
  Pallas kernels  17 us (22%)
  waiting for transfers between devices  11.5 us (15%)
  local copies, waits for them, and re-layouts  4.74 us (6%)
  between operations  0.88 us (1%)
    all_to_all x1, starting transfers between devices, per_device(): lax.all_to_all(looked.reshape(group, -1, LANES), 'date', 0, 0, tiled=True)  15.1 us
    pallas_call x2, Pallas kernels, resample_call(): pl.pallas_call(functools.partial(resample_body, d), out_shape=jax.ShapeDt...  8.78 us
    all_to_all x1, waiting for transfers between devices, per_device(): lax.all_to_all(looked.reshape(group, -1, LANES), 'date', 0, 0, tiled=True)  8.03 us
    ppermute x2, starting transfers between devices, flood(): other = lax.ppermute(value, 'date', [(i, i ^ step) for i in range(group)])  7.47 us
    all_to_all x1, starting transfers between devices, per_device(): lax.all_to_all(candidate.reshape(near, piece, LANES), 'date', 0, 0, axis_...  4.88 us
    ppermute x1, starting transfers between devices, per_device(): lax.ppermute(high_edge, 'strip', [(i, i + 1) for i in range(strips - 1)])  4.52 us
    pallas_call x2, Pallas kernels, pair(): call(functools.partial(pair_body, index), shape((blocks, LANES), F32), [V...  3.9 us
    ppermute x2, waiting for transfers between devices, exchange(): other = lax.ppermute(value, 'date', [(i, i ^ step) for i in range(group)])  3.48 us
  transfers between devices with their start and end apart: 10, of which 2 were waited for; matrix products, arithmetic and copies ran while one was open for 2% of the time, Pallas kernels for 15%

profile of v2, /device:TPU:7, one launch (start us, length us, event | category | flops | bytes accessed | tf_op | source)
XLA Modules:
  0.0 76.9 jit_solution(12826580570773042141)
XLA Ops:
  0.6 0.0 copy-start.7
  0.6 1.0 %fusion.1 = (bf16[2,2,2,16,344]{4,3,2,1,0:T(8,128)(2,1)S(1)}, bf16[2,2,2,16,344]{4,3,2,1,0:T(8,128)(2,1)S(1)}) fusion(bf16[2,2,2,320,344]{4,3,2,1,0:T(8,128)(2,1)} %bitcast.18), kind=kLoop, calls=%fused_computation.23 | loop fusion | bytes 352256 | tf_op jit(solution)/shard_map/slice | solution.py:309
  1.6 2.8 %shard_map.86 = bf16[1792,128]{1,0:T(8,128)(2,1)} custom-call(s32[2]{0:T(128)} %dates_ref, s32[1]{0:T(128)} %bitcast.me_ref, bf16[2,2,2,320,344]{4,3,2,1,0:T(8,128)(2,1)} %bitcast.19), custom_call_target="tpu_custom_call" | custom-call | flops 1000000 | bytes 880640 | tf_op jit(solution)/shard_map/pallas_call | solution.py:320
  4.4 4.9 %all-to-all-start = ((bf16[8,224,128]{2,1,0:T(8,128)(2,1)}), bf16[8,224,128]{2,1,0:T(8,128)(2,1)S(1)}, u32[]{:S(2)}, u32[]{:S(2)}) async-start(bf16[8,224,128]{2,1,0:T(8,128)(2,1)} %bitcast.22), calls=%async_computation | async-start | bytes 917504 | tf_op jit(solution)/shard_map/all_to_all | solution.py:333
  9.3 4.5 %collective-permute-start.1 = (bf16[2,2,2,16,344]{4,3,2,1,0:T(8,128)(2,1)S(1)}, bf16[2,2,2,16,344]{4,3,2,1,0:T(8,128)(2,1)S(1)}, u32[]{:S(2)}, u32[]{:S(2)}) collective-permute-start(bf16[2,2,2,16,344]{4,3,2,1,0:T(8,128)(2,1)S(1)} %get-tuple-element.27), channel_id=1, source_target_pairs={{0,1},{1,2},{2,3},{3,4},{4,5},{5,6},{6,7},{8,9},{9,10},{10,11},{11... | collective-permute-start | bytes 264200 | tf_op jit(solution)/shard_map/ppermute | solution.py:310
  13.8 3.2 %collective-permute-start.2 = (bf16[2,2,2,16,344]{4,3,2,1,0:T(8,128)(2,1)S(1)}, bf16[2,2,2,16,344]{4,3,2,1,0:T(8,128)(2,1)S(1)}, u32[]{:S(2)}, u32[]{:S(2)}) collective-permute-start(bf16[2,2,2,16,344]{4,3,2,1,0:T(8,128)(2,1)S(1)} %get-tuple-element.26), channel_id=1, source_target_pairs={{1,0},{2,1},{3,2},{4,3},{5,4},{6,5},{7,6},{9,8},{10,9},{11,10},{12... | collective-permute-start | bytes 264200 | tf_op jit(solution)/shard_map/ppermute | solution.py:311
  17.0 0.0 copy-done.7
  17.0 0.1 iota_compare_fusion
  17.1 0.0 all-to-all-done
  17.1 0.2 select_reduce_fusion
  17.4 6.2 %collective-permute-start = (bf16[2,224,128]{2,1,0:T(8,128)(2,1)S(1)}, bf16[2,224,128]{2,1,0:T(8,128)(2,1)S(1)}, u32[]{:S(2)}, u32[]{:S(2)}) collective-permute-start(bf16[2,224,128]{2,1,0:T(8,128)(2,1)S(1)} %select_reduce_fusion), channel_id=1, source_target_pairs={{0,128},{8,136},{16,144},{24,152},{32,160},{40,168},{48,176},{56,1... | collective-permute-start | bytes 344072 | tf_op jit(solution)/shard_map/ppermute | solution.py:374
  23.5 0.0 collective-permute-done.1.left_ref
  23.5 0.0 copy-start.5
  23.6 0.0 collective-permute-done.2.right_ref
  23.6 0.0 copy-start.6
  23.6 0.6 copy-done.5
  24.2 0.1 copy-done.6
  24.2 4.4 %shard_map.87.a_ref.s0_ref = bf16[2,1600,128]{2,1,0:T(8,128)(2,1)} custom-call(s32[2,2,5,2,5]{4,3,2,1,0:T(2,128)} %bitcast.28, s32[2,2,5,2,5]{4,3,2,1,0:T(2,128)} %bitcast.30, bf16[64,16,128]{2,1,0:T(8,128)(2,1)} %constant.52.clone.table_ref, bf16[2,2,2,320,344]{4,3,2,1,0:T(8,128)(2,1)} %bitcast.20, bf16[2,2,2,16,344]{4,3,2,1,0:T(8,128)(2,1)} %copy-done.5, ...), custom_call_target="tpu_custom_call" | custom-call | flops 419430400 | bytes 1761280 | tf_op jit(solution)/shard_map/pallas_call | solution.py:173
  28.6 0.0 copy-start.2
  28.6 0.0 copy-start.3
  28.6 0.0 copy-start.4
  28.6 3.1 %collective-permute-start.5 = (bf16[2,1600,128]{2,1,0:T(8,128)(2,1)}, bf16[2,1600,128]{2,1,0:T(8,128)(2,1)S(1)}, u32[]{:S(2)}, u32[]{:S(2)}) collective-permute-start(bf16[2,1600,128]{2,1,0:T(8,128)(2,1)} %shard_map.87.a_ref.s0_ref), channel_id=1, source_target_pairs={{8,0},{16,8},{24,16},{32,24},{40,32},{48,40},{56,48},{64,56},{72,6... | collective-permute-start | bytes 2457608 | tf_op jit(solution)/shard_map/ppermute | solution.py:380
  31.8 0.0 collective-permute-done
  31.8 0.1 broadcast_select_fusion.2
  31.9 1.3 %collective-permute-start.3 = (bf16[2,224,128]{2,1,0:T(8,128)(2,1)S(1)}, bf16[2,224,128]{2,1,0:T(8,128)(2,1)S(1)}, u32[]{:S(2)}, u32[]{:S(2)}) collective-permute-start(bf16[2,224,128]{2,1,0:T(8,128)(2,1)S(1)} %broadcast_select_fusion.2), channel_id=1, source_target_pairs={{0,64},{8,72},{16,80},{24,88},{32,96},{40,104},{48,112},{56,120},{... | collective-permute-start | bytes 344072 | tf_op jit(solution)/shard_map/ppermute | solution.py:374
  33.2 4.4 %shard_map.88.b_ref.a_ref.s1_ref = bf16[2,1600,128]{2,1,0:T(8,128)(2,1)} custom-call(s32[2,2,5,2,5]{4,3,2,1,0:T(2,128)} %bitcast.29, s32[2,2,5,2,5]{4,3,2,1,0:T(2,128)} %bitcast.31, bf16[64,16,128]{2,1,0:T(8,128)(2,1)} %constant.52.clone.table_ref, bf16[2,2,2,320,344]{4,3,2,1,0:T(8,128)(2,1)} %bitcast.21, bf16[2,2,2,16,344]{4,3,2,1,0:T(8,128)(2,1)} %copy-done.5, ...), custom_call_target="tpu_custom_call" | custom-call | flops 419430400 | bytes 1761280 | tf_op jit(solution)/shard_map/pallas_call | solution.py:173
  37.6 0.0 copy-done.2
  37.6 0.0 copy-done.3
  37.6 0.0 copy-done.4
  37.6 0.0 copy-start
  37.6 1.1 %copy-done = bf16[2,1600,128]{2,1,0:T(8,128)(2,1)S(1)} copy-done((bf16[2,1600,128]{2,1,0:T(8,128)(2,1)S(1)}, bf16[2,1600,128]{2,1,0:T(8,128)(2,1)}, u32[]{:S(2)}) %copy-start) | copy-done | bytes 819224
  38.7 0.0 copy-start.1
  38.7 1.6 %shard_map.89.rest_0_ = f32[64,128]{1,0:T(8,128)S(1)} custom-call(bf16[64,640]{1,0:T(8,128)(2,1)S(1)} %copy-done.3, bf16[64,640]{1,0:T(8,128)(2,1)S(1)} %copy-done.4, bf16[2,1600,128]{2,1,0:T(8,128)(2,1)S(1)} %copy-done.2, bf16[2,1600,128]{2,1,0:T(8,128)(2,1)S(1)} %copy-done), custom_call_target="tpu_custom_call" | custom-call | flops 100000000 | bytes 1761280 | tf_op jit(solution)/shard_map/pallas_call | solution.py:348
  40.3 0.0 collective-permute-done.3
  40.4 0.1 broadcast_select_fusion.3
  40.4 1.6 %collective-permute-start.4 = (bf16[2,224,128]{2,1,0:T(8,128)(2,1)S(1)}, bf16[2,224,128]{2,1,0:T(8,128)(2,1)S(1)}, u32[]{:S(2)}, u32[]{:S(2)}) collective-permute-start(bf16[2,224,128]{2,1,0:T(8,128)(2,1)S(1)} %broadcast_select_fusion.3), channel_id=1, source_target_pairs={{0,32},{8,40},{16,48},{24,56},{32,0},{40,8},{48,16},{56,24},{64,96... | collective-permute-start | bytes 344072 | tf_op jit(solution)/shard_map/ppermute | solution.py:369
  42.0 3.5 %collective-permute-done.4 = bf16[2,224,128]{2,1,0:T(8,128)(2,1)S(1)} collective-permute-done((bf16[2,224,128]{2,1,0:T(8,128)(2,1)S(1)}, bf16[2,224,128]{2,1,0:T(8,128)(2,1)S(1)}, u32[]{:S(2)}, u32[]{:S(2)}) %collective-permute-start.4) | collective-permute-done | bytes 114720 | tf_op jit(solution)/shard_map/ppermute | solution.py:369
  45.5 0.0 collective-permute-done.5.b_ref
  45.6 0.0 copy-done.1
  45.6 2.3 %shard_map.90 = f32[64,128]{1,0:T(8,128)} custom-call(bf16[64,640]{1,0:T(8,128)(2,1)S(1)} %copy-done.3, bf16[64,640]{1,0:T(8,128)(2,1)S(1)} %copy-done.4, bf16[2,1600,128]{2,1,0:T(8,128)(2,1)S(1)} %copy-done.1, bf16[2,1600,128]{2,1,0:T(8,128)(2,1)S(1)} %collective-permute-done.5.b_ref, f32[64,128]{1,0:T(8,128)S(1)} %shard_map.89.rest_0_), custom_call_target="tpu_custom_call" | custom-call | flops 100000000 | bytes 1761280 | tf_op jit(solution)/shard_map/pallas_call | solution.py:348
  47.9 1.8 %collective-permute-start.6 = (bf16[2,448,128]{2,1,0:T(8,128)(2,1)S(1)}, bf16[2,448,128]{2,1,0:T(8,128)(2,1)S(1)}, u32[]{:S(2)}, u32[]{:S(2)}) collective-permute-start(bf16[2,448,128]{2,1,0:T(8,128)(2,1)S(1)} %pad_maximum_fusion.1), channel_id=1, source_target_pairs={{0,16},{8,24},{16,0},{24,8},{32,48},{40,56},{48,32},{56,40},{64,80... | collective-permute-start | bytes 688136 | tf_op jit(solution)/shard_map/ppermute | solution.py:369
  49.7 15.1 %all-to-all-start.1 = ((f32[32,2,128]{2,1,0:T(2,128)}), f32[32,2,128]{2,1,0:T(2,128)S(1)}, u32[]{:S(2)}, u32[]{:S(2)}) async-start(f32[32,2,128]{2,1,0:T(2,128)} %bitcast.5), calls=%async_computation.1 | async-start | bytes 65536 | tf_op jit(solution)/shard_map/all_to_all | solution.py:386
  64.8 0.0 collective-permute-done.6
  64.9 8.0 %all-to-all-done.1 = f32[32,2,128]{2,1,0:T(2,128)S(1)} async-done(((f32[32,2,128]{2,1,0:T(2,128)}), f32[32,2,128]{2,1,0:T(2,128)S(1)}, u32[]{:S(2)}, u32[]{:S(2)}) %all-to-all-start.1) | async-done | bytes 32800 | tf_op jit(solution)/shard_map/all_to_all | solution.py:386
  72.9 0.4 collective-permute-start.7
  73.3 0.1 copy.24
  73.4 0.2 copy.25
  73.6 0.8 copy.27
  74.3 0.8 %shard_map.91 = f32[64,128]{1,0:T(8,128)S(1)} custom-call(s32[1]{0:T(128)} %bitcast.me_ref, bf16[2,896,128]{2,1,0:T(8,128)(2,1)S(1)} %pad_maximum_fusion.ref_ref, bf16[2,1600,128]{2,1,0:T(8,128)(2,1)S(1)} %copy-done.2, bf16[2,1600,128]{2,1,0:T(8,128)(2,1)S(1)} %copy-done.1), custom_call_target="tpu_custom_call" | custom-call | flops 10000000 | bytes 660480 | tf_op jit(solution)/shard_map/pallas_call | solution.py:360
  75.1 0.0 collective-permute-done.7.ref_ref
  75.1 0.8 %shard_map.92 = f32[64,128]{1,0:T(8,128)S(1)} custom-call(s32[1]{0:T(128)} %bitcast.me_ref, bf16[2,896,128]{2,1,0:T(8,128)(2,1)S(1)} %collective-permute-done.7.ref_ref, bf16[2,1600,128]{2,1,0:T(8,128)(2,1)S(1)} %copy-done.2, bf16[2,1600,128]{2,1,0:T(8,128)(2,1)S(1)} %copy-done.1), custom_call_target="tpu_custom_call" | custom-call | flops 10000000 | bytes 660480 | tf_op jit(solution)/shard_map/pallas_call | solution.py:360
  75.9 0.1 copy.28
  76.0 0.1 copy.29
  76.1 0.1 pad_maximum_fusion.2
  76.2 0.1 reshape.57
  76.3 0.6 copy.26
  (8 shorter events, 0.2 us)
Async XLA Ops:
  0.6 16.4 %copy-start.7 = (s32[2]{0:T(128)S(1)}, s32[2]{0:T(128)}, u32[]{:S(2)}) copy-start(s32[2]{0:T(128)} %dates_ref) | copy-start | bytes 28
  4.4 12.7 %all-to-all-start = ((bf16[8,224,128]{2,1,0:T(8,128)(2,1)}), bf16[8,224,128]{2,1,0:T(8,128)(2,1)S(1)}, u32[]{:S(2)}, u32[]{:S(2)}) async-start(bf16[8,224,128]{2,1,0:T(8,128)(2,1)} %bitcast.22), calls=%async_computation | async-start | bytes 917504 | tf_op jit(solution)/shard_map/all_to_all | solution.py:333
  9.3 14.2 %collective-permute-start.1 = (bf16[2,2,2,16,344]{4,3,2,1,0:T(8,128)(2,1)S(1)}, bf16[2,2,2,16,344]{4,3,2,1,0:T(8,128)(2,1)S(1)}, u32[]{:S(2)}, u32[]{:S(2)}) collective-permute-start(bf16[2,2,2,16,344]{4,3,2,1,0:T(8,128)(2,1)S(1)} %get-tuple-element.27), channel_id=1, source_target_pairs={{0,1},{1,2},{2,3},{3,4},{4,5},{5,6},{6,7},{8,9},{9,10},{10,11},{11... | collective-permute-start | bytes 264200 | tf_op jit(solution)/shard_map/ppermute | solution.py:310
  13.8 9.7 %collective-permute-start.2 = (bf16[2,2,2,16,344]{4,3,2,1,0:T(8,128)(2,1)S(1)}, bf16[2,2,2,16,344]{4,3,2,1,0:T(8,128)(2,1)S(1)}, u32[]{:S(2)}, u32[]{:S(2)}) collective-permute-start(bf16[2,2,2,16,344]{4,3,2,1,0:T(8,128)(2,1)S(1)} %get-tuple-element.26), channel_id=1, source_target_pairs={{1,0},{2,1},{3,2},{4,3},{5,4},{6,5},{7,6},{9,8},{10,9},{11,10},{12... | collective-permute-start | bytes 264200 | tf_op jit(solution)/shard_map/ppermute | solution.py:311
  17.4 14.4 %collective-permute-start = (bf16[2,224,128]{2,1,0:T(8,128)(2,1)S(1)}, bf16[2,224,128]{2,1,0:T(8,128)(2,1)S(1)}, u32[]{:S(2)}, u32[]{:S(2)}) collective-permute-start(bf16[2,224,128]{2,1,0:T(8,128)(2,1)S(1)} %select_reduce_fusion), channel_id=1, source_target_pairs={{0,128},{8,136},{16,144},{24,152},{32,160},{40,168},{48,176},{56,1... | collective-permute-start | bytes 344072 | tf_op jit(solution)/shard_map/ppermute | solution.py:374
  23.5 0.6 copy-start.5
  23.6 0.7 copy-start.6
  28.6 9.0 %copy-start.2 = (bf16[2,1600,128]{2,1,0:T(8,128)(2,1)S(1)}, bf16[2,1600,128]{2,1,0:T(8,128)(2,1)}, u32[]{:S(2)}) copy-start(bf16[2,1600,128]{2,1,0:T(8,128)(2,1)} %shard_map.87.a_ref.s0_ref) | copy-start | bytes 2457604
  28.6 9.0 %copy-start.3 = (bf16[64,640]{1,0:T(8,128)(2,1)S(1)}, bf16[64,640]{1,0:T(8,128)(2,1)}, u32[]{:S(2)}) copy-start(bf16[64,640]{1,0:T(8,128)(2,1)} %constant.53.clone.plain_ref) | copy-start | bytes 245764
  28.6 9.0 %copy-start.4 = (bf16[64,640]{1,0:T(8,128)(2,1)S(1)}, bf16[64,640]{1,0:T(8,128)(2,1)}, u32[]{:S(2)}) copy-start(bf16[64,640]{1,0:T(8,128)(2,1)} %constant.54.clone.signed_ref) | copy-start | bytes 245764
  28.6 16.9 %collective-permute-start.5 = (bf16[2,1600,128]{2,1,0:T(8,128)(2,1)}, bf16[2,1600,128]{2,1,0:T(8,128)(2,1)S(1)}, u32[]{:S(2)}, u32[]{:S(2)}) collective-permute-start(bf16[2,1600,128]{2,1,0:T(8,128)(2,1)} %shard_map.87.a_ref.s0_ref), channel_id=1, source_target_pairs={{8,0},{16,8},{24,16},{32,24},{40,32},{48,40},{56,48},{64,56},{72,6... | collective-permute-start | bytes 2457608 | tf_op jit(solution)/shard_map/ppermute | solution.py:380
  31.9 8.5 %collective-permute-start.3 = (bf16[2,224,128]{2,1,0:T(8,128)(2,1)S(1)}, bf16[2,224,128]{2,1,0:T(8,128)(2,1)S(1)}, u32[]{:S(2)}, u32[]{:S(2)}) collective-permute-start(bf16[2,224,128]{2,1,0:T(8,128)(2,1)S(1)} %broadcast_select_fusion.2), channel_id=1, source_target_pairs={{0,64},{8,72},{16,80},{24,88},{32,96},{40,104},{48,112},{56,120},{... | collective-permute-start | bytes 344072 | tf_op jit(solution)/shard_map/ppermute | solution.py:374
  37.6 1.1 %copy-start = (bf16[2,1600,128]{2,1,0:T(8,128)(2,1)S(1)}, bf16[2,1600,128]{2,1,0:T(8,128)(2,1)}, u32[]{:S(2)}) copy-start(bf16[2,1600,128]{2,1,0:T(8,128)(2,1)} %shard_map.88.b_ref.a_ref.s1_ref) | copy-start | bytes 2457604
  38.7 6.8 %copy-start.1 = (bf16[2,1600,128]{2,1,0:T(8,128)(2,1)S(1)}, bf16[2,1600,128]{2,1,0:T(8,128)(2,1)}, u32[]{:S(2)}) copy-start(bf16[2,1600,128]{2,1,0:T(8,128)(2,1)} %shard_map.88.b_ref.a_ref.s1_ref) | copy-start | bytes 2457604
  40.4 5.1 %collective-permute-start.4 = (bf16[2,224,128]{2,1,0:T(8,128)(2,1)S(1)}, bf16[2,224,128]{2,1,0:T(8,128)(2,1)S(1)}, u32[]{:S(2)}, u32[]{:S(2)}) collective-permute-start(bf16[2,224,128]{2,1,0:T(8,128)(2,1)S(1)} %broadcast_select_fusion.3), channel_id=1, source_target_pairs={{0,32},{8,40},{16,48},{24,56},{32,0},{40,8},{48,16},{56,24},{64,96... | collective-permute-start | bytes 344072 | tf_op jit(solution)/shard_map/ppermute | solution.py:369
  47.9 16.9 %collective-permute-start.6 = (bf16[2,448,128]{2,1,0:T(8,128)(2,1)S(1)}, bf16[2,448,128]{2,1,0:T(8,128)(2,1)S(1)}, u32[]{:S(2)}, u32[]{:S(2)}) collective-permute-start(bf16[2,448,128]{2,1,0:T(8,128)(2,1)S(1)} %pad_maximum_fusion.1), channel_id=1, source_target_pairs={{0,16},{8,24},{16,0},{24,8},{32,48},{40,56},{48,32},{56,40},{64,80... | collective-permute-start | bytes 688136 | tf_op jit(solution)/shard_map/ppermute | solution.py:369
  49.7 23.2 %all-to-all-start.1 = ((f32[32,2,128]{2,1,0:T(2,128)}), f32[32,2,128]{2,1,0:T(2,128)S(1)}, u32[]{:S(2)}, u32[]{:S(2)}) async-start(f32[32,2,128]{2,1,0:T(2,128)} %bitcast.5), calls=%async_computation.1 | async-start | bytes 65536 | tf_op jit(solution)/shard_map/all_to_all | solution.py:386
  72.9 2.2 %collective-permute-start.7 = (bf16[2,896,128]{2,1,0:T(8,128)(2,1)S(1)}, bf16[2,896,128]{2,1,0:T(8,128)(2,1)S(1)}, u32[]{:S(2)}, u32[]{:S(2)}) collective-permute-start(bf16[2,896,128]{2,1,0:T(8,128)(2,1)S(1)} %pad_maximum_fusion.ref_ref), channel_id=1, source_target_pairs={{0,8},{8,0},{16,24},{24,16},{32,40},{40,32},{48,56},{56,48},{64,72... | collective-permute-start | bytes 1376264 | tf_op jit(solution)/shard_map/ppermute | solution.py:389

commit v3 on v2

--- a/solution.py
+++ b/solution.py
@@ -11,6 +11,7 @@
 CHIP = 64
 TAPS = 8
 SUBSTEPS = 64
+MAX_SHIFT = 8
 LOOK_AZ = 5
 LOOK_RG = 20
 MARGIN = 12
@@ -60,7 +61,7 @@
         out_specs=VMEM,
         scratch_shapes=list(scratch),
         cost_estimate=pl.CostEstimate(flops=cost[0], bytes_accessed=cost[1], transcendentals=0),
-        compiler_params=pltpu.CompilerParams(vmem_limit_bytes=48 << 20),
+        compiler_params=pltpu.CompilerParams(vmem_limit_bytes=24 << 20),
     )
 
 
@@ -73,12 +74,10 @@
     return result
 
 
-def lane_tiles(image_ref, stage, index):
-    lines = image_ref.shape[-1]
+def lane_tiles(read, lines, stage):
     whole = lines // LANES
-    tiles = [image_ref[index + (slice(None), slice(k * LANES, (k + 1) * LANES))] for k in range(whole)]
-    stage[:, 0 : lines - whole * LANES] = image_ref[index + (slice(None), slice(whole * LANES, lines))]
-    return tiles + [stage[...]]
+    stage[:, 0 : lines - whole * LANES] = read(slice(whole * LANES, lines))
+    return [read(slice(k * LANES, (k + 1) * LANES)) for k in range(whole)] + [stage[...]]
 
 
 def candidate_body(group, dates_ref, me_ref, x_ref, out_ref, stage):
@@ -90,7 +89,7 @@
     def place(step):
         return (reversed_bits(step // steps, group) * steps + step % steps) * PACK
 
-    parts = [lane_tiles(x_ref, stage.at[p], (0, 0, p)) for p in range(2)]
+    parts = [lane_tiles(lambda part, p=p: x_ref[0, 0, p, :, part], lines, stage.at[p]) for p in range(2)]
     for a in range(chips_az):
         start = MARGIN + a * CHIP
         tile, offset = start // LANES, start % LANES
@@ -110,18 +109,20 @@
         out_ref[at : at + PACK, :] = jnp.zeros((PACK, LANES), BF16)
 
 
-def resample_body(date, shift_ref, frac_ref, table_ref, x_ref, left_ref, right_ref, out_ref, stage, window):
-    t = pl.program_id(0)
+def resample_body(crossed, me_ref, move_ref, table_ref, x_ref, left_ref, right_ref, *rest):
+    out_refs = rest[: 2 if crossed else 4]
+    stage, window, chips_ref = rest[len(out_refs) :]
+    date = pl.program_id(0)
+    t = 1 - date if crossed else date
     cols, lines = x_ref.shape[-2:]
     chips_az = (lines - 2 * MARGIN) // CHIP
     chips_rg = cols // CHIP
     depth = CHIP + 2 * EDGE
 
-    def fill(source_ref, scratch, at):
-        count = source_ref.shape[-2]
+    def fill(read, count, scratch, at):
         lane = lane_index((count, LANES))
         for p in range(2):
-            tiles = lane_tiles(source_ref, scratch.at[p], (0, 0, p))
+            tiles = lane_tiles(functools.partial(read, p), lines, scratch.at[p])
             turned = [pltpu.roll(tile, CHIP, 1) for tile in tiles]
             for a in range(chips_az):
                 tile = tiles[a // 2]
@@ -129,83 +130,116 @@
                     tile = jnp.where(lane < CHIP, turned[a // 2], turned[a // 2 + 1])
                 window[a, p, at : at + count, :] = tile
 
+    def left(p, part):
+        return left_ref[0, 0, p, :, part]
+
+    def right(p, part):
+        return right_ref[0, 0, p, :, part]
+
     for p in range(2):
         stage[p, :, :] = jnp.zeros(stage.shape[1:], BF16)
-    fill(left_ref, stage.at[:, 0:EDGE], 0)
-    fill(x_ref, stage, EDGE)
-    fill(right_ref, stage.at[:, 0:EDGE], EDGE + cols)
+    fill(left, EDGE, stage.at[:, 0:EDGE], 0)
+    fill(lambda p, part: x_ref[0, 0, p, :, part], cols, stage, EDGE)
+    fill(right, EDGE, stage.at[:, 0:EDGE], EDGE + cols)
     half = lane_index((depth, LANES)) < CHIP
 
-    def skewed(fraction, offset):
-        base = table_ref[fraction]
+    def skewed(move, offset):
+        offset = offset - MAX_SHIFT + lax.div(move, SUBSTEPS)
+        base = table_ref[lax.rem(move, SUBSTEPS)]
         return jnp.concatenate([pltpu.roll(base, offset + k, 1) for k in range(0, CHIP, SKEW)], axis=0)
 
     for r in range(chips_rg):
         start = r * CHIP
         firsts = []
         for a in range(chips_az):
-            azimuth = skewed(frac_ref[0, date, a, t, r], shift_ref[0, date, a, t, r] + 9)
+            azimuth = skewed(move_ref[0, date, a, t, r], 9)
             both = jnp.concatenate([azimuth, azimuth], axis=0)
             data = jnp.concatenate([window[a, p, start : start + depth, :] for p in range(2)], axis=0)
             partial = lax.dot_general(data, both, (((1,), (1,)), ((), ())), preferred_element_type=F32)
             firsts.append(jnp.where(half, partial[:depth], partial[depth:]).astype(BF16))
         if r:
             for a in range(chips_az):
-                across = skewed(frac_ref[1, date, a, t, r - 1], shift_ref[1, date, a, t, r - 1] + 13)
+                across = skewed(move_ref[1, date, a, t, r - 1], 13)
                 chip = jnp.dot(across[:, :depth], before[a], preferred_element_type=F32)
-                out_ref[0, a * cols + start - CHIP : a * cols + start, :] = chip.astype(BF16)
+                chips_ref[a * cols + start - CHIP : a * cols + start, :] = chip.astype(BF16)
         before = firsts
     for a in range(chips_az):
-        across = skewed(frac_ref[1, date, a, t, r], shift_ref[1, date, a, t, r] + 13)
+        across = skewed(move_ref[1, date, a, t, r], 13)
         chip = jnp.dot(across[:, :depth], before[a], preferred_element_type=F32)
-        out_ref[0, a * cols + start : a * cols + start + CHIP, :] = chip.astype(BF16)
-
-
-def resample_call(d, shifts, fractions, table, images, left, right):
+        chips_ref[a * cols + start : a * cols + start + CHIP, :] = chip.astype(BF16)
+
+    for d in range(2):
+
+        @pl.when(date == d)
+        def _(d=d):
+            out_refs[d][...] = chips_ref[...]
+
+    if not crossed:
+        parity = lax.rem(me_ref[0], 2)
+        for side in range(2):
+
+            @pl.when((date + parity + side) % 2 == 1)
+            def _(side=side):
+                out_refs[2 + side][...] = chips_ref[...]
+
+
+def resample_call(crossed, me, moves, table, images, edges):
     dates, tiles, parts, cols, rows = images.shape
     chips_az = (rows - 2 * MARGIN) // CHIP
     lines = chips_az * cols
 
-    def of_tile(t):
-        return (d, t, 0, 0, 0)
+    count = 2 if crossed else 4
+
+    def of_tile(date):
+        return (date, 1 - date if crossed else date, 0, 0, 0)
 
     edge = pl.BlockSpec((1, 1, parts, EDGE, rows), of_tile)
     return pl.pallas_call(
-        functools.partial(resample_body, d),
-        out_shape=jax.ShapeDtypeStruct((tiles, lines, LANES), BF16),
-        grid=(tiles,),
+        functools.partial(resample_body, crossed),
+        out_shape=[jax.ShapeDtypeStruct((lines, LANES), BF16)] * count,
+        grid=(dates,),
         in_specs=[
             SMEM,
             SMEM,
-            pl.BlockSpec(table.shape, lambda t: (0, 0, 0)),
+            pl.BlockSpec(table.shape, lambda date: (0, 0, 0)),
             pl.BlockSpec((1, 1, parts, cols, rows), of_tile),
             edge,
             edge,
         ],
-        out_specs=pl.BlockSpec((1, lines, LANES), lambda t: (t, 0, 0)),
+        out_specs=[pl.BlockSpec((lines, LANES), lambda date: (0, 0))] * count,
         scratch_shapes=[
             pltpu.VMEM((parts, cols, LANES), BF16),
             pltpu.VMEM((chips_az, parts, cols + 2 * EDGE, LANES), BF16),
+            pltpu.VMEM((lines, LANES), BF16),
         ],
         cost_estimate=pl.CostEstimate(
             flops=tiles * lines * 128 * 256 * 4, bytes_accessed=16 * rows * cols, transcendentals=0
         ),
-        compiler_params=pltpu.CompilerParams(vmem_limit_bytes=60 << 20),
-    )(shifts, fractions, table, images, left, right)
-
-
-def pair_body(pair, plain_ref, signed_ref, a_ref, b_ref, *rest):
+        compiler_params=pltpu.CompilerParams(vmem_limit_bytes=16 << 20),
+    )(me, moves, table, images, *edges)
+
+
+def pair_body(pair, plain_ref, signed_ref, *rest):
     if pair == 1:
-        before_ref, out_ref, product, looked = rest
+        me_ref, first_0, got1, got2, second_1, before_ref, out_ref, product, looked = rest
+        even = lax.rem(me_ref[0], 2) == 0
+        sources = [
+            (lambda rows: first_0[rows, :], lambda rows: jnp.where(even, got1[rows, :], got2[rows, :])),
+            (lambda rows: jnp.where(even, got2[rows, :], got1[rows, :]), lambda rows: second_1[rows, :]),
+        ]
     else:
-        out_ref, product, looked = rest
+        first_0, second_0, first_1, second_1, out_ref, product, looked = rest
+        sources = [
+            (lambda rows: first_0[rows, :], lambda rows: second_0[rows, :]),
+            (lambda rows: first_1[rows, :], lambda rows: second_1[rows, :]),
+        ]
     chips_az = plain_ref.shape[1] // LANES
-    cols = a_ref.shape[1] // chips_az
+    cols = first_0.shape[0] // chips_az
     looks = cols // LOOK_RG
-    for t in range(2):
+    for t, (read_first, read_second) in enumerate(sources):
         for a in range(chips_az):
-            first = a_ref[t, a * cols : (a + 1) * cols, :].astype(F32)
-            second = b_ref[t, a * cols : (a + 1) * cols, :].astype(F32)
+            first = read_first(slice(a * cols, (a + 1) * cols)).astype(F32)
+            second = read_second(slice(a * cols, (a + 1) * cols)).astype(F32)
             work = product.at[a % 2]
             work[0] = first * second
             work[1] = pltpu.roll(first, CHIP, 1) * second
@@ -242,9 +276,35 @@
     out_ref[...] = value
 
 
-def correlate_body(other, me_ref, ref_ref, s0_ref, s1_ref, out_ref, sums):
+def pair_places(group, blocks):
+    places = np.zeros((group, blocks, blocks, 3, LANES), np.float32)
+    for device in range(group):
+        for block in range(blocks):
+            for kind, p in enumerate((2 * device, 2 * device + 1, 2 * device - 1)):
+                if 0 <= p < 2 * group - 1:
+                    places[device, block, block, kind, p] = 1.0
+    return places.reshape(group * blocks, blocks * 3 * LANES)
+
+
+def assemble_body(places_ref, looked_ref, out_ref):
+    pairs = out_ref.shape[-1]
+    looks = out_ref.shape[-2]
+    rows = jnp.transpose(looked_ref[...])
+    spread = jnp.dot(rows, places_ref[...], precision=lax.Precision.HIGHEST, preferred_element_type=F32)
+    for q in range(2):
+        for t in range(2):
+            low = (q * 2 + t) * looks
+            for b in range(out_ref.shape[2]):
+                at = b * 3 * LANES
+                inner = spread[low : low + looks, at : at + LANES]
+                at += (1 + t) * LANES
+                outer = spread[CHIP + low : CHIP + low + looks, at : at + LANES]
+                out_ref[q, t, b] = (inner + outer)[:, :pairs]
+
+
+def correlate_body(other, me_ref, ref_ref, s00_ref, s01_ref, s10_ref, s11_ref, out_ref, sums):
     half_chips = ref_ref.shape[1] // CHIP
-    chips = s0_ref.shape[1] // CHIP
+    chips = s00_ref.shape[0] // CHIP
     half = lax.rem(me_ref[0], 2)
     base = (1 - half if other else half) * half_chips
     lane = lane_index((8, LANES))
@@ -265,8 +325,9 @@
             ref = ref_ref[t, k * CHIP : (k + 1) * CHIP, :].astype(F32)
             turned = pltpu.roll(ref, CHIP, 1)
             power = total(ref * ref)
-            for d, s_ref in enumerate((s0_ref, s1_ref)):
-                sec = s_ref[t, pl.ds(source, CHIP), :].astype(F32)
+            for d in range(2):
+                s_ref = ((s00_ref, s01_ref), (s10_ref, s11_ref))[d][t]
+                sec = s_ref[pl.ds(source, CHIP), :].astype(F32)
                 at = (d * 2 + t) * 16 + k
                 sums[0, at : at + 1, :] = total(ref * sec)
                 sums[1, at : at + 1, :] = jnp.sum(fold(turned * sec) * sign, axis=0, keepdims=True)
@@ -286,6 +347,7 @@
     group = lax.axis_size("date")
     strips = lax.axis_size("strip")
     me = lax.axis_index("date")
+    strip = lax.axis_index("strip")
     me_one = me.reshape(1).astype(jnp.int32)
     chips_az = (rows - 2 * MARGIN) // CHIP
     chips_rg = cols // CHIP
@@ -298,8 +360,7 @@
     shape = jax.ShapeDtypeStruct
     image_bytes = rows * cols * 2
     images = acquisitions.transpose(0, 1, 2, 4, 3)
-    shifts = shifts.transpose(0, 1, 3, 2, 4)
-    fractions = fractions.transpose(0, 1, 3, 2, 4)
+    moves = ((shifts + MAX_SHIFT) * SUBSTEPS + fractions).transpose(0, 1, 3, 2, 4)
     owners = ref_dates // dates
 
     table = jnp.asarray(tap_table())
@@ -307,8 +368,12 @@
 
     high_edge = images[:, :, :, cols - EDGE :]
     low_edge = images[:, :, :, :EDGE]
-    left = lax.ppermute(high_edge, "strip", [(i, i + 1) for i in range(strips - 1)])
-    right = lax.ppermute(low_edge, "strip", [(i + 1, i) for i in range(strips - 1)])
+    even = strip % 2 == 0
+    pairs1 = [(i, i ^ 1) for i in range(strips)]
+    pairs2 = [(i, (i + 1 ^ 1) - 1) for i in range(1, strips - 1)]
+    to_one, to_other = jnp.where(even, high_edge, low_edge), jnp.where(even, low_edge, high_edge)
+    from_one = lax.ppermute(to_one, "strip", pairs1)
+    from_other = lax.ppermute(to_other, "strip", pairs2)
 
     def after(value, *events):
         return lax.optimization_barrier((value, events))[0]
@@ -329,7 +394,7 @@
         ),
         cost_estimate=pl.CostEstimate(flops=10**6, bytes_accessed=4 * image_bytes, transcendentals=0),
         compiler_params=pltpu.CompilerParams(vmem_limit_bytes=60 << 20),
-    )(after(ref_dates, high_edge, low_edge), me_one, images)
+    )(after(ref_dates, to_one, to_other), me_one, images)
     scattered = lax.all_to_all(
         candidate.reshape(near, piece, LANES),
         "date",
@@ -340,15 +405,15 @@
     )
     from_owner = jnp.arange(near)[None, :] == (owners % near)[:, None]
     reference = jnp.sum(jnp.where(from_owner[:, :, None, None], scattered[None], 0), axis=1, dtype=BF16)
-    left, right = after((left, right), reference)
-
-    resample = functools.partial(resample_call, shifts=shifts, fractions=fractions, table=table, images=images, left=left, right=right)
+    edges = (jnp.where(even, from_other, from_one), jnp.where(even, from_one, from_other))
+
+    resample = functools.partial(resample_call, me=me_one, moves=moves, table=table, images=images, edges=edges)
 
     def pair(index, *values):
         return call(
             functools.partial(pair_body, index),
             shape((blocks, LANES), F32),
-            [VMEM] * (2 + len(values)),
+            [VMEM] * 2 + [SMEM] * index + [VMEM] * (len(values) - index),
             [
                 pltpu.VMEM((2, 4, cols, LANES), F32),
                 pltpu.VMEM((4 * tiles * looks, chips_az * LANES), F32),
@@ -360,10 +425,10 @@
         return call(
             functools.partial(correlate_body, other),
             shape((4 * 16, LANES), F32),
-            [SMEM, VMEM, VMEM, VMEM],
+            [SMEM] + [VMEM] * 5,
             [pltpu.VMEM((4, 4 * 16, LANES), F32)],
             cost=(10**7, 3 * image_bytes),
-        )(me_one, value.reshape(tiles, -1, LANES), first, second)
+        )(me_one, value.reshape(tiles, -1, LANES), s00, s01, s10, s11)
 
     def exchange(value, step):
         other = lax.ppermute(value, "date", [(i, i ^ step) for i in range(group)])
@@ -376,21 +441,27 @@
         return jnp.where(same[:, None, None], value, other)
 
     reference = flood(reference, 16)
-    first = resample(0)
-    following = lax.ppermute(first, "date", [(i + 1, i) for i in range(group - 1)])
-    reference = flood(after(reference, first), 8)
-    second = resample(1)
-    looked = pair(0, first, second)
+    s00, s11, send1, send2 = resample(False)
+    got1 = lax.ppermute(send1, "date", [(i, i ^ 1) for i in range(group)])
+    got2 = lax.ppermute(send2, "date", [(i, (i + 1 ^ 1) - 1) for i in range(1, group - 1)])
+    s01, s10 = resample(True)
+    looked = pair(0, s00, s10, s01, s11)
+    reference = flood(after(reference, looked), 8)
+    looked = pair(1, me_one, s10, got1, got2, s01, looked)
     reference = exchange(after(reference, looked), 4)
-    looked = pair(1, second, following, looked)
     relayed = lax.all_to_all(looked.reshape(group, -1, LANES), "date", 0, 0, tiled=True)
-    reference = exchange(after(reference, looked), 2)
+    reference = exchange(reference, 2)
     reference, relayed = lax.optimization_barrier((reference, relayed))
     other = lax.ppermute(reference, "date", [(i, i ^ 1) for i in range(group)])
 
-    relayed = relayed.reshape(group, blocks // group, 2, 2, tiles, looks)
-    coherence = relayed.transpose(3, 0, 2, 4, 1, 5).reshape(2, 2 * group, tiles, blocks // group, looks)
-    coherence = coherence[:, : 2 * group - 1]
+    share = blocks // group
+    coherence = call(
+        assemble_body,
+        shape((2, tiles, share, looks, 2 * group - 1), F32),
+        [VMEM, VMEM],
+        cost=(10**7, 10**6),
+    )(jnp.asarray(pair_places(group, share)), relayed.reshape(blocks, LANES))
+    coherence = coherence.transpose(0, 4, 1, 2, 3)
 
     here = correlate(False, reference)
     there = correlate(True, other)

time: 77.4 us -> 72.5 us (0.937)
  the two profiles are of different devices: /device:TPU:7 before, /device:TPU:19 now
where the time goes in v3:
time: 72.5 us; the launch traced here: 71.9 us
  starting transfers between devices  31.8 us (44%)
  Pallas kernels  17.7 us (24%)
  waiting for transfers between devices  13.6 us (19%)
  local copies, waits for them, and re-layouts  5.63 us (8%)
  other arithmetic  2.35 us (3%)
  between operations  0.95 us (1%)
    all_to_all x1, waiting for transfers between devices, per_device(): lax.all_to_all(looked.reshape(group, -1, LANES), 'date', 0, 0, tiled=True)  7.96 us
    ppermute x2, starting transfers between devices, flood(): other = lax.ppermute(value, 'date', [(i, i ^ step) for i in range(group)])  7.74 us
    pallas_call x2, Pallas kernels, resample_call(): pl.pallas_call(functools.partial(resample_body, crossed), out_shape=[jax....  7.09 us
    ppermute x1, starting transfers between devices, per_device(): from_other = lax.ppermute(to_other, 'strip', pairs2)  5.74 us
    unnamed x39, local copies, waits for them, and re-layouts  5.55 us
    all_to_all x1, starting transfers between devices, per_device(): lax.all_to_all(looked.reshape(group, -1, LANES), 'date', 0, 0, tiled=True)  5.36 us
    all_to_all x1, starting transfers between devices, per_device(): lax.all_to_all(candidate.reshape(near, piece, LANES), 'date', 0, 0, axis_...  5.14 us
    pallas_call x2, Pallas kernels, pair(): call(functools.partial(pair_body, index), shape((blocks, LANES), F32), [V...  5.05 us
  transfers between devices with their start and end apart: 11, of which 3 were waited for; matrix products, arithmetic and copies ran while one was open for 2% of the time, Pallas kernels for 23%

profile of v3, /device:TPU:19, one launch (start us, length us, event | category | flops | bytes accessed | tf_op | source)
XLA Modules:
  0.0 71.9 jit_solution(8057383634729566872)
XLA Ops:
  0.6 0.0 copy-start.14
  0.6 0.0 copy-start.12
  0.7 0.0 copy-start.13
  0.7 1.0 %broadcast_select_fusion.8 = (bf16[2,2,2,16,344]{4,3,2,1,0:T(8,128)(2,1)S(1)}, bf16[2,2,2,16,344]{4,3,2,1,0:T(8,128)(2,1)S(1)}) fusion(pred[]{:T(512)S(6)} %eq.40, bf16[2,2,2,320,344]{4,3,2,1,0:T(8,128)(2,1)} %bitcast.15), kind=kLoop, calls=%fused_computation.11 | loop fusion | flops 88064 | bytes 352257 | tf_op jit(solution)/shard_map/jit(_where)/select_n | solution.py:374
  1.6 0.0 copy-start
  1.7 0.0 copy-start.4
  1.7 0.1 collective-permute-start.2
  1.8 5.7 %collective-permute-start.1 = (bf16[2,2,2,16,344]{4,3,2,1,0:T(8,128)(2,1)S(1)}, bf16[2,2,2,16,344]{4,3,2,1,0:T(8,128)(2,1)S(1)}, u32[]{:S(2)}, u32[]{:S(2)}) collective-permute-start(bf16[2,2,2,16,344]{4,3,2,1,0:T(8,128)(2,1)S(1)} %get-tuple-element.30), channel_id=1, source_target_pairs={{1,2},{2,1},{3,4},{4,3},{5,6},{6,5},{9,10},{10,9},{11,12},{12,11},... | collective-permute-start | bytes 264200 | tf_op jit(solution)/shard_map/ppermute | solution.py:376
  7.6 2.8 %shard_map.95 = bf16[1792,128]{1,0:T(8,128)(2,1)} custom-call(s32[2]{0:T(128)} %dates_ref, s32[1]{0:T(128)} %bitcast.me_ref.rest_0_, bf16[2,2,2,320,344]{4,3,2,1,0:T(8,128)(2,1)} %bitcast.16), custom_call_target="tpu_custom_call" | custom-call | flops 1000000 | bytes 880640 | tf_op jit(solution)/shard_map/pallas_call | solution.py:385
  10.4 5.1 %all-to-all-start = ((bf16[8,224,128]{2,1,0:T(8,128)(2,1)}), bf16[8,224,128]{2,1,0:T(8,128)(2,1)S(1)}, u32[]{:S(2)}, u32[]{:S(2)}) async-start(bf16[8,224,128]{2,1,0:T(8,128)(2,1)} %bitcast.20), calls=%async_computation | async-start | bytes 917504 | tf_op jit(solution)/shard_map/all_to_all | solution.py:398
  15.5 0.0 copy-done.14
  15.5 0.6 and_compare_fusion.1
  16.1 0.5 copy-done.16
  16.6 0.0 copy-done.12
  16.6 0.0 copy-done.13
  16.6 0.0 copy-start.17
  16.7 0.0 copy-start.10
  16.7 0.1 iota_compare_fusion
  16.8 0.0 collective-permute-done.2
  16.8 0.0 collective-permute-done.1
  16.8 4.1 %shard_map.96 = (bf16[1600,128]{1,0:T(8,128)(2,1)S(1)}, bf16[1600,128]{1,0:T(8,128)(2,1)S(1)}, bf16[1600,128]{1,0:T(8,128)(2,1)}, bf16[1600,128]{1,0:T(8,128)(2,1)}) custom-call(s32[1]{0:T(128)} %bitcast.me_ref.rest_0_, s32[2,2,5,2,5]{4,3,2,1,0:T(2,128)S(1)} %add_bitcast_fusion.move_ref, bf16[64,16,128]{2,1,0:T(8,128)(2,1)S(1)} %copy-done.4, ...), custom_call_target="tpu_custom_call" | custom-call | flops 419430400 | bytes 1761280 | tf_op jit(solution)/shard_map/pallas_call | solution.py:197
  20.9 0.8 %copy-done.1 = bf16[1600,128]{1,0:T(8,128)(2,1)} copy-done((bf16[1600,128]{1,0:T(8,128)(2,1)}, bf16[1600,128]{1,0:T(8,128)(2,1)S(1)}, u32[]{:S(2)}) %copy-start.1) | copy-done | bytes 409624
  21.7 0.0 copy-done.10
  21.7 0.0 collective-permute-start.4
  21.7 3.7 %collective-permute-start.5 = (bf16[1600,128]{1,0:T(8,128)(2,1)}, bf16[1600,128]{1,0:T(8,128)(2,1)}, u32[]{:S(2)}, u32[]{:S(2)}) collective-permute-start(bf16[1600,128]{1,0:T(8,128)(2,1)} %get-tuple-element.20), channel_id=1, source_target_pairs={{8,16},{16,8},{24,32},{32,24},{40,48},{48,40},{56,64},{64,56},{72,... | collective-permute-start | bytes 1228808 | tf_op jit(solution)/shard_map/ppermute | solution.py:446
  25.3 0.0 all-to-all-done
  25.4 0.2 select_reduce_fusion
  25.6 6.5 %collective-permute-start = (bf16[2,224,128]{2,1,0:T(8,128)(2,1)S(1)}, bf16[2,224,128]{2,1,0:T(8,128)(2,1)S(1)}, u32[]{:S(2)}, u32[]{:S(2)}) collective-permute-start(bf16[2,224,128]{2,1,0:T(8,128)(2,1)S(1)} %select_reduce_fusion), channel_id=1, source_target_pairs={{0,128},{8,136},{16,144},{24,152},{32,160},{40,168},{48,176},{56,1... | collective-permute-start | bytes 344072 | tf_op jit(solution)/shard_map/ppermute | solution.py:439
  32.1 0.0 copy-done.17
  32.1 0.9 %copy-done.6 = bf16[2,2,2,16,344]{4,3,2,1,0:T(8,128)(2,1)S(1)} copy-done((bf16[2,2,2,16,344]{4,3,2,1,0:T(8,128)(2,1)S(1)}, bf16[2,2,2,16,344]{4,3,2,1,0:T(8,128)(2,1)}, u32[]{:S(2)}) %copy-start.6) | copy-done | bytes 88088
  33.0 0.7 %copy-done.11 = s32[2,2,5,2,5]{4,3,2,1,0:T(2,128)S(1)} copy-done((s32[2,2,5,2,5]{4,3,2,1,0:T(2,128)S(1)}, s32[2,2,5,2,5]{4,3,2,1,0:T(2,128)}, u32[]{:S(2)}) %copy-start.11) | copy-done | bytes 824
  33.7 3.0 %shard_map.97 = (bf16[1600,128]{1,0:T(8,128)(2,1)S(1)}, bf16[1600,128]{1,0:T(8,128)(2,1)S(1)}) custom-call(s32[1]{0:T(128)} %bitcast.me_ref.rest_0_, s32[2,2,5,2,5]{4,3,2,1,0:T(2,128)S(1)} %copy-done.11, bf16[64,16,128]{2,1,0:T(8,128)(2,1)S(1)} %copy-done.4, bf16[2,2,2,320,344]{4,3,2,1,0:T(8,128)(2,1)S(1)} %bitcast.18, ...), custom_call_target="tpu_custom_call" | custom-call | flops 419430400 | bytes 1761280 | tf_op jit(solution)/shard_map/pallas_call | solution.py:197
  36.8 0.0 copy-start.7
  36.8 0.9 %copy-done.7 = bf16[64,640]{1,0:T(8,128)(2,1)S(1)} copy-done((bf16[64,640]{1,0:T(8,128)(2,1)S(1)}, bf16[64,640]{1,0:T(8,128)(2,1)}, u32[]{:S(2)}) %copy-start.7) | copy-done | bytes 81944
  37.7 0.9 %copy-done.8 = bf16[64,640]{1,0:T(8,128)(2,1)S(1)} copy-done((bf16[64,640]{1,0:T(8,128)(2,1)S(1)}, bf16[64,640]{1,0:T(8,128)(2,1)}, u32[]{:S(2)}) %copy-start.8) | copy-done | bytes 81944
  38.5 1.6 %shard_map.98.rest_5_ = f32[64,128]{1,0:T(8,128)S(1)} custom-call(bf16[64,640]{1,0:T(8,128)(2,1)S(1)} %copy-done.7, bf16[64,640]{1,0:T(8,128)(2,1)S(1)} %copy-done.8, bf16[1600,128]{1,0:T(8,128)(2,1)S(1)} %get-tuple-element.14.rest_0_.s00_ref, bf16[1600,128]{1,0:T(8,128)(2,1)S(1)} %get-tuple-element.15.rest_1_.s10_ref, ...), custom_call_target="tpu_custom_call" | custom-call | flops 100000000 | bytes 1761280 | tf_op jit(solution)/shard_map/pallas_call | solution.py:413
  40.2 0.0 collective-permute-done
  40.2 0.1 broadcast_select_fusion.2
  40.2 1.3 %collective-permute-start.3 = (bf16[2,224,128]{2,1,0:T(8,128)(2,1)S(1)}, bf16[2,224,128]{2,1,0:T(8,128)(2,1)S(1)}, u32[]{:S(2)}, u32[]{:S(2)}) collective-permute-start(bf16[2,224,128]{2,1,0:T(8,128)(2,1)S(1)} %broadcast_select_fusion.2), channel_id=1, source_target_pairs={{0,64},{8,72},{16,80},{24,88},{32,96},{40,104},{48,112},{56,120},{... | collective-permute-start | bytes 344072 | tf_op jit(solution)/shard_map/ppermute | solution.py:439
  41.5 0.0 collective-permute-done.4.rest_2_
  41.5 0.0 collective-permute-done.5.rest_3_
  41.5 3.5 %shard_map.99 = f32[64,128]{1,0:T(8,128)} custom-call(bf16[64,640]{1,0:T(8,128)(2,1)S(1)} %copy-done.7, bf16[64,640]{1,0:T(8,128)(2,1)S(1)} %copy-done.8, s32[1]{0:T(128)} %bitcast.me_ref.rest_0_, bf16[1600,128]{1,0:T(8,128)(2,1)S(1)} %get-tuple-element.15.rest_1_.s10_ref, bf16[1600,128]{1,0:T(8,128)(2,1)} %collective-permute-done.4.rest_2_, ...), custom_call_target="tpu_custom_call" | custom-call | flops 100000000 | bytes 1761280 | tf_op jit(solution)/shard_map/pallas_call | solution.py:413
  45.0 2.0 %collective-permute-done.3 = bf16[2,224,128]{2,1,0:T(8,128)(2,1)S(1)} collective-permute-done((bf16[2,224,128]{2,1,0:T(8,128)(2,1)S(1)}, bf16[2,224,128]{2,1,0:T(8,128)(2,1)S(1)}, u32[]{:S(2)}, u32[]{:S(2)}) %collective-permute-start.3) | collective-permute-done | bytes 114720 | tf_op jit(solution)/shard_map/ppermute | solution.py:439
  47.0 0.0 copy-done.15
  47.0 0.1 broadcast_select_fusion.3
  47.0 0.1 collective-permute-start.6
  47.1 3.6 %collective-permute-done.6 = bf16[2,224,128]{2,1,0:T(8,128)(2,1)S(1)} collective-permute-done((bf16[2,224,128]{2,1,0:T(8,128)(2,1)S(1)}, bf16[2,224,128]{2,1,0:T(8,128)(2,1)S(1)}, u32[]{:S(2)}, u32[]{:S(2)}) %collective-permute-start.6) | collective-permute-done | bytes 114720 | tf_op jit(solution)/shard_map/ppermute | solution.py:434
  50.8 3.5 %collective-permute-start.7 = (bf16[2,448,128]{2,1,0:T(8,128)(2,1)S(1)}, bf16[2,448,128]{2,1,0:T(8,128)(2,1)S(1)}, u32[]{:S(2)}, u32[]{:S(2)}) collective-permute-start(bf16[2,448,128]{2,1,0:T(8,128)(2,1)S(1)} %pad_maximum_fusion.1), channel_id=1, source_target_pairs={{0,16},{8,24},{16,0},{24,8},{32,48},{40,56},{48,32},{56,40},{64,80... | collective-permute-start | bytes 688136 | tf_op jit(solution)/shard_map/ppermute | solution.py:434
  54.3 5.4 %all-to-all-start.1 = ((f32[32,2,128]{2,1,0:T(2,128)}), f32[32,2,128]{2,1,0:T(2,128)S(1)}, u32[]{:S(2)}, u32[]{:S(2)}) async-start(f32[32,2,128]{2,1,0:T(2,128)} %bitcast.4), calls=%async_computation.1 | async-start | bytes 65536 | tf_op jit(solution)/shard_map/all_to_all | solution.py:452
  59.6 0.0 copy-start.9
  59.7 0.0 collective-permute-done.7
  59.7 0.1 broadcast_select_fusion.1
  59.8 8.0 %all-to-all-done.1 = f32[32,2,128]{2,1,0:T(2,128)S(1)} async-done(((f32[32,2,128]{2,1,0:T(2,128)}), f32[32,2,128]{2,1,0:T(2,128)S(1)}, u32[]{:S(2)}, u32[]{:S(2)}) %all-to-all-start.1) | async-done | bytes 32800 | tf_op jit(solution)/shard_map/all_to_all | solution.py:452
  67.8 0.4 collective-permute-start.8
  68.2 0.8 %shard_map.100 = f32[64,128]{1,0:T(8,128)S(1)} custom-call(s32[1]{0:T(128)} %bitcast.me_ref.rest_0_, bf16[2,896,128]{2,1,0:T(8,128)(2,1)S(1)} %pad_maximum_fusion.ref_ref, bf16[1600,128]{1,0:T(8,128)(2,1)S(1)} %get-tuple-element.14.rest_0_.s00_ref, bf16[1600,128]{1,0:T(8,128)(2,1)S(1)} %get-tuple-element.16.rest_2_.rest_4_.s01_ref, ...), custom_call_target="tpu_custom_call" | custom-call | flops 10000000 | bytes 660480 | tf_op jit(solution)/shard_map/pallas_call | solution.py:425
  69.0 0.0 copy-done.9
  69.0 1.1 %shard_map.102 = f32[2,2,2,16,63]{4,3,2,1,0:T(8,128)} custom-call(f32[64,768]{1,0:T(8,128)S(1)} %copy-done.9, f32[64,128]{1,0:T(8,128)S(1)} %bitcast.19), custom_call_target="tpu_custom_call" | custom-call | flops 10000000 | bytes 1000000 | tf_op jit(solution)/shard_map/pallas_call | solution.py:458
  70.1 0.0 collective-permute-done.8.ref_ref
  70.1 0.8 %shard_map.101 = f32[64,128]{1,0:T(8,128)S(1)} custom-call(s32[1]{0:T(128)} %bitcast.me_ref.rest_0_, bf16[2,896,128]{2,1,0:T(8,128)(2,1)S(1)} %collective-permute-done.8.ref_ref, bf16[1600,128]{1,0:T(8,128)(2,1)S(1)} %get-tuple-element.14.rest_0_.s00_ref, bf16[1600,128]{1,0:T(8,128)(2,1)S(1)} %get-tuple-element.16.rest_2_.rest_4_.s01_ref, ...), custom_call_target="tpu_custom_call" | custom-call | flops 10000000 | bytes 660480 | tf_op jit(solution)/shard_map/pallas_call | solution.py:425
  70.9 0.1 copy.17
  71.0 0.1 copy.16
  71.2 0.1 pad_maximum_fusion.2
  71.2 0.1 reshape.54
  71.3 0.6 copy.15
  (22 shorter events, 0.2 us)
Async XLA Ops:
  0.6 14.9 %copy-start.14 = (s32[2]{0:T(128)S(1)}, s32[2]{0:T(128)}, u32[]{:S(2)}) copy-start(s32[2]{0:T(128)} %dates_ref) | copy-start | bytes 28
  0.6 16.0 %copy-start.12 = (s32[2,2,2,5,5]{4,2,3,1,0:T(2,128)S(1)}, s32[2,2,2,5,5]{4,2,3,1,0:T(2,128)}, u32[]{:S(2)}) copy-start(s32[2,2,2,5,5]{4,2,3,1,0:T(2,128)} %param.10) | copy-start | bytes 2404
  0.7 16.0 %copy-start.13 = (s32[2,2,2,5,5]{4,2,3,1,0:T(2,128)S(1)}, s32[2,2,2,5,5]{4,2,3,1,0:T(2,128)}, u32[]{:S(2)}) copy-start(s32[2,2,2,5,5]{4,2,3,1,0:T(2,128)} %param.9) | copy-start | bytes 2404
  1.6 15.2 %copy-start = (bf16[2,2,2,344,320]{3,4,2,1,0:T(8,128)(2,1)S(1)}, bf16[2,2,2,344,320]{3,4,2,1,0:T(8,128)(2,1)}, u32[]{:S(2)}) copy-start(bf16[2,2,2,344,320]{3,4,2,1,0:T(8,128)(2,1)} %param.8) | copy-start | bytes 5283844
  1.7 15.2 %copy-start.4 = (bf16[64,16,128]{2,1,0:T(8,128)(2,1)S(1)}, bf16[64,16,128]{2,1,0:T(8,128)(2,1)}, u32[]{:S(2)}) copy-start(bf16[64,16,128]{2,1,0:T(8,128)(2,1)} %constant.69.clone.table_ref) | copy-start | bytes 786436
  1.7 15.1 %collective-permute-start.2 = (bf16[2,2,2,16,344]{4,3,2,1,0:T(8,128)(2,1)S(1)}, bf16[2,2,2,16,344]{4,3,2,1,0:T(8,128)(2,1)S(1)}, u32[]{:S(2)}, u32[]{:S(2)}) collective-permute-start(bf16[2,2,2,16,344]{4,3,2,1,0:T(8,128)(2,1)S(1)} %get-tuple-element.31), channel_id=1, source_target_pairs={{0,1},{1,0},{2,3},{3,2},{4,5},{5,4},{6,7},{7,6},{8,9},{9,8},{10,11... | collective-permute-start | bytes 264200 | tf_op jit(solution)/shard_map/ppermute | solution.py:375
  1.8 14.9 %collective-permute-start.1 = (bf16[2,2,2,16,344]{4,3,2,1,0:T(8,128)(2,1)S(1)}, bf16[2,2,2,16,344]{4,3,2,1,0:T(8,128)(2,1)S(1)}, u32[]{:S(2)}, u32[]{:S(2)}) collective-permute-start(bf16[2,2,2,16,344]{4,3,2,1,0:T(8,128)(2,1)S(1)} %get-tuple-element.30), channel_id=1, source_target_pairs={{1,2},{2,1},{3,4},{4,3},{5,6},{6,5},{9,10},{10,9},{11,12},{12,11},... | collective-permute-start | bytes 264200 | tf_op jit(solution)/shard_map/ppermute | solution.py:376
  10.4 15.0 %all-to-all-start = ((bf16[8,224,128]{2,1,0:T(8,128)(2,1)}), bf16[8,224,128]{2,1,0:T(8,128)(2,1)S(1)}, u32[]{:S(2)}, u32[]{:S(2)}) async-start(bf16[8,224,128]{2,1,0:T(8,128)(2,1)} %bitcast.20), calls=%async_computation | async-start | bytes 917504 | tf_op jit(solution)/shard_map/all_to_all | solution.py:398
  16.1 0.5 copy-start.16
  16.6 15.4 %copy-start.17 = (s32[2]{0:T(128)S(1)}, s32[2]{0:T(128)}, u32[]{:S(2)}) copy-start(s32[2]{0:T(128)} %copy-done.16) | copy-start | bytes 28
  16.7 5.0 %copy-start.10 = (s32[2,2,5,2,5]{4,3,2,1,0:T(2,128)}, s32[2,2,5,2,5]{4,3,2,1,0:T(2,128)S(1)}, u32[]{:S(2)}) copy-start(s32[2,2,5,2,5]{4,3,2,1,0:T(2,128)S(1)} %add_bitcast_fusion.move_ref) | copy-start | bytes 2404
  16.8 4.1 %copy-start.5 = (bf16[2,2,2,16,344]{4,3,2,1,0:T(8,128)(2,1)}, bf16[2,2,2,16,344]{4,3,2,1,0:T(8,128)(2,1)S(1)}, u32[]{:S(2)}) copy-start(bf16[2,2,2,16,344]{4,3,2,1,0:T(8,128)(2,1)S(1)} %get-tuple-element.37.left_ref) | copy-start | bytes 264196
  20.9 0.8 %copy-start.1 = (bf16[1600,128]{1,0:T(8,128)(2,1)}, bf16[1600,128]{1,0:T(8,128)(2,1)S(1)}, u32[]{:S(2)}) copy-start(bf16[1600,128]{1,0:T(8,128)(2,1)S(1)} %get-tuple-element.17.rest_3_.s11_ref) | copy-start | bytes 1228804
  21.7 19.9 %collective-permute-start.4 = (bf16[1600,128]{1,0:T(8,128)(2,1)}, bf16[1600,128]{1,0:T(8,128)(2,1)}, u32[]{:S(2)}, u32[]{:S(2)}) collective-permute-start(bf16[1600,128]{1,0:T(8,128)(2,1)} %get-tuple-element.19), channel_id=1, source_target_pairs={{0,8},{8,0},{16,24},{24,16},{32,40},{40,32},{48,56},{56,48},{64,72... | collective-permute-start | bytes 1228808 | tf_op jit(solution)/shard_map/ppermute | solution.py:445
  21.7 19.9 %collective-permute-start.5 = (bf16[1600,128]{1,0:T(8,128)(2,1)}, bf16[1600,128]{1,0:T(8,128)(2,1)}, u32[]{:S(2)}, u32[]{:S(2)}) collective-permute-start(bf16[1600,128]{1,0:T(8,128)(2,1)} %get-tuple-element.20), channel_id=1, source_target_pairs={{8,16},{16,8},{24,32},{32,24},{40,48},{48,40},{56,64},{64,56},{72,... | collective-permute-start | bytes 1228808 | tf_op jit(solution)/shard_map/ppermute | solution.py:446
  25.3 11.4 %copy-start.2 = (bf16[1600,128]{1,0:T(8,128)(2,1)S(1)}, bf16[1600,128]{1,0:T(8,128)(2,1)}, u32[]{:S(2)}) copy-start(bf16[1600,128]{1,0:T(8,128)(2,1)} %copy-done.1) | copy-start | bytes 1228804
  25.6 14.5 %collective-permute-start = (bf16[2,224,128]{2,1,0:T(8,128)(2,1)S(1)}, bf16[2,224,128]{2,1,0:T(8,128)(2,1)S(1)}, u32[]{:S(2)}, u32[]{:S(2)}) collective-permute-start(bf16[2,224,128]{2,1,0:T(8,128)(2,1)S(1)} %select_reduce_fusion), channel_id=1, source_target_pairs={{0,128},{8,136},{16,144},{24,152},{32,160},{40,168},{48,176},{56,1... | collective-permute-start | bytes 344072 | tf_op jit(solution)/shard_map/ppermute | solution.py:439
  32.1 0.9 %copy-start.6 = (bf16[2,2,2,16,344]{4,3,2,1,0:T(8,128)(2,1)S(1)}, bf16[2,2,2,16,344]{4,3,2,1,0:T(8,128)(2,1)}, u32[]{:S(2)}) copy-start(bf16[2,2,2,16,344]{4,3,2,1,0:T(8,128)(2,1)} %copy-done.5) | copy-start | bytes 264196
  33.0 0.7 %copy-start.11 = (s32[2,2,5,2,5]{4,3,2,1,0:T(2,128)S(1)}, s32[2,2,5,2,5]{4,3,2,1,0:T(2,128)}, u32[]{:S(2)}) copy-start(s32[2,2,5,2,5]{4,3,2,1,0:T(2,128)} %copy-done.10) | copy-start | bytes 2404
  36.8 0.9 %copy-start.7 = (bf16[64,640]{1,0:T(8,128)(2,1)S(1)}, bf16[64,640]{1,0:T(8,128)(2,1)}, u32[]{:S(2)}) copy-start(bf16[64,640]{1,0:T(8,128)(2,1)} %constant.70.clone.plain_ref) | copy-start | bytes 245764
  37.7 0.9 %copy-start.8 = (bf16[64,640]{1,0:T(8,128)(2,1)S(1)}, bf16[64,640]{1,0:T(8,128)(2,1)}, u32[]{:S(2)}) copy-start(bf16[64,640]{1,0:T(8,128)(2,1)} %constant.71.clone.signed_ref) | copy-start | bytes 245764
  38.5 8.4 %copy-start.15 = (pred[2]{0:T(512)(128)(4,1)S(1)}, pred[2]{0:T(512)(128)(4,1)}, u32[]{:S(2)}) copy-start(pred[2]{0:T(512)(128)(4,1)} %get-tuple-element.28) | copy-start | bytes 10
  40.2 6.7 %collective-permute-start.3 = (bf16[2,224,128]{2,1,0:T(8,128)(2,1)S(1)}, bf16[2,224,128]{2,1,0:T(8,128)(2,1)S(1)}, u32[]{:S(2)}, u32[]{:S(2)}) collective-permute-start(bf16[2,224,128]{2,1,0:T(8,128)(2,1)S(1)} %broadcast_select_fusion.2), channel_id=1, source_target_pairs={{0,64},{8,72},{16,80},{24,88},{32,96},{40,104},{48,112},{56,120},{... | collective-permute-start | bytes 344072 | tf_op jit(solution)/shard_map/ppermute | solution.py:439
  45.0 23.2 %copy-start.3 = (bf16[1600,128]{1,0:T(8,128)(2,1)S(1)}, bf16[1600,128]{1,0:T(8,128)(2,1)}, u32[]{:S(2)}) copy-start(bf16[1600,128]{1,0:T(8,128)(2,1)} %copy-done.1) | copy-start | bytes 1228804
  47.0 3.7 %collective-permute-start.6 = (bf16[2,224,128]{2,1,0:T(8,128)(2,1)S(1)}, bf16[2,224,128]{2,1,0:T(8,128)(2,1)S(1)}, u32[]{:S(2)}, u32[]{:S(2)}) collective-permute-start(bf16[2,224,128]{2,1,0:T(8,128)(2,1)S(1)} %broadcast_select_fusion.3), channel_id=1, source_target_pairs={{0,32},{8,40},{16,48},{24,56},{32,0},{40,8},{48,16},{56,24},{64,96... | collective-permute-start | bytes 344072 | tf_op jit(solution)/shard_map/ppermute | solution.py:434
  50.8 8.8 %collective-permute-start.7 = (bf16[2,448,128]{2,1,0:T(8,128)(2,1)S(1)}, bf16[2,448,128]{2,1,0:T(8,128)(2,1)S(1)}, u32[]{:S(2)}, u32[]{:S(2)}) collective-permute-start(bf16[2,448,128]{2,1,0:T(8,128)(2,1)S(1)} %pad_maximum_fusion.1), channel_id=1, source_target_pairs={{0,16},{8,24},{16,0},{24,8},{32,48},{40,56},{48,32},{56,40},{64,80... | collective-permute-start | bytes 688136 | tf_op jit(solution)/shard_map/ppermute | solution.py:434
  54.3 13.5 %all-to-all-start.1 = ((f32[32,2,128]{2,1,0:T(2,128)}), f32[32,2,128]{2,1,0:T(2,128)S(1)}, u32[]{:S(2)}, u32[]{:S(2)}) async-start(f32[32,2,128]{2,1,0:T(2,128)} %bitcast.4), calls=%async_computation.1 | async-start | bytes 65536 | tf_op jit(solution)/shard_map/all_to_all | solution.py:452
  59.6 9.3 %copy-start.9 = (f32[64,768]{1,0:T(8,128)S(1)}, f32[64,768]{1,0:T(8,128)}, u32[]{:S(2)}) copy-start(f32[64,768]{1,0:T(8,128)} %constant.72.clone.places_ref) | copy-start | bytes 589828
  67.8 2.3 %collective-permute-start.8 = (bf16[2,896,128]{2,1,0:T(8,128)(2,1)S(1)}, bf16[2,896,128]{2,1,0:T(8,128)(2,1)S(1)}, u32[]{:S(2)}, u32[]{:S(2)}) collective-permute-start(bf16[2,896,128]{2,1,0:T(8,128)(2,1)S(1)} %pad_maximum_fusion.ref_ref), channel_id=1, source_target_pairs={{0,8},{8,0},{16,24},{24,16},{32,40},{40,32},{48,56},{56,48},{64,72... | collective-permute-start | bytes 1376264 | tf_op jit(solution)/shard_map/ppermute | solution.py:455

commit v4 on v3

--- a/solution.py
+++ b/solution.py
@@ -65,30 +65,16 @@
     )
 
 
-def reversed_bits(value, count):
-    result = 0
-    while count > 1:
-        result = result * 2 + value % 2
-        value //= 2
-        count //= 2
-    return result
-
-
 def lane_tiles(read, lines, stage):
     whole = lines // LANES
     stage[:, 0 : lines - whole * LANES] = read(slice(whole * LANES, lines))
     return [read(slice(k * LANES, (k + 1) * LANES)) for k in range(whole)] + [stage[...]]
 
 
-def candidate_body(group, dates_ref, me_ref, x_ref, out_ref, stage):
+def candidate_body(dates_ref, me_ref, x_ref, out_ref, stage):
     cols, lines = x_ref.shape[-2:]
     chips_az = (lines - 2 * MARGIN) // CHIP
     lane = lane_index((cols, LANES))
-    steps = out_ref.shape[0] // PACK // group
-
-    def place(step):
-        return (reversed_bits(step // steps, group) * steps + step % steps) * PACK
-
     parts = [lane_tiles(lambda part, p=p: x_ref[0, 0, p, :, part], lines, stage.at[p]) for p in range(2)]
     for a in range(chips_az):
         start = MARGIN + a * CHIP
@@ -101,12 +87,9 @@
                 value = jnp.where(lane < p * CHIP + LANES - offset, value, pltpu.roll(parts[p][tile + 1], shift, 1))
             halves.append(value)
         value = jnp.where(lane < CHIP, halves[0], halves[1])
-        for k in range(cols // PACK):
-            at = place(a * (cols // PACK) + k)
-            out_ref[at : at + PACK, :] = value[PACK * k : PACK * (k + 1)]
-    for step in range(chips_az * cols // PACK, out_ref.shape[0] // PACK):
-        at = place(step)
-        out_ref[at : at + PACK, :] = jnp.zeros((PACK, LANES), BF16)
+        out_ref[a * cols : (a + 1) * cols, :] = value
+    filled = chips_az * cols
+    out_ref[filled:, :] = jnp.zeros((out_ref.shape[0] - filled, LANES), BF16)
 
 
 def resample_body(crossed, me_ref, move_ref, table_ref, x_ref, left_ref, right_ref, *rest):
@@ -383,7 +366,7 @@
         return (lax.rem(dates_ref[tile], dates), tile, 0, 0, 0)
 
     candidate = pl.pallas_call(
-        functools.partial(candidate_body, near),
+        candidate_body,
         out_shape=shape((piece * near, LANES), BF16),
         grid_spec=pltpu.PrefetchScalarGridSpec(
             num_scalar_prefetch=2,
@@ -395,16 +378,20 @@
         cost_estimate=pl.CostEstimate(flops=10**6, bytes_accessed=4 * image_bytes, transcendentals=0),
         compiler_params=pltpu.CompilerParams(vmem_limit_bytes=60 << 20),
     )(after(ref_dates, to_one, to_other), me_one, images)
-    scattered = lax.all_to_all(
-        candidate.reshape(near, piece, LANES),
-        "date",
-        0,
-        0,
-        axis_index_groups=[list(range(k, k + near)) for k in range(0, group, near)],
-        tiled=True,
-    )
-    from_owner = jnp.arange(near)[None, :] == (owners % near)[:, None]
-    reference = jnp.sum(jnp.where(from_owner[:, :, None, None], scattered[None], 0), axis=1, dtype=BF16)
+    reference = jnp.stack([candidate] * tiles)
+    step = 1
+    while step < near:
+        halves = reference.reshape(tiles, 2, -1, LANES)
+        high = (me & step) != 0
+        own = jnp.where(high, halves[:, 1], halves[:, 0])
+        away = jnp.where(high, halves[:, 0], halves[:, 1])
+        if step == 1:
+            away = away[0]
+        other = lax.ppermute(away, "date", [(i, i ^ step) for i in range(group)])
+        same = ((me ^ owners) & step) == 0
+        reference = jnp.where(same[:, None, None], own, other if step > 1 else other[None])
+        step *= 2
+
     edges = (jnp.where(even, from_other, from_one), jnp.where(even, from_one, from_other))
 
     resample = functools.partial(resample_call, me=me_one, moves=moves, table=table, images=images, edges=edges)
@@ -444,13 +431,13 @@
     s00, s11, send1, send2 = resample(False)
     got1 = lax.ppermute(send1, "date", [(i, i ^ 1) for i in range(group)])
     got2 = lax.ppermute(send2, "date", [(i, (i + 1 ^ 1) - 1) for i in range(1, group - 1)])
+    reference = flood(after(reference, s00), 8)
     s01, s10 = resample(True)
     looked = pair(0, s00, s10, s01, s11)
-    reference = flood(after(reference, looked), 8)
+    reference = exchange(after(reference, looked), 4)
     looked = pair(1, me_one, s10, got1, got2, s01, looked)
-    reference = exchange(after(reference, looked), 4)
     relayed = lax.all_to_all(looked.reshape(group, -1, LANES), "date", 0, 0, tiled=True)
-    reference = exchange(reference, 2)
+    reference = exchange(after(reference, looked), 2)
     reference, relayed = lax.optimization_barrier((reference, relayed))
     other = lax.ppermute(reference, "date", [(i, i ^ 1) for i in range(group)])
 

time: 72.5 us -> 75.6 us (1.043)
  local copies, waits for them, and re-layouts: 5.63 us -> 0.98 us
  starting transfers between devices: 31.8 us -> 36.2 us
  other arithmetic: 2.35 us -> 5.69 us
  waiting for transfers between devices: 13.6 us -> 15.7 us
  Pallas kernels: 17.7 us -> 15.8 us
    ppermute x0 -> x3, waiting for transfers between devices: none -> 5.24 us  [per_device(): other = lax.ppermute(away, 'date', [(i, i ^ step) for i in range(group)])]
    all_to_all x1 -> x0, starting transfers between devices: 5.14 us -> none  [per_device(): lax.all_to_all(candidate.reshape(near, piece, LANES), 'date', 0, 0, axis_...]
    all_to_all x1, starting transfers between devices: 5.36 us -> 10.1 us  [per_device(): lax.all_to_all(looked.reshape(group, -1, LANES), 'date', 0, 0, tiled=True)]
    unnamed x39 -> x27, local copies, waits for them, and re-layouts: 5.55 us -> 0.9 us
    ppermute x2, waiting for transfers between devices: 3.63 us -> 0.01 us  [exchange(): other = lax.ppermute(value, 'date', [(i, i ^ step) for i in range(group)])]
    ppermute x0 -> x3, starting transfers between devices: none -> 3.58 us  [per_device(): other = lax.ppermute(away, 'date', [(i, i ^ step) for i in range(group)])]
    ppermute x1, starting transfers between devices: 0.01 us -> 3.21 us  [per_device(): got1 = lax.ppermute(send1, 'date', [(i, i ^ 1) for i in range(group)])]
    ppermute x1, starting transfers between devices: 5.74 us -> 3.17 us  [per_device(): from_other = lax.ppermute(to_other, 'strip', pairs2)]
  transfers between devices with their start and end apart: 11 -> 13, of which waited for: 3 -> 5; matrix products, arithmetic and copies ran while one was open for 2% -> 2% of each run, Pallas kernels for 23% -> 16%
where the time goes in v4:
time: 75.6 us; the launch traced here: 75.3 us
  starting transfers between devices  36.2 us (48%)
  Pallas kernels  15.8 us (21%)
  waiting for transfers between devices  15.7 us (21%)
  other arithmetic  5.69 us (8%)
  local copies, waits for them, and re-layouts  0.98 us (1%)
  between operations  0.95 us (1%)
    all_to_all x1, starting transfers between devices, per_device(): lax.all_to_all(looked.reshape(group, -1, LANES), 'date', 0, 0, tiled=True)  10.1 us
    ppermute x2, starting transfers between devices, flood(): other = lax.ppermute(value, 'date', [(i, i ^ step) for i in range(group)])  8.92 us
    all_to_all x1, waiting for transfers between devices, per_device(): lax.all_to_all(looked.reshape(group, -1, LANES), 'date', 0, 0, tiled=True)  8.01 us
    pallas_call x2, Pallas kernels, resample_call(): pl.pallas_call(functools.partial(resample_body, crossed), out_shape=[jax....  6.24 us
    ppermute x3, waiting for transfers between devices, per_device(): other = lax.ppermute(away, 'date', [(i, i ^ step) for i in range(group)])  5.24 us
    pallas_call x2, Pallas kernels, pair(): call(functools.partial(pair_body, index), shape((blocks, LANES), F32), [V...  3.94 us
    ppermute x3, starting transfers between devices, per_device(): other = lax.ppermute(away, 'date', [(i, i ^ step) for i in range(group)])  3.58 us
    ppermute x1, starting transfers between devices, per_device(): got1 = lax.ppermute(send1, 'date', [(i, i ^ 1) for i in range(group)])  3.21 us
  transfers between devices with their start and end apart: 13, of which 5 were waited for; matrix products, arithmetic and copies ran while one was open for 2% of the time, Pallas kernels for 16%

profile of v4, /device:TPU:19, one launch (start us, length us, event | category | flops | bytes accessed | tf_op | source)
XLA Modules:
  0.0 75.3 jit_solution(10460540176596105595)
XLA Ops:
  0.6 1.6 %broadcast_select_fusion.9 = (bf16[2,2,2,16,344]{4,3,2,1,0:T(8,128)(2,1)}, bf16[2,2,2,16,344]{4,3,2,1,0:T(8,128)(2,1)S(1)}) fusion(pred[]{:T(512)S(6)} %eq.30, bf16[2,2,2,320,344]{4,3,2,1,0:T(8,128)(2,1)} %bitcast.58), kind=kLoop, calls=%fused_computation.29 | loop fusion | flops 88064 | bytes 352257 | tf_op jit(solution)/shard_map/jit(_where)/select_n | solution.py:357
  2.3 2.9 %shard_map.95 = bf16[1792,128]{1,0:T(8,128)(2,1)} custom-call(s32[2]{0:T(128)} %dates_ref, s32[1]{0:T(128)} %bitcast.me_ref.rest_0_, bf16[2,2,2,320,344]{4,3,2,1,0:T(8,128)(2,1)} %bitcast.59), custom_call_target="tpu_custom_call" | custom-call | flops 1000000 | bytes 880640 | tf_op jit(solution)/shard_map/pallas_call | solution.py:368
  5.2 1.4 %maximum_select_fusion = (bf16[2,1,896,128]{3,2,0,1:T(8,128)(2,1)S(1)}, bf16[2,1,896,128]{3,2,0,1:T(8,128)(2,1)S(1)}) fusion(pred[]{:T(512)S(6)} %ne.34, bf16[1,2,896,128]{3,2,0,1:T(8,128)(2,1)} %bitcast.63), kind=kLoop, calls=%fused_computation.3 | loop fusion | flops 688128 | bytes 1376257 | tf_op jit(solution)/shard_map/jit(_where)/select_n | solution.py:386
  6.6 0.0 copy-start.7
  6.6 0.0 copy-start.8
  6.6 1.0 %fusion.3 = bf16[896,128]{1,0:T(8,128)(2,1)S(1)} fusion(bf16[1,2,896,128]{3,2,0,1:T(8,128)(2,1)} %bitcast.64, bf16[2,1,896,128]{3,2,0,1:T(8,128)(2,1)S(1)} %get-tuple-element.33, pred[]{:T(512)S(6)} %ne.34), kind=kLoop, calls=%fused_computation.11 | loop fusion | flops 229376 | bytes 917505 | tf_op jit(solution)/shard_map/squeeze | solution.py:389
  7.6 0.8 %collective-permute-start = (bf16[896,128]{1,0:T(8,128)(2,1)S(1)}, bf16[896,128]{1,0:T(8,128)(2,1)S(1)}, u32[]{:S(2)}, u32[]{:S(2)}) collective-permute-start(bf16[896,128]{1,0:T(8,128)(2,1)S(1)} %fusion.3), channel_id=1, source_target_pairs={{0,8},{8,0},{16,24},{24,16},{32,40},{40,32},{48,56},{56,48},{64,72... | collective-permute-start | bytes 688136 | tf_op jit(solution)/shard_map/ppermute | solution.py:390
  8.3 0.0 copy-done.10
  8.3 0.5 and_compare_fusion.4
  8.9 0.5 and_compare_fusion.3
  9.3 0.1 collective-permute-done
  9.5 0.1 broadcast_select_fusion
  9.6 1.1 %collective-permute-start.1 = (bf16[2,448,128]{2,1,0:T(8,128)(2,1)S(1)}, bf16[2,448,128]{2,1,0:T(8,128)(2,1)S(1)}, u32[]{:S(2)}, u32[]{:S(2)}) collective-permute-start(bf16[2,448,128]{2,1,0:T(8,128)(2,1)S(1)} %fusion.4), channel_id=1, source_target_pairs={{0,16},{8,24},{16,0},{24,8},{32,48},{40,56},{48,32},{56,40},{64,80... | collective-permute-start | bytes 688136 | tf_op jit(solution)/shard_map/ppermute | solution.py:390
  10.7 3.2 %collective-permute-start.4 = (bf16[2,2,2,16,344]{4,3,2,1,0:T(8,128)(2,1)}, bf16[2,2,2,16,344]{4,3,2,1,0:T(8,128)(2,1)S(1)}, u32[]{:S(2)}, u32[]{:S(2)}) collective-permute-start(bf16[2,2,2,16,344]{4,3,2,1,0:T(8,128)(2,1)} %get-tuple-element.34), channel_id=1, source_target_pairs={{1,2},{2,1},{3,4},{4,3},{5,6},{6,5},{9,10},{10,9},{11,12},{12,11},... | collective-permute-start | bytes 264200 | tf_op jit(solution)/shard_map/ppermute | solution.py:359
  13.9 1.8 %collective-permute-start.5 = (bf16[2,2,2,16,344]{4,3,2,1,0:T(8,128)(2,1)S(1)}, bf16[2,2,2,16,344]{4,3,2,1,0:T(8,128)(2,1)S(1)}, u32[]{:S(2)}, u32[]{:S(2)}) collective-permute-start(bf16[2,2,2,16,344]{4,3,2,1,0:T(8,128)(2,1)S(1)} %get-tuple-element.35), channel_id=1, source_target_pairs={{0,1},{1,0},{2,3},{3,2},{4,5},{5,4},{6,7},{7,6},{8,9},{9,8},{10,11... | collective-permute-start | bytes 264200 | tf_op jit(solution)/shard_map/ppermute | solution.py:358
  15.6 3.0 %collective-permute-done.1 = bf16[2,448,128]{2,1,0:T(8,128)(2,1)S(1)} collective-permute-done((bf16[2,448,128]{2,1,0:T(8,128)(2,1)S(1)}, bf16[2,448,128]{2,1,0:T(8,128)(2,1)S(1)}, u32[]{:S(2)}, u32[]{:S(2)}) %collective-permute-start.1) | collective-permute-done | bytes 229408 | tf_op jit(solution)/shard_map/ppermute | solution.py:390
  18.6 0.1 fusion.6
  18.7 0.0 copy-start.9
  18.7 1.7 %collective-permute-start.2 = (bf16[2,224,128]{2,1,0:T(8,128)(2,1)S(1)}, bf16[2,224,128]{2,1,0:T(8,128)(2,1)S(1)}, u32[]{:S(2)}, u32[]{:S(2)}) collective-permute-start(bf16[2,224,128]{2,1,0:T(8,128)(2,1)S(1)} %select_bitcast_fusion), channel_id=1, source_target_pairs={{0,32},{8,40},{16,48},{24,56},{32,0},{40,8},{48,16},{56,24},{64,96... | collective-permute-start | bytes 344072 | tf_op jit(solution)/shard_map/ppermute | solution.py:390
  20.5 0.0 copy-done.7
  20.5 0.0 copy-done.8
  20.5 2.2 %collective-permute-done.2 = bf16[2,224,128]{2,1,0:T(8,128)(2,1)S(1)} collective-permute-done((bf16[2,224,128]{2,1,0:T(8,128)(2,1)S(1)}, bf16[2,224,128]{2,1,0:T(8,128)(2,1)S(1)}, u32[]{:S(2)}, u32[]{:S(2)}) %collective-permute-start.2) | collective-permute-done | bytes 114720 | tf_op jit(solution)/shard_map/ppermute | solution.py:390
  22.6 0.1 bitcast_select_fusion.2
  22.7 6.8 %collective-permute-start.3 = (bf16[2,224,128]{2,1,0:T(8,128)(2,1)S(1)}, bf16[2,224,128]{2,1,0:T(8,128)(2,1)S(1)}, u32[]{:S(2)}, u32[]{:S(2)}) collective-permute-start(bf16[2,224,128]{2,1,0:T(8,128)(2,1)S(1)} %bitcast_select_fusion.2), channel_id=1, source_target_pairs={{0,128},{8,136},{16,144},{24,152},{32,160},{40,168},{48,176},{56,1... | collective-permute-start | bytes 344072 | tf_op jit(solution)/shard_map/ppermute | solution.py:426
  29.5 0.0 collective-permute-done.4
  29.6 0.0 collective-permute-done.5
  29.6 0.0 copy-done
  29.6 0.0 copy-done.3
  29.6 3.2 %shard_map.96 = (bf16[1600,128]{1,0:T(8,128)(2,1)S(1)}, bf16[1600,128]{1,0:T(8,128)(2,1)S(1)}, bf16[1600,128]{1,0:T(8,128)(2,1)S(1)}, bf16[1600,128]{1,0:T(8,128)(2,1)S(1)}) custom-call(s32[1]{0:T(128)} %bitcast.me_ref.rest_0_, s32[2,2,5,2,5]{4,3,2,1,0:T(2,128)S(1)} %add_bitcast_fusion.move_ref, bf16[64,16,128]{2,1,0:T(8,128)(2,1)S(1)} %copy-done.3, ...), custom_call_target="tpu_custom_call" | custom-call | flops 419430400 | bytes 1761280 | tf_op jit(solution)/shard_map/pallas_call | solution.py:180
  32.8 0.0 copy-start.1
  32.8 0.0 copy-start.4
  32.8 0.0 copy-start.5
  32.8 0.0 collective-permute-done.3
  32.8 0.0 copy-done.9
  32.8 0.1 broadcast_select_fusion.3
  32.9 2.1 %collective-permute-start.6 = (bf16[2,224,128]{2,1,0:T(8,128)(2,1)S(1)}, bf16[2,224,128]{2,1,0:T(8,128)(2,1)S(1)}, u32[]{:S(2)}, u32[]{:S(2)}) collective-permute-start(bf16[2,224,128]{2,1,0:T(8,128)(2,1)S(1)} %broadcast_select_fusion.3), channel_id=1, source_target_pairs={{0,64},{8,72},{16,80},{24,88},{32,96},{40,104},{48,112},{56,120},{... | collective-permute-start | bytes 344072 | tf_op jit(solution)/shard_map/ppermute | solution.py:426
  35.0 3.2 %collective-permute-start.8 = (bf16[1600,128]{1,0:T(8,128)(2,1)S(1)}, bf16[1600,128]{1,0:T(8,128)(2,1)S(1)}, u32[]{:S(2)}, u32[]{:S(2)}) collective-permute-start(bf16[1600,128]{1,0:T(8,128)(2,1)S(1)} %get-tuple-element.21), channel_id=1, source_target_pairs={{0,8},{8,0},{16,24},{24,16},{32,40},{40,32},{48,56},{56,48},{64,72... | collective-permute-start | bytes 1228808 | tf_op jit(solution)/shard_map/ppermute | solution.py:432
  38.2 2.9 %collective-permute-start.9 = (bf16[1600,128]{1,0:T(8,128)(2,1)S(1)}, bf16[1600,128]{1,0:T(8,128)(2,1)S(1)}, u32[]{:S(2)}, u32[]{:S(2)}) collective-permute-start(bf16[1600,128]{1,0:T(8,128)(2,1)S(1)} %get-tuple-element.22), channel_id=1, source_target_pairs={{8,16},{16,8},{24,32},{32,24},{40,48},{48,40},{56,64},{64,56},{72,... | collective-permute-start | bytes 1228808 | tf_op jit(solution)/shard_map/ppermute | solution.py:433
  41.2 3.1 %shard_map.97 = (bf16[1600,128]{1,0:T(8,128)(2,1)S(1)}, bf16[1600,128]{1,0:T(8,128)(2,1)S(1)}) custom-call(s32[1]{0:T(128)} %bitcast.me_ref.rest_0_, s32[2,2,5,2,5]{4,3,2,1,0:T(2,128)S(1)} %add_bitcast_fusion.move_ref, bf16[64,16,128]{2,1,0:T(8,128)(2,1)S(1)} %copy-done.3, bf16[2,2,2,320,344]{4,3,2,1,0:T(8,128)(2,1)S(1)} %bitcast.61, ...), custom_call_target="tpu_custom_call" | custom-call | flops 419430400 | bytes 1761280 | tf_op jit(solution)/shard_map/pallas_call | solution.py:180
  44.3 1.6 %shard_map.98.rest_5_ = f32[64,128]{1,0:T(8,128)S(1)} custom-call(bf16[64,640]{1,0:T(8,128)(2,1)S(1)} %copy-done.5, bf16[64,640]{1,0:T(8,128)(2,1)S(1)} %copy-done.4, bf16[1600,128]{1,0:T(8,128)(2,1)S(1)} %get-tuple-element.15.rest_0_.s00_ref, bf16[1600,128]{1,0:T(8,128)(2,1)S(1)} %get-tuple-element.17.rest_1_.s10_ref, ...), custom_call_target="tpu_custom_call" | custom-call | flops 100000000 | bytes 1761280 | tf_op jit(solution)/shard_map/pallas_call | solution.py:400
  45.9 0.0 copy-done.1
  45.9 0.0 collective-permute-done.6
  45.9 0.1 broadcast_select_fusion.4
  46.0 2.1 %collective-permute-start.7 = (bf16[2,224,128]{2,1,0:T(8,128)(2,1)S(1)}, bf16[2,224,128]{2,1,0:T(8,128)(2,1)S(1)}, u32[]{:S(2)}, u32[]{:S(2)}) collective-permute-start(bf16[2,224,128]{2,1,0:T(8,128)(2,1)S(1)} %broadcast_select_fusion.4), channel_id=1, source_target_pairs={{0,32},{8,40},{16,48},{24,56},{32,0},{40,8},{48,16},{56,24},{64,96... | collective-permute-start | bytes 344072 | tf_op jit(solution)/shard_map/ppermute | solution.py:421
  48.0 0.0 collective-permute-done.8.rest_2_
  48.1 2.4 %collective-permute-done.9.rest_3_ = bf16[1600,128]{1,0:T(8,128)(2,1)S(1)} collective-permute-done((bf16[1600,128]{1,0:T(8,128)(2,1)S(1)}, bf16[1600,128]{1,0:T(8,128)(2,1)S(1)}, u32[]{:S(2)}, u32[]{:S(2)}) %collective-permute-start.9) | collective-permute-done | bytes 409632 | tf_op jit(solution)/shard_map/ppermute | solution.py:433
  50.4 2.3 %shard_map.99 = f32[64,128]{1,0:T(8,128)} custom-call(bf16[64,640]{1,0:T(8,128)(2,1)S(1)} %copy-done.5, bf16[64,640]{1,0:T(8,128)(2,1)S(1)} %copy-done.4, s32[1]{0:T(128)} %bitcast.me_ref.rest_0_, bf16[1600,128]{1,0:T(8,128)(2,1)S(1)} %get-tuple-element.17.rest_1_.s10_ref, bf16[1600,128]{1,0:T(8,128)(2,1)S(1)} %collective-permute-done.8.rest_2_, ...), custom_call_target="tpu_custom_call" | custom-call | flops 100000000 | bytes 1761280 | tf_op jit(solution)/shard_map/pallas_call | solution.py:400
  52.8 0.0 collective-permute-done.7
  52.8 0.1 collective-permute-start.10
  52.9 10.1 %all-to-all-start = ((f32[32,2,128]{2,1,0:T(2,128)}), f32[32,2,128]{2,1,0:T(2,128)S(1)}, u32[]{:S(2)}, u32[]{:S(2)}) async-start(f32[32,2,128]{2,1,0:T(2,128)} %bitcast.16), calls=%async_computation | async-start | bytes 65536 | tf_op jit(solution)/shard_map/all_to_all | solution.py:439
  63.0 0.0 copy-start.6
  63.0 0.0 collective-permute-done.10
  63.1 8.0 %all-to-all-done = f32[32,2,128]{2,1,0:T(2,128)S(1)} async-done(((f32[32,2,128]{2,1,0:T(2,128)}), f32[32,2,128]{2,1,0:T(2,128)S(1)}, u32[]{:S(2)}, u32[]{:S(2)}) %all-to-all-start) | async-done | bytes 32800 | tf_op jit(solution)/shard_map/all_to_all | solution.py:439
  71.1 0.4 collective-permute-start.11
  71.5 0.0 copy-done.2
  71.5 0.8 %shard_map.100 = f32[64,128]{1,0:T(8,128)S(1)} custom-call(s32[1]{0:T(128)} %bitcast.me_ref.rest_0_, bf16[2,896,128]{2,1,0:T(8,128)(2,1)S(1)} %pad_maximum_fusion.ref_ref, bf16[1600,128]{1,0:T(8,128)(2,1)S(1)} %get-tuple-element.15.rest_0_.s00_ref, bf16[1600,128]{1,0:T(8,128)(2,1)S(1)} %get-tuple-element.18.rest_2_.rest_4_.s01_ref, ...), custom_call_target="tpu_custom_call" | custom-call | flops 10000000 | bytes 660480 | tf_op jit(solution)/shard_map/pallas_call | solution.py:412
  72.3 1.1 %shard_map.102 = f32[2,2,2,16,63]{4,3,2,1,0:T(8,128)} custom-call(f32[64,768]{1,0:T(8,128)S(1)} %copy-done.6, f32[64,128]{1,0:T(8,128)S(1)} %bitcast.62), custom_call_target="tpu_custom_call" | custom-call | flops 10000000 | bytes 1000000 | tf_op jit(solution)/shard_map/pallas_call | solution.py:445
  73.5 0.0 collective-permute-done.11.ref_ref
  73.5 0.8 %shard_map.101 = f32[64,128]{1,0:T(8,128)S(1)} custom-call(s32[1]{0:T(128)} %bitcast.me_ref.rest_0_, bf16[2,896,128]{2,1,0:T(8,128)(2,1)S(1)} %collective-permute-done.11.ref_ref, bf16[1600,128]{1,0:T(8,128)(2,1)S(1)} %get-tuple-element.15.rest_0_.s00_ref, bf16[1600,128]{1,0:T(8,128)(2,1)S(1)} %get-tuple-element.18.rest_2_.rest_4_.s01_ref, ...), custom_call_target="tpu_custom_call" | custom-call | flops 10000000 | bytes 660480 | tf_op jit(solution)/shard_map/pallas_call | solution.py:412
  74.3 0.1 copy.33
  74.4 0.1 copy.34
  74.5 0.1 pad_maximum_fusion.2
  74.6 0.1 reshape.60
  74.7 0.6 copy.29
  (18 shorter events, 0.2 us)
Async XLA Ops:
  2.3 6.1 %copy-start.10 = (s32[2]{0:T(128)S(1)}, s32[2]{0:T(128)}, u32[]{:S(2)}) copy-start(s32[2]{0:T(128)} %dates_ref) | copy-start | bytes 28
  6.6 13.9 %copy-start.7 = (s32[2,2,2,5,5]{4,2,3,1,0:T(2,128)S(1)}, s32[2,2,2,5,5]{4,2,3,1,0:T(2,128)}, u32[]{:S(2)}) copy-start(s32[2,2,2,5,5]{4,2,3,1,0:T(2,128)} %param.10) | copy-start | bytes 2404
  6.6 13.9 %copy-start.8 = (s32[2,2,2,5,5]{4,2,3,1,0:T(2,128)S(1)}, s32[2,2,2,5,5]{4,2,3,1,0:T(2,128)}, u32[]{:S(2)}) copy-start(s32[2,2,2,5,5]{4,2,3,1,0:T(2,128)} %param.9) | copy-start | bytes 2404
  7.6 1.9 %collective-permute-start = (bf16[896,128]{1,0:T(8,128)(2,1)S(1)}, bf16[896,128]{1,0:T(8,128)(2,1)S(1)}, u32[]{:S(2)}, u32[]{:S(2)}) collective-permute-start(bf16[896,128]{1,0:T(8,128)(2,1)S(1)} %fusion.3), channel_id=1, source_target_pairs={{0,8},{8,0},{16,24},{24,16},{32,40},{40,32},{48,56},{56,48},{64,72... | collective-permute-start | bytes 688136 | tf_op jit(solution)/shard_map/ppermute | solution.py:390
  9.4 20.1 %copy-start = (bf16[2,2,2,344,320]{3,4,2,1,0:T(8,128)(2,1)S(1)}, bf16[2,2,2,344,320]{3,4,2,1,0:T(8,128)(2,1)}, u32[]{:S(2)}) copy-start(bf16[2,2,2,344,320]{3,4,2,1,0:T(8,128)(2,1)} %param.8) | copy-start | bytes 5283844
  9.5 20.1 %copy-start.3 = (bf16[64,16,128]{2,1,0:T(8,128)(2,1)S(1)}, bf16[64,16,128]{2,1,0:T(8,128)(2,1)}, u32[]{:S(2)}) copy-start(bf16[64,16,128]{2,1,0:T(8,128)(2,1)} %constant.56.clone.table_ref) | copy-start | bytes 786436
  9.6 9.0 %collective-permute-start.1 = (bf16[2,448,128]{2,1,0:T(8,128)(2,1)S(1)}, bf16[2,448,128]{2,1,0:T(8,128)(2,1)S(1)}, u32[]{:S(2)}, u32[]{:S(2)}) collective-permute-start(bf16[2,448,128]{2,1,0:T(8,128)(2,1)S(1)} %fusion.4), channel_id=1, source_target_pairs={{0,16},{8,24},{16,0},{24,8},{32,48},{40,56},{48,32},{56,40},{64,80... | collective-permute-start | bytes 688136 | tf_op jit(solution)/shard_map/ppermute | solution.py:390
  10.7 18.9 %collective-permute-start.4 = (bf16[2,2,2,16,344]{4,3,2,1,0:T(8,128)(2,1)}, bf16[2,2,2,16,344]{4,3,2,1,0:T(8,128)(2,1)S(1)}, u32[]{:S(2)}, u32[]{:S(2)}) collective-permute-start(bf16[2,2,2,16,344]{4,3,2,1,0:T(8,128)(2,1)} %get-tuple-element.34), channel_id=1, source_target_pairs={{1,2},{2,1},{3,4},{4,3},{5,6},{6,5},{9,10},{10,9},{11,12},{12,11},... | collective-permute-start | bytes 264200 | tf_op jit(solution)/shard_map/ppermute | solution.py:359
  13.9 15.7 %collective-permute-start.5 = (bf16[2,2,2,16,344]{4,3,2,1,0:T(8,128)(2,1)S(1)}, bf16[2,2,2,16,344]{4,3,2,1,0:T(8,128)(2,1)S(1)}, u32[]{:S(2)}, u32[]{:S(2)}) collective-permute-start(bf16[2,2,2,16,344]{4,3,2,1,0:T(8,128)(2,1)S(1)} %get-tuple-element.35), channel_id=1, source_target_pairs={{0,1},{1,0},{2,3},{3,2},{4,5},{5,4},{6,7},{7,6},{8,9},{9,8},{10,11... | collective-permute-start | bytes 264200 | tf_op jit(solution)/shard_map/ppermute | solution.py:358
  18.7 14.1 %copy-start.9 = (pred[2]{0:T(512)(128)(4,1)S(1)}, pred[2]{0:T(512)(128)(4,1)}, u32[]{:S(2)}) copy-start(pred[2]{0:T(512)(128)(4,1)} %get-tuple-element.44) | copy-start | bytes 10
  18.7 3.9 %collective-permute-start.2 = (bf16[2,224,128]{2,1,0:T(8,128)(2,1)S(1)}, bf16[2,224,128]{2,1,0:T(8,128)(2,1)S(1)}, u32[]{:S(2)}, u32[]{:S(2)}) collective-permute-start(bf16[2,224,128]{2,1,0:T(8,128)(2,1)S(1)} %select_bitcast_fusion), channel_id=1, source_target_pairs={{0,32},{8,40},{16,48},{24,56},{32,0},{40,8},{48,16},{56,24},{64,96... | collective-permute-start | bytes 344072 | tf_op jit(solution)/shard_map/ppermute | solution.py:390
  22.7 10.1 %collective-permute-start.3 = (bf16[2,224,128]{2,1,0:T(8,128)(2,1)S(1)}, bf16[2,224,128]{2,1,0:T(8,128)(2,1)S(1)}, u32[]{:S(2)}, u32[]{:S(2)}) collective-permute-start(bf16[2,224,128]{2,1,0:T(8,128)(2,1)S(1)} %bitcast_select_fusion.2), channel_id=1, source_target_pairs={{0,128},{8,136},{16,144},{24,152},{32,160},{40,168},{48,176},{56,1... | collective-permute-start | bytes 344072 | tf_op jit(solution)/shard_map/ppermute | solution.py:426
  32.8 13.1 %copy-start.1 = (bf16[1600,128]{1,0:T(8,128)(2,1)}, bf16[1600,128]{1,0:T(8,128)(2,1)S(1)}, u32[]{:S(2)}) copy-start(bf16[1600,128]{1,0:T(8,128)(2,1)S(1)} %get-tuple-element.19.rest_3_.s11_ref) | copy-start | bytes 1228804
  32.8 11.4 %copy-start.4 = (bf16[64,640]{1,0:T(8,128)(2,1)S(1)}, bf16[64,640]{1,0:T(8,128)(2,1)}, u32[]{:S(2)}) copy-start(bf16[64,640]{1,0:T(8,128)(2,1)} %constant.58.clone.signed_ref) | copy-start | bytes 245764
  32.8 11.4 %copy-start.5 = (bf16[64,640]{1,0:T(8,128)(2,1)S(1)}, bf16[64,640]{1,0:T(8,128)(2,1)}, u32[]{:S(2)}) copy-start(bf16[64,640]{1,0:T(8,128)(2,1)} %constant.57.clone.plain_ref) | copy-start | bytes 245764
  32.9 12.9 %collective-permute-start.6 = (bf16[2,224,128]{2,1,0:T(8,128)(2,1)S(1)}, bf16[2,224,128]{2,1,0:T(8,128)(2,1)S(1)}, u32[]{:S(2)}, u32[]{:S(2)}) collective-permute-start(bf16[2,224,128]{2,1,0:T(8,128)(2,1)S(1)} %broadcast_select_fusion.3), channel_id=1, source_target_pairs={{0,64},{8,72},{16,80},{24,88},{32,96},{40,104},{48,112},{56,120},{... | collective-permute-start | bytes 344072 | tf_op jit(solution)/shard_map/ppermute | solution.py:426
  35.0 13.0 %collective-permute-start.8 = (bf16[1600,128]{1,0:T(8,128)(2,1)S(1)}, bf16[1600,128]{1,0:T(8,128)(2,1)S(1)}, u32[]{:S(2)}, u32[]{:S(2)}) collective-permute-start(bf16[1600,128]{1,0:T(8,128)(2,1)S(1)} %get-tuple-element.21), channel_id=1, source_target_pairs={{0,8},{8,0},{16,24},{24,16},{32,40},{40,32},{48,56},{56,48},{64,72... | collective-permute-start | bytes 1228808 | tf_op jit(solution)/shard_map/ppermute | solution.py:432
  38.2 7.6 %copy-start.11 = (pred[2]{0:T(512)(128)(4,1)S(1)}, pred[2]{0:T(512)(128)(4,1)}, u32[]{:S(2)}) copy-start(pred[2]{0:T(512)(128)(4,1)} %get-tuple-element.30) | copy-start | bytes 10
  38.2 12.2 %collective-permute-start.9 = (bf16[1600,128]{1,0:T(8,128)(2,1)S(1)}, bf16[1600,128]{1,0:T(8,128)(2,1)S(1)}, u32[]{:S(2)}, u32[]{:S(2)}) collective-permute-start(bf16[1600,128]{1,0:T(8,128)(2,1)S(1)} %get-tuple-element.22), channel_id=1, source_target_pairs={{8,16},{16,8},{24,32},{32,24},{40,48},{48,40},{56,64},{64,56},{72,... | collective-permute-start | bytes 1228808 | tf_op jit(solution)/shard_map/ppermute | solution.py:433
  46.0 25.6 %copy-start.2 = (bf16[1600,128]{1,0:T(8,128)(2,1)S(1)}, bf16[1600,128]{1,0:T(8,128)(2,1)}, u32[]{:S(2)}) copy-start(bf16[1600,128]{1,0:T(8,128)(2,1)} %copy-done.1) | copy-start | bytes 1228804
  46.0 6.8 %collective-permute-start.7 = (bf16[2,224,128]{2,1,0:T(8,128)(2,1)S(1)}, bf16[2,224,128]{2,1,0:T(8,128)(2,1)S(1)}, u32[]{:S(2)}, u32[]{:S(2)}) collective-permute-start(bf16[2,224,128]{2,1,0:T(8,128)(2,1)S(1)} %broadcast_select_fusion.4), channel_id=1, source_target_pairs={{0,32},{8,40},{16,48},{24,56},{32,0},{40,8},{48,16},{56,24},{64,96... | collective-permute-start | bytes 344072 | tf_op jit(solution)/shard_map/ppermute | solution.py:421
  52.8 10.2 %collective-permute-start.10 = (bf16[2,448,128]{2,1,0:T(8,128)(2,1)S(1)}, bf16[2,448,128]{2,1,0:T(8,128)(2,1)S(1)}, u32[]{:S(2)}, u32[]{:S(2)}) collective-permute-start(bf16[2,448,128]{2,1,0:T(8,128)(2,1)S(1)} %pad_maximum_fusion.1), channel_id=1, source_target_pairs={{0,16},{8,24},{16,0},{24,8},{32,48},{40,56},{48,32},{56,40},{64,80... | collective-permute-start | bytes 688136 | tf_op jit(solution)/shard_map/ppermute | solution.py:421
  52.9 18.2 %all-to-all-start = ((f32[32,2,128]{2,1,0:T(2,128)}), f32[32,2,128]{2,1,0:T(2,128)S(1)}, u32[]{:S(2)}, u32[]{:S(2)}) async-start(f32[32,2,128]{2,1,0:T(2,128)} %bitcast.16), calls=%async_computation | async-start | bytes 65536 | tf_op jit(solution)/shard_map/all_to_all | solution.py:439
  63.0 9.3 %copy-start.6 = (f32[64,768]{1,0:T(8,128)S(1)}, f32[64,768]{1,0:T(8,128)}, u32[]{:S(2)}) copy-start(f32[64,768]{1,0:T(8,128)} %constant.59.clone.places_ref) | copy-start | bytes 589828
  71.1 2.3 %collective-permute-start.11 = (bf16[2,896,128]{2,1,0:T(8,128)(2,1)S(1)}, bf16[2,896,128]{2,1,0:T(8,128)(2,1)S(1)}, u32[]{:S(2)}, u32[]{:S(2)}) collective-permute-start(bf16[2,896,128]{2,1,0:T(8,128)(2,1)S(1)} %pad_maximum_fusion.ref_ref), channel_id=1, source_target_pairs={{0,8},{8,0},{16,24},{24,16},{32,40},{40,32},{48,56},{56,48},{64,72... | collective-permute-start | bytes 1376264 | tf_op jit(solution)/shard_map/ppermute | solution.py:442

commit v5 on v3

--- a/solution.py
+++ b/solution.py
@@ -393,7 +393,7 @@
             scratch_shapes=[pltpu.VMEM((parts, cols, LANES), BF16)],
         ),
         cost_estimate=pl.CostEstimate(flops=10**6, bytes_accessed=4 * image_bytes, transcendentals=0),
-        compiler_params=pltpu.CompilerParams(vmem_limit_bytes=60 << 20),
+        compiler_params=pltpu.CompilerParams(vmem_limit_bytes=16 << 20),
     )(after(ref_dates, to_one, to_other), me_one, images)
     scattered = lax.all_to_all(
         candidate.reshape(near, piece, LANES),

time: 72.5 us -> 73.5 us (1.014)
  local copies, waits for them, and re-layouts: 5.63 us -> 7.34 us
  Pallas kernels: 17.7 us -> 16.5 us
    unnamed x39 -> x45, local copies, waits for them, and re-layouts: 5.55 us -> 7.25 us
    pallas_call x1, Pallas kernels: 2.8 us -> 1.64 us  [per_device(): pl.pallas_call(functools.partial(candidate_body, near), out_shape=shape((...]
  transfers between devices with their start and end apart: 11 -> 11, of which waited for: 3 -> 3; matrix products, arithmetic and copies ran while one was open for 2% -> 2% of each run, Pallas kernels for 23% -> 22%
where the time goes in v5:
time: 73.5 us; the launch traced here: 73 us
  starting transfers between devices  31.7 us (43%)
  Pallas kernels  16.5 us (22%)
  waiting for transfers between devices  13.6 us (19%)
  local copies, waits for them, and re-layouts  7.34 us (10%)
  other arithmetic  2.85 us (4%)
  between operations  0.98 us (1%)
    all_to_all x1, waiting for transfers between devices, per_device(): lax.all_to_all(looked.reshape(group, -1, LANES), 'date', 0, 0, tiled=True)  7.96 us
    ppermute x2, starting transfers between devices, flood(): other = lax.ppermute(value, 'date', [(i, i ^ step) for i in range(group)])  7.75 us
    unnamed x45, local copies, waits for them, and re-layouts  7.25 us
    pallas_call x2, Pallas kernels, resample_call(): pl.pallas_call(functools.partial(resample_body, crossed), out_shape=[jax....  7.09 us
    ppermute x1, starting transfers between devices, per_device(): from_other = lax.ppermute(to_other, 'strip', pairs2)  5.74 us
    all_to_all x1, starting transfers between devices, per_device(): lax.all_to_all(looked.reshape(group, -1, LANES), 'date', 0, 0, tiled=True)  5.35 us
    all_to_all x1, starting transfers between devices, per_device(): lax.all_to_all(candidate.reshape(near, piece, LANES), 'date', 0, 0, axis_...  5.14 us
    pallas_call x2, Pallas kernels, pair(): call(functools.partial(pair_body, index), shape((blocks, LANES), F32), [V...  5.06 us
  transfers between devices with their start and end apart: 11, of which 3 were waited for; matrix products, arithmetic and copies ran while one was open for 2% of the time, Pallas kernels for 22%

profile of v5, /device:TPU:19, one launch (start us, length us, event | category | flops | bytes accessed | tf_op | source)
XLA Modules:
  0.0 73.0 jit_solution(16572947668979536007)
XLA Ops:
  0.6 0.0 copy-start.14
  0.7 0.0 copy-start.5
  0.7 1.0 %broadcast_select_fusion.8 = (bf16[2,2,2,16,344]{4,3,2,1,0:T(8,128)(2,1)S(1)}, bf16[2,2,2,16,344]{4,3,2,1,0:T(8,128)(2,1)S(1)}) fusion(pred[]{:T(512)S(6)} %eq.40, bf16[2,2,2,320,344]{4,3,2,1,0:T(8,128)(2,1)} %bitcast.15), kind=kLoop, calls=%fused_computation.11 | loop fusion | flops 88064 | bytes 352257 | tf_op jit(solution)/shard_map/jit(_where)/select_n | solution.py:374
  1.7 0.1 collective-permute-start.2
  1.8 5.7 %collective-permute-start.1 = (bf16[2,2,2,16,344]{4,3,2,1,0:T(8,128)(2,1)S(1)}, bf16[2,2,2,16,344]{4,3,2,1,0:T(8,128)(2,1)S(1)}, u32[]{:S(2)}, u32[]{:S(2)}) collective-permute-start(bf16[2,2,2,16,344]{4,3,2,1,0:T(8,128)(2,1)S(1)} %get-tuple-element.30), channel_id=1, source_target_pairs={{1,2},{2,1},{3,4},{4,3},{5,6},{6,5},{9,10},{10,9},{11,12},{12,11},... | collective-permute-start | bytes 264200 | tf_op jit(solution)/shard_map/ppermute | solution.py:376
  7.6 0.0 copy-start
  7.6 1.5 %copy-done = bf16[2,2,2,344,320]{3,4,2,1,0:T(8,128)(2,1)S(1)} copy-done((bf16[2,2,2,344,320]{3,4,2,1,0:T(8,128)(2,1)S(1)}, bf16[2,2,2,344,320]{3,4,2,1,0:T(8,128)(2,1)}, u32[]{:S(2)}) %copy-start) | copy-done | bytes 1761304
  9.1 0.7 copy-done.13
  9.8 1.6 %shard_map.95 = bf16[1792,128]{1,0:T(8,128)(2,1)} custom-call(s32[2]{0:T(128)S(1)} %copy-done.13, s32[1]{0:T(128)} %bitcast.me_ref.rest_0_, bf16[2,2,2,320,344]{4,3,2,1,0:T(8,128)(2,1)S(1)} %bitcast.16), custom_call_target="tpu_custom_call" | custom-call | flops 1000000 | bytes 880640 | tf_op jit(solution)/shard_map/pallas_call | solution.py:385
  11.4 5.1 %all-to-all-start = ((bf16[8,224,128]{2,1,0:T(8,128)(2,1)}), bf16[8,224,128]{2,1,0:T(8,128)(2,1)S(1)}, u32[]{:S(2)}, u32[]{:S(2)}) async-start(bf16[8,224,128]{2,1,0:T(8,128)(2,1)} %bitcast.2), calls=%async_computation | async-start | bytes 917504 | tf_op jit(solution)/shard_map/all_to_all | solution.py:398
  16.6 0.5 and_compare_fusion.1
  17.2 0.0 copy-start.11
  17.2 0.6 iota_compare_fusion
  17.8 0.0 collective-permute-done.2
  17.8 0.0 collective-permute-done.1
  17.8 0.0 copy-start.6
  17.8 0.0 copy-done.18
  17.8 0.0 copy-done.5
  17.8 0.0 copy-done.1
  17.9 0.0 copy-start.19
  17.9 4.1 %shard_map.96 = (bf16[1600,128]{1,0:T(8,128)(2,1)S(1)}, bf16[1600,128]{1,0:T(8,128)(2,1)S(1)}, bf16[1600,128]{1,0:T(8,128)(2,1)}, bf16[1600,128]{1,0:T(8,128)(2,1)}) custom-call(s32[1]{0:T(128)} %bitcast.me_ref.rest_0_, s32[2,2,5,2,5]{4,3,2,1,0:T(2,128)S(1)} %add_bitcast_fusion.move_ref, bf16[64,16,128]{2,1,0:T(8,128)(2,1)S(1)} %copy-done.5, ...), custom_call_target="tpu_custom_call" | custom-call | flops 419430400 | bytes 1761280 | tf_op jit(solution)/shard_map/pallas_call | solution.py:197
  21.9 0.0 copy-done.6
  21.9 0.8 %copy-done.2 = bf16[1600,128]{1,0:T(8,128)(2,1)} copy-done((bf16[1600,128]{1,0:T(8,128)(2,1)}, bf16[1600,128]{1,0:T(8,128)(2,1)S(1)}, u32[]{:S(2)}) %copy-start.2) | copy-done | bytes 409624
  22.7 0.0 collective-permute-start.4
  22.7 3.7 %collective-permute-start.5 = (bf16[1600,128]{1,0:T(8,128)(2,1)}, bf16[1600,128]{1,0:T(8,128)(2,1)}, u32[]{:S(2)}, u32[]{:S(2)}) collective-permute-start(bf16[1600,128]{1,0:T(8,128)(2,1)} %get-tuple-element.20), channel_id=1, source_target_pairs={{8,16},{16,8},{24,32},{32,24},{40,48},{48,40},{56,64},{64,56},{72,... | collective-permute-start | bytes 1228808 | tf_op jit(solution)/shard_map/ppermute | solution.py:446
  26.4 0.0 all-to-all-done
  26.4 0.0 copy-done.20
  26.4 0.0 copy-start.3
  26.4 0.2 select_reduce_fusion
  26.7 6.5 %collective-permute-start = (bf16[2,224,128]{2,1,0:T(8,128)(2,1)S(1)}, bf16[2,224,128]{2,1,0:T(8,128)(2,1)S(1)}, u32[]{:S(2)}, u32[]{:S(2)}) collective-permute-start(bf16[2,224,128]{2,1,0:T(8,128)(2,1)S(1)} %select_reduce_fusion), channel_id=1, source_target_pairs={{0,128},{8,136},{16,144},{24,152},{32,160},{40,168},{48,176},{56,1... | collective-permute-start | bytes 344072 | tf_op jit(solution)/shard_map/ppermute | solution.py:439
  33.1 0.0 copy-done.19
  33.2 0.9 %copy-done.7 = bf16[2,2,2,16,344]{4,3,2,1,0:T(8,128)(2,1)S(1)} copy-done((bf16[2,2,2,16,344]{4,3,2,1,0:T(8,128)(2,1)S(1)}, bf16[2,2,2,16,344]{4,3,2,1,0:T(8,128)(2,1)}, u32[]{:S(2)}) %copy-start.7) | copy-done | bytes 88088
  34.0 0.7 copy-done.12
  34.8 3.0 %shard_map.97 = (bf16[1600,128]{1,0:T(8,128)(2,1)S(1)}, bf16[1600,128]{1,0:T(8,128)(2,1)S(1)}) custom-call(s32[1]{0:T(128)} %bitcast.me_ref.rest_0_, s32[2,2,5,2,5]{4,3,2,1,0:T(2,128)S(1)} %copy-done.12, bf16[64,16,128]{2,1,0:T(8,128)(2,1)S(1)} %copy-done.5, bf16[2,2,2,320,344]{4,3,2,1,0:T(8,128)(2,1)S(1)} %bitcast.18, ...), custom_call_target="tpu_custom_call" | custom-call | flops 419430400 | bytes 1761280 | tf_op jit(solution)/shard_map/pallas_call | solution.py:197
  37.8 0.0 copy-start.8
  37.8 0.9 %copy-done.8 = bf16[64,640]{1,0:T(8,128)(2,1)S(1)} copy-done((bf16[64,640]{1,0:T(8,128)(2,1)S(1)}, bf16[64,640]{1,0:T(8,128)(2,1)}, u32[]{:S(2)}) %copy-start.8) | copy-done | bytes 81944
  38.7 0.9 %copy-done.9 = bf16[64,640]{1,0:T(8,128)(2,1)S(1)} copy-done((bf16[64,640]{1,0:T(8,128)(2,1)S(1)}, bf16[64,640]{1,0:T(8,128)(2,1)}, u32[]{:S(2)}) %copy-start.9) | copy-done | bytes 81944
  39.6 1.6 %shard_map.98.rest_5_ = f32[64,128]{1,0:T(8,128)S(1)} custom-call(bf16[64,640]{1,0:T(8,128)(2,1)S(1)} %copy-done.8, bf16[64,640]{1,0:T(8,128)(2,1)S(1)} %copy-done.9, bf16[1600,128]{1,0:T(8,128)(2,1)S(1)} %get-tuple-element.14.rest_0_.s00_ref, bf16[1600,128]{1,0:T(8,128)(2,1)S(1)} %get-tuple-element.15.rest_1_.s10_ref, ...), custom_call_target="tpu_custom_call" | custom-call | flops 100000000 | bytes 1761280 | tf_op jit(solution)/shard_map/pallas_call | solution.py:413
  41.2 0.0 collective-permute-done
  41.2 0.1 broadcast_select_fusion.2
  41.3 1.3 %collective-permute-start.3 = (bf16[2,224,128]{2,1,0:T(8,128)(2,1)S(1)}, bf16[2,224,128]{2,1,0:T(8,128)(2,1)S(1)}, u32[]{:S(2)}, u32[]{:S(2)}) collective-permute-start(bf16[2,224,128]{2,1,0:T(8,128)(2,1)S(1)} %broadcast_select_fusion.2), channel_id=1, source_target_pairs={{0,64},{8,72},{16,80},{24,88},{32,96},{40,104},{48,112},{56,120},{... | collective-permute-start | bytes 344072 | tf_op jit(solution)/shard_map/ppermute | solution.py:439
  42.6 0.0 collective-permute-done.4.rest_2_
  42.6 0.0 collective-permute-done.5.rest_3_
  42.6 3.5 %shard_map.99 = f32[64,128]{1,0:T(8,128)} custom-call(bf16[64,640]{1,0:T(8,128)(2,1)S(1)} %copy-done.8, bf16[64,640]{1,0:T(8,128)(2,1)S(1)} %copy-done.9, s32[1]{0:T(128)} %bitcast.me_ref.rest_0_, bf16[1600,128]{1,0:T(8,128)(2,1)S(1)} %get-tuple-element.15.rest_1_.s10_ref, bf16[1600,128]{1,0:T(8,128)(2,1)} %collective-permute-done.4.rest_2_, ...), custom_call_target="tpu_custom_call" | custom-call | flops 100000000 | bytes 1761280 | tf_op jit(solution)/shard_map/pallas_call | solution.py:413
  46.1 2.0 %collective-permute-done.3 = bf16[2,224,128]{2,1,0:T(8,128)(2,1)S(1)} collective-permute-done((bf16[2,224,128]{2,1,0:T(8,128)(2,1)S(1)}, bf16[2,224,128]{2,1,0:T(8,128)(2,1)S(1)}, u32[]{:S(2)}, u32[]{:S(2)}) %collective-permute-start.3) | collective-permute-done | bytes 114720 | tf_op jit(solution)/shard_map/ppermute | solution.py:439
  48.0 0.1 broadcast_select_fusion.3
  48.1 0.1 collective-permute-start.6
  48.2 3.6 %collective-permute-done.6 = bf16[2,224,128]{2,1,0:T(8,128)(2,1)S(1)} collective-permute-done((bf16[2,224,128]{2,1,0:T(8,128)(2,1)S(1)}, bf16[2,224,128]{2,1,0:T(8,128)(2,1)S(1)}, u32[]{:S(2)}, u32[]{:S(2)}) %collective-permute-start.6) | collective-permute-done | bytes 114720 | tf_op jit(solution)/shard_map/ppermute | solution.py:434
  51.9 3.5 %collective-permute-start.7 = (bf16[2,448,128]{2,1,0:T(8,128)(2,1)S(1)}, bf16[2,448,128]{2,1,0:T(8,128)(2,1)S(1)}, u32[]{:S(2)}, u32[]{:S(2)}) collective-permute-start(bf16[2,448,128]{2,1,0:T(8,128)(2,1)S(1)} %pad_maximum_fusion.1), channel_id=1, source_target_pairs={{0,16},{8,24},{16,0},{24,8},{32,48},{40,56},{48,32},{56,40},{64,80... | collective-permute-start | bytes 688136 | tf_op jit(solution)/shard_map/ppermute | solution.py:434
  55.3 5.4 %all-to-all-start.1 = ((f32[32,2,128]{2,1,0:T(2,128)}), f32[32,2,128]{2,1,0:T(2,128)S(1)}, u32[]{:S(2)}, u32[]{:S(2)}) async-start(f32[32,2,128]{2,1,0:T(2,128)} %bitcast.4), calls=%async_computation.1 | async-start | bytes 65536 | tf_op jit(solution)/shard_map/all_to_all | solution.py:452
  60.7 0.0 copy-start.10
  60.7 0.0 collective-permute-done.7
  60.7 0.1 broadcast_select_fusion.1
  60.9 8.0 %all-to-all-done.1 = f32[32,2,128]{2,1,0:T(2,128)S(1)} async-done(((f32[32,2,128]{2,1,0:T(2,128)}), f32[32,2,128]{2,1,0:T(2,128)S(1)}, u32[]{:S(2)}, u32[]{:S(2)}) %all-to-all-start.1) | async-done | bytes 32800 | tf_op jit(solution)/shard_map/all_to_all | solution.py:452
  68.8 0.4 collective-permute-start.8
  69.2 0.8 %shard_map.100 = f32[64,128]{1,0:T(8,128)S(1)} custom-call(s32[1]{0:T(128)} %bitcast.me_ref.rest_0_, bf16[2,896,128]{2,1,0:T(8,128)(2,1)S(1)} %pad_maximum_fusion.ref_ref, bf16[1600,128]{1,0:T(8,128)(2,1)S(1)} %get-tuple-element.14.rest_0_.s00_ref, bf16[1600,128]{1,0:T(8,128)(2,1)S(1)} %get-tuple-element.16.rest_2_.rest_4_.s01_ref, ...), custom_call_target="tpu_custom_call" | custom-call | flops 10000000 | bytes 660480 | tf_op jit(solution)/shard_map/pallas_call | solution.py:425
  70.0 1.1 %shard_map.102 = f32[2,2,2,16,63]{4,3,2,1,0:T(8,128)} custom-call(f32[64,768]{1,0:T(8,128)S(1)} %copy-done.10, f32[64,128]{1,0:T(8,128)S(1)} %bitcast.19), custom_call_target="tpu_custom_call" | custom-call | flops 10000000 | bytes 1000000 | tf_op jit(solution)/shard_map/pallas_call | solution.py:458
  71.2 0.0 collective-permute-done.8.ref_ref
  71.2 0.8 %shard_map.101 = f32[64,128]{1,0:T(8,128)S(1)} custom-call(s32[1]{0:T(128)} %bitcast.me_ref.rest_0_, bf16[2,896,128]{2,1,0:T(8,128)(2,1)S(1)} %collective-permute-done.8.ref_ref, bf16[1600,128]{1,0:T(8,128)(2,1)S(1)} %get-tuple-element.14.rest_0_.s00_ref, bf16[1600,128]{1,0:T(8,128)(2,1)S(1)} %get-tuple-element.16.rest_2_.rest_4_.s01_ref, ...), custom_call_target="tpu_custom_call" | custom-call | flops 10000000 | bytes 660480 | tf_op jit(solution)/shard_map/pallas_call | solution.py:425
  72.0 0.1 copy.17
  72.1 0.1 copy.16
  72.2 0.1 pad_maximum_fusion.2
  72.3 0.1 reshape.54
  72.4 0.6 copy.15
  (28 shorter events, 0.2 us)
Async XLA Ops:
  0.6 16.0 %copy-start.14 = (s32[2]{0:T(128)S(1)}, s32[2]{0:T(128)}, u32[]{:S(2)}) copy-start(s32[2]{0:T(128)} %dates_ref) | copy-start | bytes 28
  0.6 16.5 %copy-start.15 = (s32[2,2,2,5,5]{4,2,3,1,0:T(2,128)S(1)}, s32[2,2,2,5,5]{4,2,3,1,0:T(2,128)}, u32[]{:S(2)}) copy-start(s32[2,2,2,5,5]{4,2,3,1,0:T(2,128)} %param.10) | copy-start | bytes 2404
  0.7 16.5 %copy-start.16 = (s32[2,2,2,5,5]{4,2,3,1,0:T(2,128)S(1)}, s32[2,2,2,5,5]{4,2,3,1,0:T(2,128)}, u32[]{:S(2)}) copy-start(s32[2,2,2,5,5]{4,2,3,1,0:T(2,128)} %param.9) | copy-start | bytes 2404
  0.7 17.2 %copy-start.5 = (bf16[64,16,128]{2,1,0:T(8,128)(2,1)S(1)}, bf16[64,16,128]{2,1,0:T(8,128)(2,1)}, u32[]{:S(2)}) copy-start(bf16[64,16,128]{2,1,0:T(8,128)(2,1)} %constant.69.clone.table_ref) | copy-start | bytes 786436
  1.7 16.1 %collective-permute-start.2 = (bf16[2,2,2,16,344]{4,3,2,1,0:T(8,128)(2,1)S(1)}, bf16[2,2,2,16,344]{4,3,2,1,0:T(8,128)(2,1)S(1)}, u32[]{:S(2)}, u32[]{:S(2)}) collective-permute-start(bf16[2,2,2,16,344]{4,3,2,1,0:T(8,128)(2,1)S(1)} %get-tuple-element.31), channel_id=1, source_target_pairs={{0,1},{1,0},{2,3},{3,2},{4,5},{5,4},{6,7},{7,6},{8,9},{9,8},{10,11... | collective-permute-start | bytes 264200 | tf_op jit(solution)/shard_map/ppermute | solution.py:375
  1.8 15.9 %collective-permute-start.1 = (bf16[2,2,2,16,344]{4,3,2,1,0:T(8,128)(2,1)S(1)}, bf16[2,2,2,16,344]{4,3,2,1,0:T(8,128)(2,1)S(1)}, u32[]{:S(2)}, u32[]{:S(2)}) collective-permute-start(bf16[2,2,2,16,344]{4,3,2,1,0:T(8,128)(2,1)S(1)} %get-tuple-element.30), channel_id=1, source_target_pairs={{1,2},{2,1},{3,4},{4,3},{5,6},{6,5},{9,10},{10,9},{11,12},{12,11},... | collective-permute-start | bytes 264200 | tf_op jit(solution)/shard_map/ppermute | solution.py:376
  7.6 1.5 %copy-start = (bf16[2,2,2,344,320]{3,4,2,1,0:T(8,128)(2,1)S(1)}, bf16[2,2,2,344,320]{3,4,2,1,0:T(8,128)(2,1)}, u32[]{:S(2)}) copy-start(bf16[2,2,2,344,320]{3,4,2,1,0:T(8,128)(2,1)} %param.8) | copy-start | bytes 5283844
  9.1 0.7 copy-start.13
  9.8 8.0 %copy-start.1 = (bf16[2,2,2,344,320]{3,4,2,1,0:T(8,128)(2,1)S(1)}, bf16[2,2,2,344,320]{3,4,2,1,0:T(8,128)(2,1)}, u32[]{:S(2)}) copy-start(bf16[2,2,2,344,320]{3,4,2,1,0:T(8,128)(2,1)} %param.8) | copy-start | bytes 5283844
  11.4 14.9 %all-to-all-start = ((bf16[8,224,128]{2,1,0:T(8,128)(2,1)}), bf16[8,224,128]{2,1,0:T(8,128)(2,1)S(1)}, u32[]{:S(2)}, u32[]{:S(2)}) async-start(bf16[8,224,128]{2,1,0:T(8,128)(2,1)} %bitcast.2), calls=%async_computation | async-start | bytes 917504 | tf_op jit(solution)/shard_map/all_to_all | solution.py:398
  17.1 0.7 copy-start.18
  17.2 5.5 %copy-start.11 = (s32[2,2,5,2,5]{4,3,2,1,0:T(2,128)}, s32[2,2,5,2,5]{4,3,2,1,0:T(2,128)S(1)}, u32[]{:S(2)}) copy-start(s32[2,2,5,2,5]{4,3,2,1,0:T(2,128)S(1)} %add_bitcast_fusion.move_ref) | copy-start | bytes 2404
  17.8 8.6 %copy-start.20 = (pred[2,8]{1,0:T(4,128)(4,1)S(1)}, pred[2,8]{1,0:T(4,128)(4,1)}, u32[]{:S(2)}) copy-start(pred[2,8]{1,0:T(4,128)(4,1)} %iota_compare_fusion) | copy-start | bytes 52
  17.8 4.1 %copy-start.6 = (bf16[2,2,2,16,344]{4,3,2,1,0:T(8,128)(2,1)}, bf16[2,2,2,16,344]{4,3,2,1,0:T(8,128)(2,1)S(1)}, u32[]{:S(2)}) copy-start(bf16[2,2,2,16,344]{4,3,2,1,0:T(8,128)(2,1)S(1)} %get-tuple-element.37.left_ref) | copy-start | bytes 264196
  17.9 15.3 %copy-start.19 = (s32[2]{0:T(128)S(1)}, s32[2]{0:T(128)}, u32[]{:S(2)}) copy-start(s32[2]{0:T(128)} %copy-done.18) | copy-start | bytes 28
  21.9 0.8 %copy-start.2 = (bf16[1600,128]{1,0:T(8,128)(2,1)}, bf16[1600,128]{1,0:T(8,128)(2,1)S(1)}, u32[]{:S(2)}) copy-start(bf16[1600,128]{1,0:T(8,128)(2,1)S(1)} %get-tuple-element.17.rest_3_.s11_ref) | copy-start | bytes 1228804
  22.7 19.9 %collective-permute-start.4 = (bf16[1600,128]{1,0:T(8,128)(2,1)}, bf16[1600,128]{1,0:T(8,128)(2,1)}, u32[]{:S(2)}, u32[]{:S(2)}) collective-permute-start(bf16[1600,128]{1,0:T(8,128)(2,1)} %get-tuple-element.19), channel_id=1, source_target_pairs={{0,8},{8,0},{16,24},{24,16},{32,40},{40,32},{48,56},{56,48},{64,72... | collective-permute-start | bytes 1228808 | tf_op jit(solution)/shard_map/ppermute | solution.py:445
  22.7 19.9 %collective-permute-start.5 = (bf16[1600,128]{1,0:T(8,128)(2,1)}, bf16[1600,128]{1,0:T(8,128)(2,1)}, u32[]{:S(2)}, u32[]{:S(2)}) collective-permute-start(bf16[1600,128]{1,0:T(8,128)(2,1)} %get-tuple-element.20), channel_id=1, source_target_pairs={{8,16},{16,8},{24,32},{32,24},{40,48},{48,40},{56,64},{64,56},{72,... | collective-permute-start | bytes 1228808 | tf_op jit(solution)/shard_map/ppermute | solution.py:446
  26.4 11.4 %copy-start.3 = (bf16[1600,128]{1,0:T(8,128)(2,1)S(1)}, bf16[1600,128]{1,0:T(8,128)(2,1)}, u32[]{:S(2)}) copy-start(bf16[1600,128]{1,0:T(8,128)(2,1)} %copy-done.2) | copy-start | bytes 1228804
  26.7 14.5 %collective-permute-start = (bf16[2,224,128]{2,1,0:T(8,128)(2,1)S(1)}, bf16[2,224,128]{2,1,0:T(8,128)(2,1)S(1)}, u32[]{:S(2)}, u32[]{:S(2)}) collective-permute-start(bf16[2,224,128]{2,1,0:T(8,128)(2,1)S(1)} %select_reduce_fusion), channel_id=1, source_target_pairs={{0,128},{8,136},{16,144},{24,152},{32,160},{40,168},{48,176},{56,1... | collective-permute-start | bytes 344072 | tf_op jit(solution)/shard_map/ppermute | solution.py:439
  33.2 0.9 %copy-start.7 = (bf16[2,2,2,16,344]{4,3,2,1,0:T(8,128)(2,1)S(1)}, bf16[2,2,2,16,344]{4,3,2,1,0:T(8,128)(2,1)}, u32[]{:S(2)}) copy-start(bf16[2,2,2,16,344]{4,3,2,1,0:T(8,128)(2,1)} %copy-done.6) | copy-start | bytes 264196
  34.0 0.7 copy-start.12
  37.8 0.9 %copy-start.8 = (bf16[64,640]{1,0:T(8,128)(2,1)S(1)}, bf16[64,640]{1,0:T(8,128)(2,1)}, u32[]{:S(2)}) copy-start(bf16[64,640]{1,0:T(8,128)(2,1)} %constant.70.clone.plain_ref) | copy-start | bytes 245764
  38.7 0.9 %copy-start.9 = (bf16[64,640]{1,0:T(8,128)(2,1)S(1)}, bf16[64,640]{1,0:T(8,128)(2,1)}, u32[]{:S(2)}) copy-start(bf16[64,640]{1,0:T(8,128)(2,1)} %constant.71.clone.signed_ref) | copy-start | bytes 245764
  39.6 8.4 %copy-start.17 = (pred[2]{0:T(512)(128)(4,1)S(1)}, pred[2]{0:T(512)(128)(4,1)}, u32[]{:S(2)}) copy-start(pred[2]{0:T(512)(128)(4,1)} %get-tuple-element.28) | copy-start | bytes 10
  41.3 6.7 %collective-permute-start.3 = (bf16[2,224,128]{2,1,0:T(8,128)(2,1)S(1)}, bf16[2,224,128]{2,1,0:T(8,128)(2,1)S(1)}, u32[]{:S(2)}, u32[]{:S(2)}) collective-permute-start(bf16[2,224,128]{2,1,0:T(8,128)(2,1)S(1)} %broadcast_select_fusion.2), channel_id=1, source_target_pairs={{0,64},{8,72},{16,80},{24,88},{32,96},{40,104},{48,112},{56,120},{... | collective-permute-start | bytes 344072 | tf_op jit(solution)/shard_map/ppermute | solution.py:439
  46.1 23.2 %copy-start.4 = (bf16[1600,128]{1,0:T(8,128)(2,1)S(1)}, bf16[1600,128]{1,0:T(8,128)(2,1)}, u32[]{:S(2)}) copy-start(bf16[1600,128]{1,0:T(8,128)(2,1)} %copy-done.2) | copy-start | bytes 1228804
  48.1 3.7 %collective-permute-start.6 = (bf16[2,224,128]{2,1,0:T(8,128)(2,1)S(1)}, bf16[2,224,128]{2,1,0:T(8,128)(2,1)S(1)}, u32[]{:S(2)}, u32[]{:S(2)}) collective-permute-start(bf16[2,224,128]{2,1,0:T(8,128)(2,1)S(1)} %broadcast_select_fusion.3), channel_id=1, source_target_pairs={{0,32},{8,40},{16,48},{24,56},{32,0},{40,8},{48,16},{56,24},{64,96... | collective-permute-start | bytes 344072 | tf_op jit(solution)/shard_map/ppermute | solution.py:434
  51.9 8.8 %collective-permute-start.7 = (bf16[2,448,128]{2,1,0:T(8,128)(2,1)S(1)}, bf16[2,448,128]{2,1,0:T(8,128)(2,1)S(1)}, u32[]{:S(2)}, u32[]{:S(2)}) collective-permute-start(bf16[2,448,128]{2,1,0:T(8,128)(2,1)S(1)} %pad_maximum_fusion.1), channel_id=1, source_target_pairs={{0,16},{8,24},{16,0},{24,8},{32,48},{40,56},{48,32},{56,40},{64,80... | collective-permute-start | bytes 688136 | tf_op jit(solution)/shard_map/ppermute | solution.py:434
  55.3 13.5 %all-to-all-start.1 = ((f32[32,2,128]{2,1,0:T(2,128)}), f32[32,2,128]{2,1,0:T(2,128)S(1)}, u32[]{:S(2)}, u32[]{:S(2)}) async-start(f32[32,2,128]{2,1,0:T(2,128)} %bitcast.4), calls=%async_computation.1 | async-start | bytes 65536 | tf_op jit(solution)/shard_map/all_to_all | solution.py:452
  60.7 9.3 %copy-start.10 = (f32[64,768]{1,0:T(8,128)S(1)}, f32[64,768]{1,0:T(8,128)}, u32[]{:S(2)}) copy-start(f32[64,768]{1,0:T(8,128)} %constant.72.clone.places_ref) | copy-start | bytes 589828
  68.8 2.3 %collective-permute-start.8 = (bf16[2,896,128]{2,1,0:T(8,128)(2,1)S(1)}, bf16[2,896,128]{2,1,0:T(8,128)(2,1)S(1)}, u32[]{:S(2)}, u32[]{:S(2)}) collective-permute-start(bf16[2,896,128]{2,1,0:T(8,128)(2,1)S(1)} %pad_maximum_fusion.ref_ref), channel_id=1, source_target_pairs={{0,8},{8,0},{16,24},{24,16},{32,40},{40,32},{48,56},{56,48},{64,72... | collective-permute-start | bytes 1376264 | tf_op jit(solution)/shard_map/ppermute | solution.py:455
